TPU v7x, 128 devices: a whole 4x4x4 slice. The times are simulated.
128 devices in a mesh: fsdp: 16 (over x, z), dp: 8 (over y, core).
Axes of the slice: x: 4, y: 4, z: 4, core: 2. Of those that a mesh axis runs over, the one named last changes fastest.
Arguments:
- grad_parts: bfloat16 [8, 16384, 2048], P('dp', 'fsdp'), may hold values from -6 to 6
- old_master: float32 [16384, 2048], P(('fsdp', 'dp')), may hold values from -0.25 to 0.25
- old_mean: bfloat16 [16384, 2048], P(('fsdp', 'dp')), may hold values from -1 to 1
- old_mean_scale: bfloat16 [16384], P(('fsdp', 'dp')), may hold values from 0.049804688 to 0.5
- old_square: bfloat16 [16384, 2048], P(('fsdp', 'dp')), may hold values from 0.049804688 to 1
- old_square_scale: bfloat16 [16384], P(('fsdp', 'dp')), may hold values from 0.29882812 to 3
- old_map: int32 [16384], replicated, may hold values from 0 to 16383, as said below
Outputs:
- weights: bfloat16 [16384, 2048], P('fsdp')
- master: float32 [16384, 2048], P(('fsdp', 'dp'))
- mean_codes: bfloat16 [16384, 2048], P(('fsdp', 'dp'))
- mean_scales: bfloat16 [16384], P(('fsdp', 'dp'))
- square_codes: bfloat16 [16384, 2048], P(('fsdp', 'dp'))
- square_scales: bfloat16 [16384], P(('fsdp', 'dp'))
Inputs may be any that keep to these rules, and one draw needn't show every extreme that they name: old_map is a permutation of the old slots; old slot s lies on device s // 128 counted along fsdp+dp with fsdp major, and block b belongs to new owner b // 128 counted the same way. Every device holds exactly 128 old slots; one device holds at most 2 blocks of one new owner, and every draw has a pair with exactly 2.
All inputs are finite; a program needn't handle non-finite values. Where the computation divides by a largest or mean magnitude, that divisor is 1e-20 or more.
Results may differ from a plain program's by a relative error of at most 0.02.
Values may be sent and summed in bfloat16 or wider, within the bound.
No kernel may reach another device: no remote copies, remote signals or barrier semaphores. Data moves between devices by JAX's collectives and lax.ppermute only.
A program may use at most 64 MiB of HBM per device.

v0:
```python
import jax
import jax.numpy as jnp
from jax import lax
from jax.sharding import PartitionSpec as P


def pair_rank(owners, keyed):
    matching = owners[:, None] == owners[None, :]
    before = keyed[None, :] < keyed[:, None]
    return jnp.sum(jnp.where(matching & before, 1, 0), axis=1).astype(jnp.int32)


def route_bf16(chooser, values):
    flat_values = values.reshape((values.shape[0], -1))
    moved = jnp.dot(chooser.astype(jnp.bfloat16), flat_values, preferred_element_type=jnp.float32)
    return moved.astype(jnp.bfloat16).reshape((chooser.shape[0],) + values.shape[1:])


def route_f32(chooser, values):
    return jnp.dot(
        chooser.astype(jnp.float32),
        values,
        precision=lax.Precision.HIGHEST,
        preferred_element_type=jnp.float32,
    )


def block_peak(values):
    return (jnp.max(values, axis=1) + 1e-06).astype(jnp.bfloat16)


def local(grad_parts, old_master, old_mean, old_mean_scale, old_square, old_square_scale, old_map):
    count_all = lax.axis_size(("fsdp", "dp"))
    block_rows = old_master.shape[0]
    block_len = old_master.shape[1]
    peer_cap = max(2, 2 * block_rows // count_all)
    slot_total = count_all * peer_cap
    self_index = lax.axis_index(("fsdp", "dp"))
    gradient = lax.psum_scatter(
        grad_parts[0].astype(jnp.float32).astype(jnp.bfloat16),
        "dp",
        scatter_dimension=0,
        tiled=True,
    ).astype(jnp.float32)
    total_blocks = old_map.shape[0]
    my_slots = self_index * block_rows + jnp.arange(block_rows, dtype=jnp.int32)
    block_ids = jnp.arange(total_blocks, dtype=jnp.int32)
    held_blocks = jnp.sum(
        jnp.where(old_map[None, :] == my_slots[:, None], block_ids[None, :], 0), axis=1
    )
    target = held_blocks // block_rows
    local_pos = held_blocks % block_rows
    sent_rank = pair_rank(target, local_pos)
    wanted = lax.dynamic_slice_in_dim(old_map, self_index * block_rows, block_rows)
    source = wanted // block_rows
    got_rank = pair_rank(source, jnp.arange(block_rows, dtype=jnp.int32))
    slot_ids = jnp.arange(slot_total, dtype=jnp.int32)
    send_flat = target * peer_cap + sent_rank
    placing = slot_ids[:, None] == send_flat[None, :]
    moment_codes = jnp.stack([old_mean, old_square], axis=1)
    moment_scales = jnp.stack([old_mean_scale, old_square_scale], axis=1)
    code_buffer = route_bf16(placing, moment_codes).reshape((count_all, peer_cap, 2, block_len))
    scale_buffer = route_bf16(placing, moment_scales).reshape((count_all, peer_cap, 2))
    master_buffer = route_f32(placing, old_master).reshape((count_all, peer_cap, block_len))
    code_in, scale_in = (
        lax.all_to_all(code_buffer, ("fsdp", "dp"), split_axis=0, concat_axis=0, tiled=True),
        lax.all_to_all(scale_buffer, ("fsdp", "dp"), split_axis=0, concat_axis=0, tiled=True),
    )
    master_in = lax.all_to_all(
        master_buffer.astype(jnp.bfloat16), ("fsdp", "dp"), split_axis=0, concat_axis=0, tiled=True
    ).astype(master_buffer.dtype)
    recv_flat = source * peer_cap + got_rank
    picking = recv_flat[:, None] == slot_ids[None, :]
    code_rows = route_bf16(picking, code_in.reshape((slot_total, 2, block_len))).astype(jnp.float32)
    scale_rows = route_bf16(picking, scale_in.reshape((slot_total, 2))).astype(jnp.float32)
    weight_old = route_f32(picking, master_in.reshape((slot_total, block_len)))
    mean_old = code_rows[:, 0] * scale_rows[:, 0:1]
    square_old = code_rows[:, 1] * scale_rows[:, 1:2]
    mean_next = 0.9 * mean_old + 0.1 * gradient
    square_next = 0.95 * square_old + 0.05 * gradient * gradient
    master = weight_old - 0.05 * (mean_next / (jnp.sqrt(square_next) + 1e-08) + 0.1 * weight_old)
    mean_scales = block_peak(jnp.abs(mean_next))
    square_scales = block_peak(square_next)
    mean_codes = (mean_next / mean_scales.astype(jnp.float32)[:, None]).astype(jnp.bfloat16)
    square_codes = (square_next / square_scales.astype(jnp.float32)[:, None]).astype(jnp.bfloat16)
    weights = lax.all_gather(master.astype(jnp.bfloat16), "dp", axis=0, tiled=True)
    return (weights, master, mean_codes, mean_scales, square_codes, square_scales)


def solution(mesh):
    in_specs = (
        P("dp", "fsdp", None),
        P(("fsdp", "dp"), None),
        P(("fsdp", "dp"), None),
        P(("fsdp", "dp")),
        P(("fsdp", "dp"), None),
        P(("fsdp", "dp")),
        P(),
    )
    out_specs = (
        P("fsdp", None),
        P(("fsdp", "dp"), None),
        P(("fsdp", "dp"), None),
        P(("fsdp", "dp")),
        P(("fsdp", "dp"), None),
        P(("fsdp", "dp")),
    )
    return jax.shard_map(local, mesh=mesh, in_specs=in_specs, out_specs=out_specs, check_vma=False)
```

profile of v0, /device:TPU:1, one launch (start us, length us, event | category | flops | bytes accessed | tf_op | source)
XLA Modules:
  0.0 145.3 jit_solution(600305273660461602)
XLA Ops:
  7.3 0.7 reduce-scatter.2.cloned.1.call-update
  7.9 0.2 copy-done.4
  8.1 1.3 select_reduce_fusion
  9.5 0.2 select_reduce_fusion.1
  10.0 0.7 copy.29
  10.7 11.5 %all-to-all-start.2 = ((bf16[128,2,2]{1,2,0:T(2,128)(2,1)}), bf16[128,2,2]{1,2,0:T(2,128)(2,1)S(1)}, u32[]{:S(2)}, u32[]{:S(2)}) async-start(bf16[128,2,2]{1,2,0:T(2,128)(2,1)} %copy.29), calls=%async_computation.2 | async-start | bytes 131072 | tf_op jit(solution)/shard_map/all_to_all | solution.py:67
  22.2 1.0 convolution_convert_fusion.2
  23.3 1.5 %convert_element_type.77 = bf16[128,2,2048]{2,1,0:T(2,128)(2,1)} reshape(bf16[256,2048]{1,0:T(8,128)(2,1)S(1)} %convolution_convert_fusion.2) | data formatting | bytes 2097152 | tf_op jit(solution)/shard_map/convert_element_type | solution.py:70
  24.8 6.9 %all-to-all-done.2 = bf16[128,2,2]{1,2,0:T(2,128)(2,1)S(1)} async-done(((bf16[128,2,2]{1,2,0:T(2,128)(2,1)}), bf16[128,2,2]{1,2,0:T(2,128)(2,1)S(1)}, u32[]{:S(2)}, u32[]{:S(2)}) %all-to-all-start.2) | async-done | bytes 1056 | tf_op jit(solution)/shard_map/all_to_all | solution.py:67
  31.7 5.4 %all-to-all-start = ((bf16[128,2,2048]{2,1,0:T(2,128)(2,1)}), bf16[128,2,2048]{2,1,0:T(2,128)(2,1)}, u32[]{:S(2)}, u32[]{:S(2)}) async-start(bf16[128,2,2048]{2,1,0:T(2,128)(2,1)} %convert_element_type.77), calls=%async_computation | async-start | bytes 2097152 | tf_op jit(solution)/shard_map/all_to_all | solution.py:69
  37.0 0.3 copy.25
  37.3 0.3 copy.26
  37.7 0.7 convolution_convert_fusion
  38.4 2.8 %reshape_reshape.6 = bf16[128,2,2,2048]{3,2,1,0:T(2,128)(2,1)} reshape(bf16[256,4096]{1,0:T(8,128)(2,1)S(1)} %convolution_convert_fusion) | data formatting | bytes 4194304 | tf_op jit(solution)/shard_map/reshape;reshape | solution.py:62
  41.2 14.7 %all-to-all-done = bf16[128,2,2048]{2,1,0:T(2,128)(2,1)} async-done(((bf16[128,2,2048]{2,1,0:T(2,128)(2,1)}), bf16[128,2,2048]{2,1,0:T(2,128)(2,1)}, u32[]{:S(2)}, u32[]{:S(2)}) %all-to-all-start) | async-done | bytes 1048608 | tf_op jit(solution)/shard_map/all_to_all | solution.py:69
  55.9 5.8 %all-to-all-start.1 = ((bf16[128,2,2,2048]{3,2,1,0:T(2,128)(2,1)}), bf16[128,2,2,2048]{3,2,1,0:T(2,128)(2,1)S(1)}, u32[]{:S(2)}, u32[]{:S(2)}) async-start(bf16[128,2,2,2048]{3,2,1,0:T(2,128)(2,1)} %reshape_reshape.6), calls=%async_computation.1 | async-start | bytes 4194304 | tf_op jit(solution)/shard_map/all_to_all | solution.py:66
  61.7 0.2 all-gather.2.cloned.1.call-start
  62.4 0.2 fusion.1
  62.6 2.3 %reshape.113 = bf16[256,2048]{1,0:T(8,128)(2,1)} reshape(bf16[128,2,2048]{2,1,0:T(2,128)(2,1)} %all-to-all-done) | data formatting | bytes 2097152 | tf_op jit(solution)/shard_map/reshape | solution.py:76
  64.9 27.1 %all-to-all-done.1 = bf16[128,2,2,2048]{3,2,1,0:T(2,128)(2,1)S(1)} async-done(((bf16[128,2,2,2048]{3,2,1,0:T(2,128)(2,1)}), bf16[128,2,2,2048]{3,2,1,0:T(2,128)(2,1)S(1)}, u32[]{:S(2)}, u32[]{:S(2)}) %all-to-all-start.1) | async-done | bytes 2097184 | tf_op jit(solution)/shard_map/all_to_all | solution.py:66
  92.1 0.9 copy.34
  93.0 1.8 %fusion = f32[128,4096]{1,0:T(8,128)} fusion(bf16[256,4096]{1,0:T(8,128)(2,1)S(1)} %bitcast.49, s32[128]{0:T(128)S(1)} %multiply_add_fusion.1), kind=kOutput, calls=%fused_computation.3 | convolution fusion | flops 269516800 | bytes 4194816 | tf_op jit(solution)/shard_map/dot_general | solution.py:15
  94.8 1.9 %copy.27 = f32[128,4096]{0,1:T(8,128)S(1)} copy(f32[128,4096]{1,0:T(8,128)} %fusion) | data formatting | bytes 4194304 | tf_op jit(solution)/shard_map/convert_element_type | solution.py:74
  96.7 1.5 fusion.21
  98.1 1.6 %copy.33 = f32[128,1,2048]{2,0,1:T(8,128)S(1)} copy(f32[128,1,2048]{0,2,1:T(8,128)} %get-tuple-element.12) | data formatting | bytes 2097152
  99.7 1.6 %copy.32 = f32[128,1,2048]{2,0,1:T(8,128)S(1)} copy(f32[128,1,2048]{0,2,1:T(8,128)} %get-tuple-element.13) | data formatting | bytes 2097152
  101.3 3.5 %fusion.22 = (bf16[128,2048]{1,0:T(8,128)(2,1)}, f32[128,2048]{1,0:T(8,128)}) fusion(f32[128]{0:T(128)S(1)} %get-tuple-element.16, f32[128,1,2048]{2,0,1:T(8,128)S(1)} %copy.33, bf16[128,2048]{1,0:T(8,128)(2,1)} %reduce-scatter.2.cloned.1.call-done, f32[128]{0:T(128)S(1)} %get-tuple-element.17, f32[128,1,2048]{2,0,1:T(8,128)S(1)} %copy.32, ...), kind=kOutput, calls=%fused_computation.58 | convolution fusion | flops 138706944 | bytes 5244416 | tf_op jit(solution)/shard_map/dot_general | solution.py:20
  104.9 1.7 %fusion.18 = (f32[128]{0:T(128)S(1)}, f32[128]{0:T(128)S(1)}) fusion(bf16[128,2048]{1,0:T(8,128)(2,1)} %reduce-scatter.2.cloned.1.call-done, f32[128]{0:T(128)S(1)} %get-tuple-element.16, f32[128,1,2048]{2,0,1:T(8,128)S(1)} %copy.33, f32[128]{0:T(128)S(1)} %get-tuple-element.17, f32[128,1,2048]{2,0,1:T(8,128)S(1)} %copy.32), kind=kLoop, calls=%fused_computation.54 | loop fusion | flops 3407616 | bytes 2623488 | tf_op jit(solution)/shard_map/reduce_max | solution.py:29
  106.5 0.5 fusion.19
  107.1 1.4 divide_convert_fusion
  108.5 25.1 %all-gather.2.cloned.1.call-done = bf16[1024,2048]{1,0:T(8,128)(2,1)} async-done(((bf16[128,2048]{1,0:T(8,128)(2,1)}), bf16[1024,2048]{1,0:T(8,128)(2,1)}) %all-gather.2.cloned.1.call-update) | async-done | bytes 4194320 | tf_op jit(solution)/shard_map/all_gather | solution.py:86
  133.6 4.8 %copy.36 = bf16[1024,2048]{1,0:T(8,128)(2,1)} copy(bf16[1024,2048]{1,0:T(8,128)(2,1)} %all-gather.2.cloned.1.call-done) | data formatting | bytes 8388608
  (28 shorter events, 1.1 us)
Async XLA Ops:
  7.2 15.1 %copy-start = (f32[128,2048]{1,0:T(8,128)S(1)}, f32[128,2048]{1,0:T(8,128)}, u32[]{:S(2)}) copy-start(f32[128,2048]{1,0:T(8,128)} %param.8) | copy-start | bytes 3145732
  7.2 94.1 %reduce-scatter.2.cloned.1.call-start = ((), (), s32[]{:S(2)}) async-start(), calls=%async_computation.4 | async-start | bytes 4718592 | tf_op jit(solution)/shard_map/reduce_scatter | solution.py:39
  7.2 0.9 copy-start.4
  7.2 2.4 %copy-start.5 = (bf16[128]{0:T(256)(128)(2,1)S(1)}, bf16[128]{0:T(256)(128)(2,1)}, u32[]{:S(2)}) copy-start(bf16[128]{0:T(256)(128)(2,1)} %param.12) | copy-start | bytes 772
  7.2 2.4 %copy-start.6 = (bf16[128]{0:T(256)(128)(2,1)S(1)}, bf16[128]{0:T(256)(128)(2,1)}, u32[]{:S(2)}) copy-start(bf16[128]{0:T(256)(128)(2,1)} %param.10) | copy-start | bytes 772
  10.7 20.9 %all-to-all-start.2 = ((bf16[128,2,2]{1,2,0:T(2,128)(2,1)}), bf16[128,2,2]{1,2,0:T(2,128)(2,1)S(1)}, u32[]{:S(2)}, u32[]{:S(2)}) async-start(bf16[128,2,2]{1,2,0:T(2,128)(2,1)} %copy.29), calls=%async_computation.2 | async-start | bytes 131072 | tf_op jit(solution)/shard_map/all_to_all | solution.py:67
  23.3 13.8 %copy-start.2 = (bf16[128,2048]{1,0:T(8,128)(2,1)S(1)}, bf16[128,2048]{1,0:T(8,128)(2,1)}, u32[]{:S(2)}) copy-start(bf16[128,2048]{1,0:T(8,128)(2,1)} %param.9) | copy-start | bytes 1572868
  23.3 14.0 %copy-start.3 = (bf16[128,2048]{1,0:T(8,128)(2,1)S(1)}, bf16[128,2048]{1,0:T(8,128)(2,1)}, u32[]{:S(2)}) copy-start(bf16[128,2048]{1,0:T(8,128)(2,1)} %param.11) | copy-start | bytes 1572868
  31.7 24.2 %all-to-all-start = ((bf16[128,2,2048]{2,1,0:T(2,128)(2,1)}), bf16[128,2,2048]{2,1,0:T(2,128)(2,1)}, u32[]{:S(2)}, u32[]{:S(2)}) async-start(bf16[128,2,2048]{2,1,0:T(2,128)(2,1)} %convert_element_type.77), calls=%async_computation | async-start | bytes 2097152 | tf_op jit(solution)/shard_map/all_to_all | solution.py:69
  55.9 36.2 %all-to-all-start.1 = ((bf16[128,2,2,2048]{3,2,1,0:T(2,128)(2,1)}), bf16[128,2,2,2048]{3,2,1,0:T(2,128)(2,1)S(1)}, u32[]{:S(2)}, u32[]{:S(2)}) async-start(bf16[128,2,2,2048]{3,2,1,0:T(2,128)(2,1)} %reshape_reshape.6), calls=%async_computation.1 | async-start | bytes 4194304 | tf_op jit(solution)/shard_map/all_to_all | solution.py:66
  61.7 72.0 %all-gather.2.cloned.1.call-start = ((), (), s32[]{:S(2)}) async-start(), calls=%async_computation.5 | async-start | bytes 4718592 | tf_op jit(solution)/shard_map/all_gather | solution.py:86
  104.9 2.2 %copy-start.1 = (bf16[128,2048]{1,0:T(8,128)(2,1)S(1)}, bf16[128,2048]{1,0:T(8,128)(2,1)}, u32[]{:S(2)}) copy-start(bf16[128,2048]{1,0:T(8,128)(2,1)} %reduce-scatter.2.cloned.1.call-done) | copy-start | bytes 1572868
Sparse Core Ops, SparseCore 0:
  10.4 50.0 reduce-scatter.1
  105.0 28.6 all-gather.1
where the time goes:
time: 146 us; the launch traced here: 145 us
  waiting for transfers between devices  74.5 us (51%)
  starting transfers between devices  22.9 us (16%)
  local copies, waits for them, and re-layouts  20.5 us (14%)
  between operations  14.3 us (10%)
  matrix products  7.42 us (5%)
  other arithmetic  5.6 us (4%)
    all_to_all x1, waiting for transfers between devices, local(): lax.all_to_all(code_buffer, ('fsdp', 'dp'), split_axis=0, concat_axis=0,...  27.1 us
    all_gather x1, waiting for transfers between devices, local(): lax.all_gather(master.astype(jnp.bfloat16), 'dp', axis=0, tiled=True)  25.1 us
    all_to_all x1, waiting for transfers between devices, local(): lax.all_to_all(master_buffer.astype(jnp.bfloat16), ('fsdp', 'dp'), split_...  14.7 us
    all_to_all x1, starting transfers between devices, local(): lax.all_to_all(scale_buffer, ('fsdp', 'dp'), split_axis=0, concat_axis=0,...  11.5 us
    unnamed x20, local copies, waits for them, and re-layouts  9.58 us
    all_to_all x1, waiting for transfers between devices, local(): lax.all_to_all(scale_buffer, ('fsdp', 'dp'), split_axis=0, concat_axis=0,...  6.87 us
    all_to_all x1, starting transfers between devices, local(): lax.all_to_all(code_buffer, ('fsdp', 'dp'), split_axis=0, concat_axis=0,...  5.78 us
    all_to_all x1, starting transfers between devices, local(): lax.all_to_all(master_buffer.astype(jnp.bfloat16), ('fsdp', 'dp'), split_...  5.36 us
  transfers between devices with their start and end apart: 5, of which 4 were waited for; matrix products, arithmetic and copies ran while one was open for 17% of the time, Pallas kernels for 0%

commit v1 on v0

v1 whole, which is shorter than its diff:
```python
import functools

import jax
import jax.numpy as jnp
from jax import lax
from jax.experimental import pallas as pl
from jax.experimental.pallas import tpu as pltpu
from jax.sharding import PartitionSpec as P

ALL = ("fsdp", "dp")
LANES = 128
SUB = 8


def to_tiles(values):
    rows, cols = values.shape
    tiled = values.reshape(rows // SUB, SUB, cols // LANES, LANES)
    return tiled.transpose(0, 2, 1, 3).reshape(rows * cols // LANES, LANES)


def from_tiles(values, rows, cols):
    tiled = values.reshape(rows // SUB, cols // LANES, SUB, LANES)
    return tiled.transpose(0, 2, 1, 3).reshape(rows, cols)


def pair_rank(owners, keyed):
    matching = owners[:, None] == owners[None, :]
    before = keyed[None, :] < keyed[:, None]
    return jnp.sum(jnp.where(matching & before, 1, 0), axis=1).astype(jnp.int32)


def pack_kernel(rows, chunks, slot_ref, mscale_ref, sscale_ref, master_ref, mean_ref, square_ref, out_ref, wide_mean, wide_square):
    wide_mean[...] = mean_ref[...].astype(jnp.float32)
    wide_square[...] = square_ref[...].astype(jnp.float32)
    for row in range(rows):
        base = (row // SUB) * chunks * SUB + row % SUB
        spots = pl.ds(base, chunks, stride=SUB)
        slot = slot_ref[row]
        out_ref[slot, pl.ds(0, chunks), :] = master_ref[spots, :].astype(jnp.bfloat16)
        out_ref[slot, pl.ds(chunks, chunks), :] = (wide_mean[spots, :] * mscale_ref[row]).astype(jnp.bfloat16)
        out_ref[slot, pl.ds(2 * chunks, chunks), :] = (wide_square[spots, :] * sscale_ref[row]).astype(jnp.bfloat16)


def pack(slots, mean_scale, square_scale, master, mean, square, slot_total):
    rows, cols = master.shape
    chunks = cols // LANES
    smem = pl.BlockSpec(memory_space=pltpu.SMEM)
    vmem = pl.BlockSpec(memory_space=pltpu.VMEM)
    flat = (rows * chunks, LANES)
    return pl.pallas_call(
        functools.partial(pack_kernel, rows, chunks),
        out_shape=jax.ShapeDtypeStruct((slot_total, 3 * chunks, LANES), jnp.bfloat16),
        in_specs=[smem, smem, smem, vmem, vmem, vmem],
        out_specs=vmem,
        scratch_shapes=[pltpu.VMEM(flat, jnp.float32), pltpu.VMEM(flat, jnp.float32)],
        compiler_params=pltpu.CompilerParams(vmem_limit_bytes=24 * 1024 * 1024),
        name="pack",
    )(slots, mean_scale, square_scale, to_tiles(master), to_tiles(mean), to_tiles(square))


def adam_kernel(rows, chunks, slot_ref, in_ref, grad_ref, weights_ref, master_ref, mcode_ref, scode_ref, mscale_ref, sscale_ref, weight_old, mean_old, square_old):
    span = chunks * SUB
    lane = lax.broadcasted_iota(jnp.int32, (SUB, LANES), 1)
    sub = lax.broadcasted_iota(jnp.int32, (SUB, LANES), 0)
    mline = jnp.zeros((SUB, LANES), jnp.float32)
    sline = jnp.zeros((SUB, LANES), jnp.float32)
    for group in range(rows // SUB):
        buf = group % 2
        for r in range(SUB):
            slot = slot_ref[group * SUB + r]
            spots = pl.ds(buf * span + r, chunks, stride=SUB)
            weight_old[spots, :] = in_ref[slot, pl.ds(0, chunks), :].astype(jnp.float32)
            mean_old[spots, :] = in_ref[slot, pl.ds(chunks, chunks), :].astype(jnp.float32)
            square_old[spots, :] = in_ref[slot, pl.ds(2 * chunks, chunks), :].astype(jnp.float32)
        here = pl.ds(buf * span, span)
        there = pl.ds(group * span, span)
        gradient = grad_ref[there, :].astype(jnp.float32)
        old = weight_old[here, :]
        mean_next = 0.9 * mean_old[here, :] + 0.1 * gradient
        square_next = 0.95 * square_old[here, :] + 0.05 * gradient * gradient
        master = old - 0.05 * (mean_next / (jnp.sqrt(square_next) + 1e-08) + 0.1 * old)
        master_ref[there, :] = master
        weights_ref[there, :] = master.astype(jnp.bfloat16)
        mean_next = mean_next.reshape(chunks, SUB, LANES)
        square_next = square_next.reshape(chunks, SUB, LANES)
        mpeak = jnp.max(jnp.max(jnp.abs(mean_next), axis=0), axis=1, keepdims=True)
        speak = jnp.max(jnp.max(square_next, axis=0), axis=1, keepdims=True)
        mscale = (mpeak + 1e-06).astype(jnp.bfloat16).astype(jnp.float32)
        sscale = (speak + 1e-06).astype(jnp.bfloat16).astype(jnp.float32)
        mcode_ref[there, :] = (mean_next * (1.0 / mscale)[None]).reshape(span, LANES).astype(jnp.bfloat16)
        scode_ref[there, :] = (square_next * (1.0 / sscale)[None]).reshape(span, LANES).astype(jnp.bfloat16)
        mine = lane == sub + group * SUB
        mline = jnp.where(mine, mscale, mline)
        sline = jnp.where(mine, sscale, sline)
    mscale_ref[...] = jnp.sum(mline, axis=0, keepdims=True).astype(jnp.bfloat16)
    sscale_ref[...] = jnp.sum(sline, axis=0, keepdims=True).astype(jnp.bfloat16)


def adam(slots, arrived, gradient):
    rows, cols = gradient.shape
    chunks = cols // LANES
    smem = pl.BlockSpec(memory_space=pltpu.SMEM)
    vmem = pl.BlockSpec(memory_space=pltpu.VMEM)
    flat = (rows * chunks, LANES)
    bf16, f32 = jnp.bfloat16, jnp.float32
    stage = pltpu.VMEM((2 * chunks * SUB, LANES), f32)
    outs = pl.pallas_call(
        functools.partial(adam_kernel, rows, chunks),
        out_shape=[
            jax.ShapeDtypeStruct(flat, bf16),
            jax.ShapeDtypeStruct(flat, f32),
            jax.ShapeDtypeStruct(flat, bf16),
            jax.ShapeDtypeStruct(flat, bf16),
            jax.ShapeDtypeStruct((1, rows), bf16),
            jax.ShapeDtypeStruct((1, rows), bf16),
        ],
        in_specs=[smem, vmem, vmem],
        out_specs=[vmem] * 6,
        scratch_shapes=[stage, stage, stage],
        compiler_params=pltpu.CompilerParams(vmem_limit_bytes=24 * 1024 * 1024),
        name="adam",
    )(slots, arrived, to_tiles(gradient))
    blocks = [from_tiles(x, rows, cols) for x in outs[:4]]
    return (*blocks, outs[4].reshape(rows), outs[5].reshape(rows))


def routes(old_map, block_rows, peer_cap):
    self_index = lax.axis_index(ALL)
    my_slots = self_index * block_rows + jnp.arange(block_rows, dtype=jnp.int32)
    block_ids = jnp.arange(old_map.shape[0], dtype=jnp.int32)
    held = jnp.sum(jnp.where(old_map[None, :] == my_slots[:, None], block_ids[None, :], 0), axis=1)
    target = held // block_rows
    sent_rank = pair_rank(target, held % block_rows)
    wanted = lax.dynamic_slice_in_dim(old_map, self_index * block_rows, block_rows)
    source = wanted // block_rows
    got_rank = pair_rank(source, jnp.arange(block_rows, dtype=jnp.int32))
    return target * peer_cap + sent_rank, source * peer_cap + got_rank


def local(grad_parts, old_master, old_mean, old_mean_scale, old_square, old_square_scale, old_map):
    count_all = lax.axis_size(ALL)
    block_rows, block_len = old_master.shape
    peer_cap = 2
    slot_total = count_all * peer_cap
    chunks = block_len // LANES
    gradient = lax.psum_scatter(grad_parts[0], "dp", scatter_dimension=0, tiled=True)
    send_slot, recv_slot = routes(old_map, block_rows, peer_cap)
    packed = pack(
        send_slot,
        old_mean_scale.astype(jnp.float32),
        old_square_scale.astype(jnp.float32),
        old_master,
        old_mean,
        old_square,
        slot_total,
    )
    arrived = lax.all_to_all(
        packed.reshape(count_all, peer_cap * 3 * chunks, LANES), ALL, split_axis=0, concat_axis=0, tiled=True
    ).reshape(slot_total, 3 * chunks, LANES)
    mine, master, mean_codes, square_codes, mean_scales, square_scales = adam(recv_slot, arrived, gradient)
    weights = lax.all_gather(mine, "dp", axis=0, tiled=True)
    return (weights, master, mean_codes, mean_scales, square_codes, square_scales)


def solution(mesh):
    in_specs = (
        P("dp", "fsdp", None),
        P(ALL, None),
        P(ALL, None),
        P(ALL),
        P(ALL, None),
        P(ALL),
        P(),
    )
    out_specs = (
        P("fsdp", None),
        P(ALL, None),
        P(ALL, None),
        P(ALL),
        P(ALL, None),
        P(ALL),
    )
    return jax.shard_map(local, mesh=mesh, in_specs=in_specs, out_specs=out_specs, check_vma=False)
```

time: 146 us -> 133 us (0.911)
  waiting for transfers between devices: 74.5 us -> 92.8 us
  local copies, waits for them, and re-layouts: 20.5 us -> 6.65 us
  starting transfers between devices: 22.9 us -> 11.6 us
  matrix products: 7.42 us -> 0 us
  Pallas kernels: 0 us -> 6.03 us
  other arithmetic: 5.6 us -> 1.89 us
    reduce_scatter x1, waiting for transfers between devices: 0.02 us -> 16.2 us  [local(): lax.psum_scatter(grad_parts[0], 'dp', scatter_dimension=0, tiled=True)]
    all_to_all x3 -> x1, starting transfers between devices: 22.6 us -> 11.5 us  [local(): lax.all_to_all(packed.reshape(count_all, peer_cap * 3 * chunks, LANES), A...]
    all_gather x1, waiting for transfers between devices: 25.1 us -> 34.6 us  [local(): weights = lax.all_gather(mine, 'dp', axis=0, tiled=True)]
    dot_general x6 -> x0, matrix products: 7.42 us -> none  [the longest x2 4.54 us: route_f32(): jnp.dot(chooser.astype(jnp.float32), values, precision=lax.Precision.HIGH...]
    all_to_all x3 -> x1, waiting for transfers between devices: 48.7 us -> 41.3 us  [local(): lax.all_to_all(packed.reshape(count_all, peer_cap * 3 * chunks, LANES), A...]
    pallas_call x0 -> x2, Pallas kernels: none -> 6.03 us  [the longest x1 3.19 us: adam(): pl.pallas_call(functools.partial(adam_kernel, rows, chunks), out_shape=[j...]
    convert_element_type x2 -> x0, local copies, waits for them, and re-layouts: 3.41 us -> none  [the longest x1 1.91 us: local(): route_bf16(picking, code_in.reshape((slot_total, 2, block_len)))]
    reshape x4 -> x0, local copies, waits for them, and re-layouts: 3.31 us -> none  [the longest x1 2.29 us: local(): weight_old = route_f32(picking, master_in.reshape((slot_total, block_len)))]
  transfers between devices with their start and end apart: 5 -> 3, of which waited for: 4 -> 3; matrix products, arithmetic and copies ran while one was open for 17% -> 1% of each run, Pallas kernels for 0% -> 2%
where the time goes in v1:
time: 133 us
  waiting for transfers between devices  92.8 us (70%)
  between operations  14.2 us (11%)
  starting transfers between devices  11.6 us (9%)
  local copies, waits for them, and re-layouts  6.65 us (5%)
  Pallas kernels  6.03 us (5%)
  other arithmetic  1.89 us (1%)
    all_to_all x1, waiting for transfers between devices, local(): lax.all_to_all(packed.reshape(count_all, peer_cap * 3 * chunks, LANES), A...  41.3 us
    all_gather x1, waiting for transfers between devices, local(): weights = lax.all_gather(mine, 'dp', axis=0, tiled=True)  34.6 us
    reduce_scatter x1, waiting for transfers between devices, local(): lax.psum_scatter(grad_parts[0], 'dp', scatter_dimension=0, tiled=True)  16.2 us
    all_to_all x1, starting transfers between devices, local(): lax.all_to_all(packed.reshape(count_all, peer_cap * 3 * chunks, LANES), A...  11.5 us
    unnamed x17, local copies, waits for them, and re-layouts  6.65 us
    pallas_call x1, Pallas kernels, adam(): pl.pallas_call(functools.partial(adam_kernel, rows, chunks), out_shape=[j...  3.19 us
    pallas_call x1, Pallas kernels, pack(): pl.pallas_call(functools.partial(pack_kernel, rows, chunks), out_shape=ja...  2.84 us
  transfers between devices with their start and end apart: 3, of which 3 were waited for; matrix products, arithmetic and copies ran while one was open for 1% of the time, Pallas kernels for 2%

profile of v1, /device:TPU:1, one launch (start us, length us, event | category | flops | bytes accessed | tf_op | source)
XLA Modules:
  0.0 133.2 jit_solution(4700605151909884730)
XLA Ops:
  7.2 0.0 copy-start.6
  7.2 0.0 copy-start.7
  7.2 0.0 copy-start.5
  7.2 0.0 copy-start.2
  7.2 0.0 copy-start.1
  7.2 0.0 copy-start
  7.2 0.0 reduce-scatter.2.cloned.1.call-start
  7.3 0.7 reduce-scatter.2.cloned.1.call-update
  8.0 0.0 copy-done.6
  8.0 0.0 copy-done.7
  8.0 0.0 copy-done.5
  8.0 1.3 select_reduce_fusion
  9.4 0.2 select_reduce_fusion.1
  9.6 0.0 copy-done.2
  9.6 0.0 copy-done.1
  9.6 0.0 copy-done
  9.6 2.8 %pack.1 = bf16[256,48,128]{2,1,0:T(8,128)(2,1)} custom-call(s32[128]{0:T(128)S(1)} %multiply_add_fusion.slot_ref, f32[128]{0:T(128)S(1)} %convert_element_type.6.mscale_ref, f32[128]{0:T(128)S(1)} %convert_element_type.7.sscale_ref, f32[2048,128]{1,0:T(8,128)S(1)} %bitcast.46, bf16[2048,128]{1,0:T(8,128)(2,1)S(1)} %bitcast.47, bf16[2048,128]{1,0:T(8,128)(2,1)S(1)} %bitcast.48), custom_call_target="tpu_custom_call" | custom-call | tf_op jit(solution)/shard_map/pack/pallas_call | solution.py:50
  12.5 11.5 %all-to-all-start = ((bf16[128,96,128]{2,1,0:T(8,128)(2,1)}), bf16[128,96,128]{2,1,0:T(8,128)(2,1)S(1)}, u32[]{:S(2)}, u32[]{:S(2)}) async-start(bf16[128,96,128]{2,1,0:T(8,128)(2,1)} %bitcast.9), calls=%async_computation | async-start | bytes 6291456 | tf_op jit(solution)/shard_map/all_to_all | solution.py:157
  24.0 0.0 all-gather.2.cloned.1.call-start
  24.0 0.1 and_select_fusion.2
  24.1 0.2 select_reduce_fusion.2
  24.3 0.1 multiply_add_fusion.1.slot_ref
  24.4 41.3 %all-to-all-done = bf16[128,96,128]{2,1,0:T(8,128)(2,1)S(1)} async-done(((bf16[128,96,128]{2,1,0:T(8,128)(2,1)}), bf16[128,96,128]{2,1,0:T(8,128)(2,1)S(1)}, u32[]{:S(2)}, u32[]{:S(2)}) %all-to-all-start) | async-done | bytes 3145760 | tf_op jit(solution)/shard_map/all_to_all | solution.py:157
  65.7 16.2 %reduce-scatter.2.cloned.1.call-done = bf16[128,2048]{1,0:T(8,128)(2,1)} async-done(((bf16[1024,2048]{1,0:T(8,128)(2,1)}), bf16[128,2048]{1,0:T(8,128)(2,1)}) %reduce-scatter.2.cloned.1.call-update) | async-done | bytes 524304 | tf_op jit(solution)/shard_map/reduce_scatter | solution.py:146
  81.9 0.0 copy-start.4
  81.9 1.0 copy-done.4
  82.9 3.2 %adam.1 = (bf16[2048,128]{1,0:T(8,128)(2,1)S(1)}, f32[2048,128]{1,0:T(8,128)}, bf16[2048,128]{1,0:T(8,128)(2,1)}, bf16[2048,128]{1,0:T(8,128)(2,1)}, bf16[1,128]{1,0:T(2,128)(2,1)}, /*index=5*/bf16[1,128]{1,0:T(2,128)(2,1)}) custom-call(s32[128]{0:T(128)S(1)} %multiply_add_fusion.1.slot_ref, bf16[256,48,128]{2,1,0:T(8,128)(2,1)S(1)} %bitcast.45, ...), custom_call_target="tpu_custom_call" | custom-call | tf_op jit(solution)/shard_map/adam/pallas_call | solution.py:107
  86.1 0.0 copy-start.3
  86.1 0.8 copy-done.3
  86.9 0.0 all-gather.2.cloned.1.call-update
  86.9 34.6 %all-gather.2.cloned.1.call-done = bf16[1024,2048]{1,0:T(8,128)(2,1)} async-done(((bf16[128,2048]{1,0:T(8,128)(2,1)}), bf16[1024,2048]{1,0:T(8,128)(2,1)}) %all-gather.2.cloned.1.call-update) | async-done | bytes 4194320 | tf_op jit(solution)/shard_map/all_gather | solution.py:161
  121.5 4.8 %copy.14 = bf16[1024,2048]{1,0:T(8,128)(2,1)} copy(bf16[1024,2048]{1,0:T(8,128)(2,1)} %all-gather.2.cloned.1.call-done) | data formatting | bytes 8388608
  (5 shorter events, 0.0 us)
Async XLA Ops:
  7.2 0.8 copy-start.6
  7.2 0.8 copy-start.7
  7.2 0.9 copy-start.5
  7.2 2.4 %copy-start.2 = (bf16[128,2048]{1,0:T(8,128)(2,1)S(1)}, bf16[128,2048]{1,0:T(8,128)(2,1)}, u32[]{:S(2)}) copy-start(bf16[128,2048]{1,0:T(8,128)(2,1)} %param.11) | copy-start | bytes 1572868
  7.2 2.4 %copy-start.1 = (bf16[128,2048]{1,0:T(8,128)(2,1)S(1)}, bf16[128,2048]{1,0:T(8,128)(2,1)}, u32[]{:S(2)}) copy-start(bf16[128,2048]{1,0:T(8,128)(2,1)} %param.9) | copy-start | bytes 1572868
  7.2 2.4 %copy-start = (f32[128,2048]{1,0:T(8,128)S(1)}, f32[128,2048]{1,0:T(8,128)}, u32[]{:S(2)}) copy-start(f32[128,2048]{1,0:T(8,128)} %param.8) | copy-start | bytes 3145732
  7.2 74.6 %reduce-scatter.2.cloned.1.call-start = ((), (), s32[]{:S(2)}) async-start(), calls=%async_computation.2 | async-start | bytes 4718592 | tf_op jit(solution)/shard_map/reduce_scatter | solution.py:146
  12.5 53.2 %all-to-all-start = ((bf16[128,96,128]{2,1,0:T(8,128)(2,1)}), bf16[128,96,128]{2,1,0:T(8,128)(2,1)S(1)}, u32[]{:S(2)}, u32[]{:S(2)}) async-start(bf16[128,96,128]{2,1,0:T(8,128)(2,1)} %bitcast.9), calls=%async_computation | async-start | bytes 6291456 | tf_op jit(solution)/shard_map/all_to_all | solution.py:157
  24.0 97.6 %all-gather.2.cloned.1.call-start = ((), (), s32[]{:S(2)}) async-start(), calls=%async_computation.3 | async-start | bytes 4718592 | tf_op jit(solution)/shard_map/all_gather | solution.py:161
  81.9 1.0 copy-start.4
  86.1 0.8 copy-start.3
Sparse Core Ops, SparseCore 0:
  10.5 71.3 reduce-scatter.1
  87.0 34.4 all-gather.1

commit v2 on v1

--- a/solution.py
+++ b/solution.py
@@ -10,6 +10,11 @@
 ALL = ("fsdp", "dp")
 LANES = 128
 SUB = 8
+RING = 4
+CORES = 2
+STEPS = (2, 1, 3, 0)
+FAR = ((2, 0), (2, 1), (1, 1), (3, 0))
+NEAR = ((1, 0), (3, 1))
 
 
 def to_tiles(values):
@@ -58,7 +63,7 @@
     )(slots, mean_scale, square_scale, to_tiles(master), to_tiles(mean), to_tiles(square))
 
 
-def adam_kernel(rows, chunks, slot_ref, in_ref, grad_ref, weights_ref, master_ref, mcode_ref, scode_ref, mscale_ref, sscale_ref, weight_old, mean_old, square_old):
+def adam_kernel(rows, chunks, slot_ref, in_ref, own_ref, sib_ref, up_lo_ref, up_hi_ref, dn_lo_ref, dn_hi_ref, weights_ref, master_ref, mcode_ref, scode_ref, mscale_ref, sscale_ref, weight_old, mean_old, square_old):
     span = chunks * SUB
     lane = lax.broadcasted_iota(jnp.int32, (SUB, LANES), 1)
     sub = lax.broadcasted_iota(jnp.int32, (SUB, LANES), 0)
@@ -74,7 +79,11 @@
             square_old[spots, :] = in_ref[slot, pl.ds(2 * chunks, chunks), :].astype(jnp.float32)
         here = pl.ds(buf * span, span)
         there = pl.ds(group * span, span)
-        gradient = grad_ref[there, :].astype(jnp.float32)
+        low = group < rows // SUB // 2
+        part = there if low else pl.ds((group - rows // SUB // 2) * span, span)
+        up_ref, dn_ref = (up_lo_ref, dn_lo_ref) if low else (up_hi_ref, dn_hi_ref)
+        gradient = own_ref[there, :].astype(jnp.float32) + sib_ref[there, :].astype(jnp.float32)
+        gradient += up_ref[part, :].astype(jnp.float32) + dn_ref[part, :].astype(jnp.float32)
         old = weight_old[here, :]
         mean_next = 0.9 * mean_old[here, :] + 0.1 * gradient
         square_next = 0.95 * square_old[here, :] + 0.05 * gradient * gradient
@@ -96,14 +105,11 @@
     sscale_ref[...] = jnp.sum(sline, axis=0, keepdims=True).astype(jnp.bfloat16)
 
 
-def adam(slots, arrived, gradient):
-    rows, cols = gradient.shape
-    chunks = cols // LANES
-    smem = pl.BlockSpec(memory_space=pltpu.SMEM)
-    vmem = pl.BlockSpec(memory_space=pltpu.VMEM)
+def adam(slots, arrived, grads, rows, chunks):
     flat = (rows * chunks, LANES)
     bf16, f32 = jnp.bfloat16, jnp.float32
     stage = pltpu.VMEM((2 * chunks * SUB, LANES), f32)
+    vmem = pl.BlockSpec(memory_space=pltpu.VMEM)
     outs = pl.pallas_call(
         functools.partial(adam_kernel, rows, chunks),
         out_shape=[
@@ -114,14 +120,171 @@
             jax.ShapeDtypeStruct((1, rows), bf16),
             jax.ShapeDtypeStruct((1, rows), bf16),
         ],
-        in_specs=[smem, vmem, vmem],
+        in_specs=[pl.BlockSpec(memory_space=pltpu.SMEM)] + [vmem] * 7,
         out_specs=[vmem] * 6,
         scratch_shapes=[stage, stage, stage],
         compiler_params=pltpu.CompilerParams(vmem_limit_bytes=24 * 1024 * 1024),
         name="adam",
-    )(slots, arrived, to_tiles(gradient))
-    blocks = [from_tiles(x, rows, cols) for x in outs[:4]]
-    return (*blocks, outs[4].reshape(rows), outs[5].reshape(rows))
+    )(slots, arrived, *grads)
+    return outs
+
+
+def place():
+    me = lax.axis_index("dp")
+    return me // CORES, me % CORES
+
+
+def shard_at(y, step, core):
+    return lax.rem(y + step, RING) * CORES + core
+
+
+def sends(shift, flip):
+    return [
+        (y * CORES + c, (y + shift) % RING * CORES + (CORES - 1 - c if flip else c))
+        for y in range(RING)
+        for c in range(CORES)
+    ]
+
+
+def send(values, shift, flip=False):
+    return lax.ppermute(values, "dp", sends(shift, flip))
+
+
+def cut_kernel(grad_ref, far_ref, near_ref, sems):
+    y, core = place()
+    copies = []
+    for k, step in enumerate(STEPS):
+        target = far_ref.at[k] if k < 3 else near_ref
+        copies.append(pltpu.make_async_copy(grad_ref.at[shard_at(y, step, CORES - 1 - core)], target, sems.at[k]))
+    for copy in copies:
+        copy.start()
+    for copy in copies:
+        copy.wait()
+
+
+def cut(grads):
+    _, span, lanes = grads.shape
+    hbm = pl.BlockSpec(memory_space=pltpu.HBM)
+    return pl.pallas_call(
+        cut_kernel,
+        out_shape=[
+            jax.ShapeDtypeStruct((3, span, lanes), grads.dtype),
+            jax.ShapeDtypeStruct((span, lanes), grads.dtype),
+        ],
+        in_specs=[hbm],
+        out_specs=[hbm, hbm],
+        scratch_shapes=[pltpu.SemaphoreType.DMA((4,))],
+        name="cut",
+    )(grads)
+
+
+def keep_kernel(half, grad_ref, far_ref, near_ref, own_ref, sems):
+    y, core = place()
+    jobs = [(step, part * half, half, far_ref.at[k]) for k, (step, part) in enumerate(FAR)]
+    jobs += [(step, part * half, half, near_ref.at[k]) for k, (step, part) in enumerate(NEAR)]
+    jobs += [(0, 0, 2 * half, own_ref)]
+    copies = [
+        pltpu.make_async_copy(grad_ref.at[shard_at(y, step, core), pl.ds(start, size)], target, sems.at[k])
+        for k, (step, start, size, target) in enumerate(jobs)
+    ]
+    for copy in copies:
+        copy.start()
+    for copy in copies:
+        copy.wait()
+
+
+def keep(grads):
+    _, span, lanes = grads.shape
+    half = span // 2
+    hbm = pl.BlockSpec(memory_space=pltpu.HBM)
+    shapes = [(len(FAR), half, lanes), (len(NEAR), half, lanes), (span, lanes)]
+    return pl.pallas_call(
+        functools.partial(keep_kernel, half),
+        out_shape=[jax.ShapeDtypeStruct(shape, grads.dtype) for shape in shapes],
+        in_specs=[hbm],
+        out_specs=[hbm] * 3,
+        scratch_shapes=[pltpu.SemaphoreType.DMA((len(FAR) + len(NEAR) + 1,))],
+        name="keep",
+    )(grads)
+
+
+def add_kernel(half, jobs, own_ref, got_ref, *refs):
+    more_refs, out_refs = refs[: -len(jobs)], refs[-len(jobs) :]
+    for k, (step, part) in enumerate(jobs):
+        total = own_ref[k].astype(jnp.float32)
+        total += got_ref[STEPS.index(step), pl.ds(part * half, half), :].astype(jnp.float32)
+        if more_refs:
+            total += more_refs[k][...].astype(jnp.float32)
+        out_refs[k][...] = total.astype(own_ref.dtype)
+
+
+def add(jobs, own, got, *more):
+    _, half, lanes = own.shape
+    vmem = pl.BlockSpec(memory_space=pltpu.VMEM)
+    return pl.pallas_call(
+        functools.partial(add_kernel, half, jobs),
+        out_shape=[jax.ShapeDtypeStruct((half, lanes), own.dtype)] * len(jobs),
+        in_specs=[vmem] * (2 + len(more)),
+        out_specs=[vmem] * len(jobs),
+        compiler_params=pltpu.CompilerParams(vmem_limit_bytes=16 * 1024 * 1024),
+        name="add_near" if more else "add_far",
+    )(own, got, *more)
+
+
+def reduce_shards(grads, far, near):
+    far_got = send(far, 0, True)
+    near_got = send(near, 0, True)
+    own_far, own_near, own = keep(grads)
+    opp_lo, opp_hi, up_hi, dn_lo = add(FAR, own_far, far_got)
+    up_got = send(opp_lo, 1)
+    dn_got = send(opp_hi, 3)
+    up_hi_got = send(up_hi, 1)
+    dn_lo_got = send(dn_lo, 3)
+    up_lo, dn_hi = add(NEAR, own_near, far_got, up_got, dn_got)
+    up_lo_got = send(up_lo, 1)
+    dn_hi_got = send(dn_hi, 3)
+    return own, near_got, up_lo_got, up_hi_got, dn_lo_got, dn_hi_got
+
+
+def join_kernel(span, starts, *refs):
+    parts, (out_ref, sems) = refs[: len(starts)], refs[-2:]
+    y, core = place()
+    copies = []
+    for k, (step, flip, offset) in enumerate(starts):
+        side = CORES - 1 - core if flip else core
+        base = pl.multiple_of(shard_at(y, step, side) * span + offset, span // 2)
+        copies.append(pltpu.make_async_copy(parts[k], out_ref.at[pl.ds(base, parts[k].shape[0])], sems.at[k]))
+    for copy in copies:
+        copy.start()
+    for copy in copies:
+        copy.wait()
+
+
+def join(span, starts, parts, whole=None):
+    lanes = parts[0].shape[1]
+    hbm = pl.BlockSpec(memory_space=pl.ANY)
+    given = list(parts) + ([] if whole is None else [whole])
+    return pl.pallas_call(
+        functools.partial(join_kernel, span, starts),
+        out_shape=jax.ShapeDtypeStruct((RING * CORES * span, lanes), parts[0].dtype),
+        in_specs=[hbm] * len(given),
+        out_specs=hbm,
+        scratch_shapes=[pltpu.SemaphoreType.DMA((len(parts),))],
+        input_output_aliases={} if whole is None else {len(parts): 0},
+        name="join",
+    )(*given)
+
+
+def gather_shards(mine):
+    span = mine.shape[0]
+    half = span // 2
+    up, dn, sib = send(mine, 1), send(mine, 3), send(mine, 0, True)
+    opp_lo, opp_hi = send(up[:half], 1), send(dn[half:], 3)
+    up_sib, dn_sib = send(up, 0, True), send(dn, 0, True)
+    starts = [(0, 0, 0), (0, 1, 0), (3, 0, 0), (1, 0, 0), (3, 1, 0), (1, 1, 0)]
+    most = join(span, starts, [mine, sib, up, dn, up_sib, dn_sib])
+    starts = [(2, 0, 0), (2, 0, half), (2, 1, 0), (2, 1, half)]
+    return join(span, starts, [opp_lo, opp_hi, send(opp_lo, 0, True), send(opp_hi, 0, True)], most)
 
 
 def routes(old_map, block_rows, peer_cap):
@@ -143,7 +306,9 @@
     peer_cap = 2
     slot_total = count_all * peer_cap
     chunks = block_len // LANES
-    gradient = lax.psum_scatter(grad_parts[0], "dp", scatter_dimension=0, tiled=True)
+    grads = to_tiles(grad_parts[0]).reshape(RING * CORES, block_rows * chunks, LANES)
+    far, near, old_map = lax.optimization_barrier((*cut(grads), old_map))
+    addends = reduce_shards(grads, far, near)
     send_slot, recv_slot = routes(old_map, block_rows, peer_cap)
     packed = pack(
         send_slot,
@@ -157,9 +322,10 @@
     arrived = lax.all_to_all(
         packed.reshape(count_all, peer_cap * 3 * chunks, LANES), ALL, split_axis=0, concat_axis=0, tiled=True
     ).reshape(slot_total, 3 * chunks, LANES)
-    mine, master, mean_codes, square_codes, mean_scales, square_scales = adam(recv_slot, arrived, gradient)
-    weights = lax.all_gather(mine, "dp", axis=0, tiled=True)
-    return (weights, master, mean_codes, mean_scales, square_codes, square_scales)
+    mine, *blocks, mean_scales, square_scales = adam(recv_slot, arrived, addends, block_rows, chunks)
+    master, mean_codes, square_codes = (from_tiles(x, block_rows, block_len) for x in blocks)
+    weights = from_tiles(gather_shards(mine), RING * CORES * block_rows, block_len)
+    return (weights, master, mean_codes, mean_scales.reshape(-1), square_codes, square_scales.reshape(-1))
 
 
 def solution(mesh):

time: 133 us -> 343 us (2.58)
  Pallas kernels: 6.03 us -> 269 us
  waiting for transfers between devices: 92.8 us -> 17.3 us
  starting transfers between devices: 11.6 us -> 38.8 us
  between operations: 14.2 us -> 0.94 us
  local copies, waits for them, and re-layouts: 6.65 us -> 12.2 us
    pallas_call x0 -> x6, Pallas kernels: none -> 263 us  [the longest x2 129 us: join(): pl.pallas_call(functools.partial(join_kernel, span, starts), out_shape=ja...]
    all_to_all x1, waiting for transfers between devices: 41.3 us -> 0.01 us  [local(): lax.all_to_all(packed.reshape(count_all, peer_cap * 3 * chunks, LANES), A...]
    all_gather x1 -> x0, waiting for transfers between devices: 34.6 us -> none  [local(): weights = lax.all_gather(mine, 'dp', axis=0, tiled=True)]
    ppermute x0 -> x17, starting transfers between devices: none -> 27.3 us  [send(): return lax.ppermute(values, 'dp', sends(shift, flip))]
    ppermute x0 -> x17, waiting for transfers between devices: none -> 17.3 us  [send(): return lax.ppermute(values, 'dp', sends(shift, flip))]
    reduce_scatter x1 -> x0, waiting for transfers between devices: 16.2 us -> none  [local(): lax.psum_scatter(grad_parts[0], 'dp', scatter_dimension=0, tiled=True)]
    unnamed x17 -> x48, local copies, waits for them, and re-layouts: 6.65 us -> 12.1 us
  transfers between devices with their start and end apart: 3 -> 18, of which waited for: 3 -> 4; matrix products, arithmetic and copies ran while one was open for 1% -> 0% of each run, Pallas kernels for 2% -> 48%
where the time goes in v2:
time: 343 us; the launch traced here: 342 us
  Pallas kernels  269 us (78%)
  starting transfers between devices  38.8 us (11%)
  waiting for transfers between devices  17.3 us (5%)
  local copies, waits for them, and re-layouts  12.2 us (4%)
    pallas_call x2, Pallas kernels, join(): pl.pallas_call(functools.partial(join_kernel, span, starts), out_shape=ja...  129 us
    pallas_call x1, Pallas kernels, keep(): pl.pallas_call(functools.partial(keep_kernel, half), out_shape=[jax.Shape...  64.7 us
    pallas_call x1, Pallas kernels, cut(): pl.pallas_call(cut_kernel, out_shape=[jax.ShapeDtypeStruct((3, span, lane...  64.7 us
    ppermute x17, starting transfers between devices, send(): return lax.ppermute(values, 'dp', sends(shift, flip))  27.3 us
    ppermute x17, waiting for transfers between devices, send(): return lax.ppermute(values, 'dp', sends(shift, flip))  17.3 us
    unnamed x48, local copies, waits for them, and re-layouts  12.1 us
    all_to_all x1, starting transfers between devices, local(): lax.all_to_all(packed.reshape(count_all, peer_cap * 3 * chunks, LANES), A...  11.5 us
  transfers between devices with their start and end apart: 18, of which 4 were waited for; matrix products, arithmetic and copies ran while one was open for 0% of the time, Pallas kernels for 48%

profile of v2, /device:TPU:1, one launch (start us, length us, event | category | flops | bytes accessed | tf_op | source)
XLA Modules:
  0.0 342.0 jit_solution(10784868408132734036)
XLA Ops:
  0.7 0.8 convert_element_type.6.mscale_ref
  2.2 64.7 %cut.1 = (bf16[3,2048,128]{2,1,0:T(8,128)(2,1)}, bf16[2048,128]{1,0:T(8,128)(2,1)}) custom-call(bf16[8,2048,128]{2,1,0:T(8,128)(2,1)} %bitcast.49), custom_call_target="tpu_custom_call" | custom-call | tf_op jit(solution)/shard_map/cut/pallas_call | solution.py:168
  66.8 1.3 select_reduce_fusion
  68.4 2.8 pack.1
  71.2 11.5 %all-to-all-start = ((bf16[128,96,128]{2,1,0:T(8,128)(2,1)}), bf16[128,96,128]{2,1,0:T(8,128)(2,1)S(1)}, u32[]{:S(2)}, u32[]{:S(2)}) async-start(bf16[128,96,128]{2,1,0:T(8,128)(2,1)} %bitcast.12), calls=%async_computation | async-start | bytes 6291456 | tf_op jit(solution)/shard_map/all_to_all | solution.py:322
  82.7 1.1 collective-permute-start.1
  83.9 64.7 %keep.1 = (bf16[4,1024,128]{2,1,0:T(8,128)(2,1)}, bf16[2,1024,128]{2,1,0:T(8,128)(2,1)}, bf16[2048,128]{1,0:T(8,128)(2,1)}) custom-call(bf16[8,2048,128]{2,1,0:T(8,128)(2,1)} %bitcast.50), custom_call_target="tpu_custom_call" | custom-call | tf_op jit(solution)/shard_map/keep/pallas_call | solution.py:201
  148.6 1.2 copy-done
  149.8 2.3 add_far.1
  154.2 2.0 collective-permute-start.3
  156.9 2.7 collective-permute-start.6
  159.5 3.3 collective-permute-done.2.refs_0_
  162.8 1.0 copy-done.5
  163.9 1.6 add_near.1
  165.9 2.4 collective-permute-start.7
  169.9 3.2 collective-permute-done.4.up_lo_ref
  173.9 1.0 copy-done.6
  174.9 0.9 copy-done.8
  175.9 0.9 copy-done.10
  176.8 0.9 copy-done.12
  177.8 4.0 %adam.1 = (bf16[2048,128]{1,0:T(8,128)(2,1)S(1)}, f32[2048,128]{1,0:T(8,128)}, bf16[2048,128]{1,0:T(8,128)(2,1)}, bf16[2048,128]{1,0:T(8,128)(2,1)}, bf16[1,128]{1,0:T(2,128)(2,1)}, /*index=5*/bf16[1,128]{1,0:T(2,128)(2,1)}) custom-call(s32[128]{0:T(128)S(1)} %multiply_add_fusion.1.slot_ref, bf16[256,48,128]{2,1,0:T(8,128)(2,1)S(1)} %bitcast.44, ...), custom_call_target="tpu_custom_call" | custom-call | tf_op jit(solution)/shard_map/adam/pallas_call | solution.py:113
  181.8 2.3 collective-permute-start.10
  184.2 3.0 collective-permute-start.14
  187.1 5.8 %collective-permute-done.10.refs_3_ = bf16[2048,128]{1,0:T(8,128)(2,1)S(1)} collective-permute-done((bf16[2048,128]{1,0:T(8,128)(2,1)S(1)}, bf16[2048,128]{1,0:T(8,128)(2,1)S(1)}, u32[]{:S(2)}, u32[]{:S(2)}) %collective-permute-start.10) | collective-permute-done | bytes 524320 | tf_op jit(solution)/shard_map/ppermute | solution.py:150
  193.0 3.2 collective-permute-start.11
  196.2 3.9 %collective-permute-start.16 = (bf16[2048,128]{1,0:T(8,128)(2,1)S(1)}, bf16[2048,128]{1,0:T(8,128)(2,1)S(1)}, u32[]{:S(2)}, u32[]{:S(2)}) collective-permute-start(bf16[2048,128]{1,0:T(8,128)(2,1)S(1)} %collective-permute-done.10.refs_3_), channel_id=1, source_target_pairs={{0,1},{1,0},{2,3},{3,2},{4,5},{5,4},{6,7},{7,6},{8,9},{9,8},{10,11... | collective-permute-start | bytes 1572872 | tf_op jit(solution)/shard_map/ppermute | solution.py:150
  200.3 3.7 %collective-permute-start.13 = (bf16[1024,128]{1,0:T(8,128)(2,1)S(1)}, bf16[1024,128]{1,0:T(8,128)(2,1)S(1)}, u32[]{:S(2)}, u32[]{:S(2)}) collective-permute-start(bf16[1024,128]{1,0:T(8,128)(2,1)S(1)} %collective-permute-done.11.refs_1_), channel_id=1, source_target_pairs={{0,1},{1,0},{2,3},{3,2},{4,5},{5,4},{6,7},{7,6},{8,9},{9,8},{10,11... | collective-permute-start | bytes 786440 | tf_op jit(solution)/shard_map/ppermute | solution.py:150
  204.0 5.0 %collective-permute-done.9.refs_0_ = bf16[1024,128]{1,0:T(8,128)(2,1)S(1)} collective-permute-done((bf16[1024,128]{1,0:T(8,128)(2,1)S(1)}, bf16[1024,128]{1,0:T(8,128)(2,1)S(1)}, u32[]{:S(2)}, u32[]{:S(2)}) %collective-permute-start.9) | collective-permute-done | bytes 262176 | tf_op jit(solution)/shard_map/ppermute | solution.py:150
  208.9 1.3 collective-permute-start.12
  211.2 0.8 copy-done.19
  212.0 96.4 %join.2.refs_4_ = bf16[16384,128]{1,0:T(8,128)(2,1)} custom-call(bf16[2048,128]{1,0:T(8,128)(2,1)} %copy-done.2, bf16[2048,128]{1,0:T(8,128)(2,1)} %copy-done.17, bf16[2048,128]{1,0:T(8,128)(2,1)} %copy-done.16, bf16[2048,128]{1,0:T(8,128)(2,1)} %copy-done.15, bf16[2048,128]{1,0:T(8,128)(2,1)} %copy-done.19, bf16[2048,128]{1,0:T(8,128)(2,1)} %copy-done.18), custom_call_target="tpu_custom_call" | custom-call | tf_op jit(solution)/shard_map/join/pallas_call | solution.py:267
  309.1 32.9 %join.3 = bf16[16384,128]{1,0:T(8,128)(2,1)} custom-call(bf16[1024,128]{1,0:T(8,128)(2,1)} %copy-done.21, bf16[1024,128]{1,0:T(8,128)(2,1)} %copy-done.20, bf16[1024,128]{1,0:T(8,128)(2,1)} %collective-permute-done.12.refs_2_, bf16[1024,128]{1,0:T(8,128)(2,1)} %copy-done.22, bf16[16384,128]{1,0:T(8,128)(2,1)} %join.2.refs_4_), custom_call_target="tpu_custom_call", output_to_operand_aliasing={{}: (4, {})} | custom-call | tf_op jit(solution)/shard_map/join/pallas_call | solution.py:267
  (72 shorter events, 8.3 us)
Async XLA Ops:
  0.6 66.2 %copy-start.23 = (s32[16384]{0:T(1024)S(1)}, s32[16384]{0:T(1024)}, u32[]{:S(2)}) copy-start(s32[16384]{0:T(1024)} %param.13) | copy-start | bytes 196612
  0.6 67.7 %copy-start.4 = (bf16[128,2048]{1,0:T(8,128)(2,1)S(1)}, bf16[128,2048]{1,0:T(8,128)(2,1)}, u32[]{:S(2)}) copy-start(bf16[128,2048]{1,0:T(8,128)(2,1)} %param.11) | copy-start | bytes 1572868
  0.7 67.7 %copy-start.3 = (bf16[128,2048]{1,0:T(8,128)(2,1)S(1)}, bf16[128,2048]{1,0:T(8,128)(2,1)}, u32[]{:S(2)}) copy-start(bf16[128,2048]{1,0:T(8,128)(2,1)} %param.9) | copy-start | bytes 1572868
  0.7 67.7 %copy-start.1 = (f32[128,2048]{1,0:T(8,128)S(1)}, f32[128,2048]{1,0:T(8,128)}, u32[]{:S(2)}) copy-start(f32[128,2048]{1,0:T(8,128)} %param.8) | copy-start | bytes 3145732
  71.2 102.7 %all-to-all-start = ((bf16[128,96,128]{2,1,0:T(8,128)(2,1)}), bf16[128,96,128]{2,1,0:T(8,128)(2,1)S(1)}, u32[]{:S(2)}, u32[]{:S(2)}) async-start(bf16[128,96,128]{2,1,0:T(8,128)(2,1)} %bitcast.12), calls=%async_computation | async-start | bytes 6291456 | tf_op jit(solution)/shard_map/all_to_all | solution.py:322
  82.7 65.8 %collective-permute-start.1 = (bf16[3,2048,128]{2,1,0:T(8,128)(2,1)}, bf16[3,2048,128]{2,1,0:T(8,128)(2,1)}, u32[]{:S(2)}, u32[]{:S(2)}) collective-permute-start(bf16[3,2048,128]{2,1,0:T(8,128)(2,1)} %get-tuple-element.32), channel_id=1, source_target_pairs={{0,1},{1,0},{2,3},{3,2},{4,5},{5,4},{6,7},{7,6},{8,9},{9,8},{10,11... | collective-permute-start | bytes 4718600 | tf_op jit(solution)/shard_map/ppermute | solution.py:150
  148.6 1.2 copy-start
  153.5 9.3 %collective-permute-start.2 = (bf16[1024,128]{1,0:T(8,128)(2,1)}, bf16[1024,128]{1,0:T(8,128)(2,1)S(1)}, u32[]{:S(2)}, u32[]{:S(2)}) collective-permute-start(bf16[1024,128]{1,0:T(8,128)(2,1)} %get-tuple-element.34), channel_id=1, source_target_pairs={{0,2},{1,3},{2,4},{3,5},{4,6},{5,7},{6,0},{7,1},{8,10},{9,11},{10,... | collective-permute-start | bytes 786440 | tf_op jit(solution)/shard_map/ppermute | solution.py:150
  154.2 8.6 %collective-permute-start.3 = (bf16[1024,128]{1,0:T(8,128)(2,1)}, bf16[1024,128]{1,0:T(8,128)(2,1)}, u32[]{:S(2)}, u32[]{:S(2)}) collective-permute-start(bf16[1024,128]{1,0:T(8,128)(2,1)} %get-tuple-element.35), channel_id=1, source_target_pairs={{0,6},{1,7},{2,0},{3,1},{4,2},{5,3},{6,4},{7,5},{8,14},{9,15},{10,... | collective-permute-start | bytes 786440 | tf_op jit(solution)/shard_map/ppermute | solution.py:150
  156.2 12.3 %collective-permute-start = (bf16[2048,128]{1,0:T(8,128)(2,1)}, bf16[2048,128]{1,0:T(8,128)(2,1)}, u32[]{:S(2)}, u32[]{:S(2)}) collective-permute-start(bf16[2048,128]{1,0:T(8,128)(2,1)} %get-tuple-element.30), channel_id=1, source_target_pairs={{0,1},{1,0},{2,3},{3,2},{4,5},{5,4},{6,7},{7,6},{8,9},{9,8},{10,11... | collective-permute-start | bytes 1572872 | tf_op jit(solution)/shard_map/ppermute | solution.py:150
  156.9 11.6 %collective-permute-start.5 = (bf16[1024,128]{1,0:T(8,128)(2,1)}, bf16[1024,128]{1,0:T(8,128)(2,1)S(1)}, u32[]{:S(2)}, u32[]{:S(2)}) collective-permute-start(bf16[1024,128]{1,0:T(8,128)(2,1)} %copy-done.14), channel_id=1, source_target_pairs={{0,2},{1,3},{2,4},{3,5},{4,6},{5,7},{6,0},{7,1},{8,10},{9,11},{10,... | collective-permute-start | bytes 786440 | tf_op jit(solution)/shard_map/ppermute | solution.py:150
  156.9 12.3 %collective-permute-start.6 = (bf16[1024,128]{1,0:T(8,128)(2,1)}, bf16[1024,128]{1,0:T(8,128)(2,1)S(1)}, u32[]{:S(2)}, u32[]{:S(2)}) collective-permute-start(bf16[1024,128]{1,0:T(8,128)(2,1)} %copy-done.13), channel_id=1, source_target_pairs={{0,6},{1,7},{2,0},{3,1},{4,2},{5,3},{6,4},{7,5},{8,14},{9,15},{10,... | collective-permute-start | bytes 786440 | tf_op jit(solution)/shard_map/ppermute | solution.py:150
  162.8 1.0 copy-start.5
  165.5 7.7 %collective-permute-start.4 = (bf16[1024,128]{1,0:T(8,128)(2,1)S(1)}, bf16[1024,128]{1,0:T(8,128)(2,1)S(1)}, u32[]{:S(2)}, u32[]{:S(2)}) collective-permute-start(bf16[1024,128]{1,0:T(8,128)(2,1)S(1)} %get-tuple-element.36), channel_id=1, source_target_pairs={{0,2},{1,3},{2,4},{3,5},{4,6},{5,7},{6,0},{7,1},{8,10},{9,11},{10,... | collective-permute-start | bytes 786440 | tf_op jit(solution)/shard_map/ppermute | solution.py:150
  165.9 7.3 %collective-permute-start.7 = (bf16[1024,128]{1,0:T(8,128)(2,1)S(1)}, bf16[1024,128]{1,0:T(8,128)(2,1)S(1)}, u32[]{:S(2)}, u32[]{:S(2)}) collective-permute-start(bf16[1024,128]{1,0:T(8,128)(2,1)S(1)} %get-tuple-element.39), channel_id=1, source_target_pairs={{0,6},{1,7},{2,0},{3,1},{4,2},{5,3},{6,4},{7,5},{8,14},{9,15},{10,... | collective-permute-start | bytes 786440 | tf_op jit(solution)/shard_map/ppermute | solution.py:150
  173.9 1.0 copy-start.6
  174.9 0.9 copy-start.8
  181.8 2.3 copy-start.2
  181.8 11.1 %collective-permute-start.10 = (bf16[2048,128]{1,0:T(8,128)(2,1)S(1)}, bf16[2048,128]{1,0:T(8,128)(2,1)S(1)}, u32[]{:S(2)}, u32[]{:S(2)}) collective-permute-start(bf16[2048,128]{1,0:T(8,128)(2,1)S(1)} %get-tuple-element.40.refs_0_), channel_id=1, source_target_pairs={{0,6},{1,7},{2,0},{3,1},{4,2},{5,3},{6,4},{7,5},{8,14},{9,15},{10,... | collective-permute-start | bytes 1572872 | tf_op jit(solution)/shard_map/ppermute | solution.py:150
  184.2 15.9 %collective-permute-start.8 = (bf16[2048,128]{1,0:T(8,128)(2,1)S(1)}, bf16[2048,128]{1,0:T(8,128)(2,1)S(1)}, u32[]{:S(2)}, u32[]{:S(2)}) collective-permute-start(bf16[2048,128]{1,0:T(8,128)(2,1)S(1)} %get-tuple-element.40.refs_0_), channel_id=1, source_target_pairs={{0,2},{1,3},{2,4},{3,5},{4,6},{5,7},{6,0},{7,1},{8,10},{9,11},{10,... | collective-permute-start | bytes 1572872 | tf_op jit(solution)/shard_map/ppermute | solution.py:150
  184.2 26.0 %collective-permute-start.14 = (bf16[2048,128]{1,0:T(8,128)(2,1)S(1)}, bf16[2048,128]{1,0:T(8,128)(2,1)S(1)}, u32[]{:S(2)}, u32[]{:S(2)}) collective-permute-start(bf16[2048,128]{1,0:T(8,128)(2,1)S(1)} %get-tuple-element.40.refs_0_), channel_id=1, source_target_pairs={{0,1},{1,0},{2,3},{3,2},{4,5},{5,4},{6,7},{7,6},{8,9},{9,8},{10,11... | collective-permute-start | bytes 1572872 | tf_op jit(solution)/shard_map/ppermute | solution.py:150
  192.9 17.3 %copy-start.15 = (bf16[2048,128]{1,0:T(8,128)(2,1)}, bf16[2048,128]{1,0:T(8,128)(2,1)S(1)}, u32[]{:S(2)}) copy-start(bf16[2048,128]{1,0:T(8,128)(2,1)S(1)} %collective-permute-done.10.refs_3_) | copy-start | bytes 1572868
  193.0 7.3 %collective-permute-start.11 = (bf16[1024,128]{1,0:T(8,128)(2,1)S(1)}, bf16[1024,128]{1,0:T(8,128)(2,1)S(1)}, u32[]{:S(2)}, u32[]{:S(2)}) collective-permute-start(bf16[1024,128]{1,0:T(8,128)(2,1)S(1)} %slice.9), channel_id=1, source_target_pairs={{0,6},{1,7},{2,0},{3,1},{4,2},{5,3},{6,4},{7,5},{8,14},{9,15},{10,... | collective-permute-start | bytes 786440 | tf_op jit(solution)/shard_map/ppermute | solution.py:150
  196.2 14.0 %collective-permute-start.16 = (bf16[2048,128]{1,0:T(8,128)(2,1)S(1)}, bf16[2048,128]{1,0:T(8,128)(2,1)S(1)}, u32[]{:S(2)}, u32[]{:S(2)}) collective-permute-start(bf16[2048,128]{1,0:T(8,128)(2,1)S(1)} %collective-permute-done.10.refs_3_), channel_id=1, source_target_pairs={{0,1},{1,0},{2,3},{3,2},{4,5},{5,4},{6,7},{7,6},{8,9},{9,8},{10,11... | collective-permute-start | bytes 1572872 | tf_op jit(solution)/shard_map/ppermute | solution.py:150
  200.1 10.2 %copy-start.16 = (bf16[2048,128]{1,0:T(8,128)(2,1)}, bf16[2048,128]{1,0:T(8,128)(2,1)S(1)}, u32[]{:S(2)}) copy-start(bf16[2048,128]{1,0:T(8,128)(2,1)S(1)} %collective-permute-done.8.refs_2_) | copy-start | bytes 1572868
  200.1 10.1 %collective-permute-start.15 = (bf16[2048,128]{1,0:T(8,128)(2,1)S(1)}, bf16[2048,128]{1,0:T(8,128)(2,1)S(1)}, u32[]{:S(2)}, u32[]{:S(2)}) collective-permute-start(bf16[2048,128]{1,0:T(8,128)(2,1)S(1)} %collective-permute-done.8.refs_2_), channel_id=1, source_target_pairs={{0,1},{1,0},{2,3},{3,2},{4,5},{5,4},{6,7},{7,6},{8,9},{9,8},{10,11... | collective-permute-start | bytes 1572872 | tf_op jit(solution)/shard_map/ppermute | solution.py:150
  200.2 8.7 %collective-permute-start.9 = (bf16[1024,128]{1,0:T(8,128)(2,1)S(1)}, bf16[1024,128]{1,0:T(8,128)(2,1)S(1)}, u32[]{:S(2)}, u32[]{:S(2)}) collective-permute-start(bf16[1024,128]{1,0:T(8,128)(2,1)S(1)} %slice.8), channel_id=1, source_target_pairs={{0,2},{1,3},{2,4},{3,5},{4,6},{5,7},{6,0},{7,1},{8,10},{9,11},{10,... | collective-permute-start | bytes 786440 | tf_op jit(solution)/shard_map/ppermute | solution.py:150
  200.3 108.2 %copy-start.20 = (bf16[1024,128]{1,0:T(8,128)(2,1)}, bf16[1024,128]{1,0:T(8,128)(2,1)S(1)}, u32[]{:S(2)}) copy-start(bf16[1024,128]{1,0:T(8,128)(2,1)S(1)} %collective-permute-done.11.refs_1_) | copy-start | bytes 786436
  200.3 108.1 %collective-permute-start.13 = (bf16[1024,128]{1,0:T(8,128)(2,1)S(1)}, bf16[1024,128]{1,0:T(8,128)(2,1)S(1)}, u32[]{:S(2)}, u32[]{:S(2)}) collective-permute-start(bf16[1024,128]{1,0:T(8,128)(2,1)S(1)} %collective-permute-done.11.refs_1_), channel_id=1, source_target_pairs={{0,1},{1,0},{2,3},{3,2},{4,5},{5,4},{6,7},{7,6},{8,9},{9,8},{10,11... | collective-permute-start | bytes 786440 | tf_op jit(solution)/shard_map/ppermute | solution.py:150
  208.9 99.5 %copy-start.21 = (bf16[1024,128]{1,0:T(8,128)(2,1)}, bf16[1024,128]{1,0:T(8,128)(2,1)S(1)}, u32[]{:S(2)}) copy-start(bf16[1024,128]{1,0:T(8,128)(2,1)S(1)} %collective-permute-done.9.refs_0_) | copy-start | bytes 786436
  208.9 99.5 %collective-permute-start.12 = (bf16[1024,128]{1,0:T(8,128)(2,1)S(1)}, bf16[1024,128]{1,0:T(8,128)(2,1)}, u32[]{:S(2)}, u32[]{:S(2)}) collective-permute-start(bf16[1024,128]{1,0:T(8,128)(2,1)S(1)} %collective-permute-done.9.refs_0_), channel_id=1, source_target_pairs={{0,1},{1,0},{2,3},{3,2},{4,5},{5,4},{6,7},{7,6},{8,9},{9,8},{10,11... | collective-permute-start | bytes 786440 | tf_op jit(solution)/shard_map/ppermute | solution.py:150
  210.2 1.0 copy-start.18
  (10 other events, 7.8 us)

commit v3 on v1

v3 whole, which is shorter than its diff:
```python
import functools

import jax
import jax.numpy as jnp
from jax import lax
from jax.experimental import pallas as pl
from jax.experimental.pallas import tpu as pltpu
from jax.sharding import PartitionSpec as P

ALL = ("fsdp", "dp")
LANES = 128
SUB = 8
RING = 4
CORES = 2
ADDENDS = 3


def to_tiles(values):
    rows, cols = values.shape
    tiled = values.reshape(rows // SUB, SUB, cols // LANES, LANES)
    return tiled.transpose(0, 2, 1, 3).reshape(rows * cols // LANES, LANES)


def from_tiles(values, rows, cols):
    tiled = values.reshape(rows // SUB, cols // LANES, SUB, LANES)
    return tiled.transpose(0, 2, 1, 3).reshape(rows, cols)


def pair_rank(owners, keyed):
    matching = owners[:, None] == owners[None, :]
    before = keyed[None, :] < keyed[:, None]
    return jnp.sum(jnp.where(matching & before, 1, 0), axis=1).astype(jnp.int32)


def send_slots(block_map, rows):
    owners = block_map.shape[0]
    first_slot = (lax.axis_index("fsdp") * lax.axis_size("dp") + lax.axis_index("dp")) * rows
    held = block_map - first_slot
    here = (held >= 0) & (held < rows)
    spot = lax.broadcasted_iota(jnp.int32, block_map.shape, 1)
    first = jnp.min(jnp.where(here, spot, rows), axis=1, keepdims=True)
    one = jnp.max(jnp.where(here & (spot == first), held, -1), axis=1, keepdims=True)
    two = jnp.max(jnp.where(here & (spot > first), held, -1), axis=1, keepdims=True)
    owner = lax.broadcasted_iota(jnp.int32, (owners, rows), 0)
    slot = lax.broadcasted_iota(jnp.int32, (owners, rows), 1)
    place_of = jnp.where(one == slot, 2 * owner, 0) + jnp.where(two == slot, 2 * owner + 1, 0)
    return jnp.sum(place_of, axis=0, keepdims=True)


def pack_kernel(rows, chunks, map_ref, mscale_ref, sscale_ref, master_ref, mean_ref, square_ref, out_ref, *scratch):
    held_map, master, mean, square, wide_mean, wide_square, slots, mscale, sscale, slot_of, mscale_of, sscale_of = scratch[:12]
    load_sems, table_sems = scratch[12:]
    pairs = [(map_ref, held_map), (mean_ref, mean), (square_ref, square), (master_ref, master)]
    loads = [pltpu.make_async_copy(ref, room, load_sems.at[k]) for k, (ref, room) in enumerate(pairs)]
    for load in loads:
        load.start()
    mscale[...] = mscale_ref[...].astype(jnp.float32)
    sscale[...] = sscale_ref[...].astype(jnp.float32)
    loads[0].wait()
    slots[...] = send_slots(held_map[...], rows)
    tables = [(slots, slot_of), (mscale, mscale_of), (sscale, sscale_of)]
    tables = [pltpu.make_async_copy(table, room, table_sems.at[k]) for k, (table, room) in enumerate(tables)]
    for table in tables:
        table.start()
    loads[1].wait()
    wide_mean[...] = mean[...].astype(jnp.float32)
    loads[2].wait()
    wide_square[...] = square[...].astype(jnp.float32)
    for table in tables:
        table.wait()
    loads[3].wait()
    for row in range(rows):
        base = (row // SUB) * chunks * SUB + row % SUB
        spots = pl.ds(base, chunks, stride=SUB)
        slot = slot_of[0, row]
        out_ref[slot, pl.ds(0, chunks), :] = master[spots, :].astype(jnp.bfloat16)
        out_ref[slot, pl.ds(chunks, chunks), :] = (wide_mean[spots, :] * mscale_of[0, row]).astype(jnp.bfloat16)
        out_ref[slot, pl.ds(2 * chunks, chunks), :] = (wide_square[spots, :] * sscale_of[0, row]).astype(jnp.bfloat16)


def pack(old_map, mean_scale, square_scale, master, mean, square, slot_total):
    rows, cols = master.shape
    chunks = cols // LANES
    hbm = pl.BlockSpec(memory_space=pl.ANY)
    vmem = pl.BlockSpec(memory_space=pltpu.VMEM)
    flat = (rows * chunks, LANES)
    f32, i32 = jnp.float32, jnp.int32
    block_map = old_map.reshape(-1, rows)
    return pl.pallas_call(
        functools.partial(pack_kernel, rows, chunks),
        out_shape=jax.ShapeDtypeStruct((slot_total, 3 * chunks, LANES), jnp.bfloat16),
        in_specs=[hbm, vmem, vmem, hbm, hbm, hbm],
        out_specs=vmem,
        scratch_shapes=[
            pltpu.VMEM(block_map.shape, i32),
            pltpu.VMEM(flat, f32),
            pltpu.VMEM(flat, mean.dtype),
            pltpu.VMEM(flat, square.dtype),
            pltpu.VMEM(flat, f32),
            pltpu.VMEM(flat, f32),
            pltpu.VMEM((1, rows), i32),
            pltpu.VMEM((1, rows), f32),
            pltpu.VMEM((1, rows), f32),
            pltpu.SMEM((1, rows), i32),
            pltpu.SMEM((1, rows), f32),
            pltpu.SMEM((1, rows), f32),
            pltpu.SemaphoreType.DMA((4,)),
            pltpu.SemaphoreType.DMA((3,)),
        ],
        compiler_params=pltpu.CompilerParams(vmem_limit_bytes=56 * 1024 * 1024),
        name="pack",
    )(
        block_map,
        mean_scale.reshape(1, rows),
        square_scale.reshape(1, rows),
        to_tiles(master),
        to_tiles(mean),
        to_tiles(square),
    )


def unpack_kernel(rows, chunks, slot_ref, in_ref, out_ref, weight_old, mean_old, square_old):
    span = chunks * SUB
    stages = (weight_old, mean_old, square_old)
    for group in range(rows // SUB):
        buf = group % 2
        for r in range(SUB):
            slot = slot_ref[group * SUB + r]
            spots = pl.ds(buf * span + r, chunks, stride=SUB)
            for k, stage in enumerate(stages):
                stage[spots, :] = in_ref[slot, pl.ds(k * chunks, chunks), :].astype(jnp.float32)
        for k, stage in enumerate(stages):
            out_ref[k, pl.ds(group * span, span), :] = stage[pl.ds(buf * span, span), :].astype(out_ref.dtype)


def unpack(slots, arrived, rows, chunks):
    stage = pltpu.VMEM((2 * chunks * SUB, LANES), jnp.float32)
    vmem = pl.BlockSpec(memory_space=pltpu.VMEM)
    return pl.pallas_call(
        functools.partial(unpack_kernel, rows, chunks),
        out_shape=jax.ShapeDtypeStruct((3, rows * chunks, LANES), arrived.dtype),
        in_specs=[pl.BlockSpec(memory_space=pltpu.SMEM), vmem],
        out_specs=vmem,
        scratch_shapes=[stage, stage, stage],
        compiler_params=pltpu.CompilerParams(vmem_limit_bytes=24 * 1024 * 1024),
        name="unpack",
    )(slots, arrived)


def adam_kernel(rows, chunks, old_ref, mine_ref, *refs):
    side_refs, refs = refs[:4], refs[4:]
    weights_ref, master_ref, mcode_ref, scode_ref, mscale_ref, sscale_ref = refs[:6]
    old, addends, sems = refs[6:]
    span = chunks * SUB
    groups = rows // SUB
    half = groups // 2 * span
    loads = []
    for h in range(2):
        part = pl.ds(h * half, half)
        pairs = [(mine_ref.at[part], addends.at[0, part])]
        pairs += [(side_refs[2 * k + h], addends.at[1 + k, part]) for k in range(2)]
        pairs += [(old_ref.at[k, part], old.at[k, part]) for k in range(3)]
        loads.append([pltpu.make_async_copy(ref, room, sems.at[h, k]) for k, (ref, room) in enumerate(pairs)])
    for load in loads[0] + loads[1]:
        load.start()
    lane = lax.broadcasted_iota(jnp.int32, (SUB, LANES), 1)
    sub = lax.broadcasted_iota(jnp.int32, (SUB, LANES), 0)
    mline = jnp.zeros((SUB, LANES), jnp.float32)
    sline = jnp.zeros((SUB, LANES), jnp.float32)
    for group in range(groups):
        if group % (groups // 2) == 0:
            for load in loads[group * 2 // groups]:
                load.wait()
        there = pl.ds(group * span, span)
        gradient = addends[0, there, :].astype(jnp.float32)
        for k in range(1, ADDENDS):
            gradient += addends[k, there, :].astype(jnp.float32)
        weight_old, mean_old, square_old = (old[k, there, :].astype(jnp.float32) for k in range(3))
        mean_next = 0.9 * mean_old + 0.1 * gradient
        square_next = 0.95 * square_old + 0.05 * gradient * gradient
        master = weight_old - 0.05 * (mean_next / (jnp.sqrt(square_next) + 1e-08) + 0.1 * weight_old)
        master_ref[there, :] = master
        weights_ref[there, :] = master.astype(jnp.bfloat16)
        mean_next = mean_next.reshape(chunks, SUB, LANES)
        square_next = square_next.reshape(chunks, SUB, LANES)
        mpeak = jnp.max(jnp.max(jnp.abs(mean_next), axis=0), axis=1, keepdims=True)
        speak = jnp.max(jnp.max(square_next, axis=0), axis=1, keepdims=True)
        mscale = (mpeak + 1e-06).astype(jnp.bfloat16).astype(jnp.float32)
        sscale = (speak + 1e-06).astype(jnp.bfloat16).astype(jnp.float32)
        mcode_ref[there, :] = (mean_next * (1.0 / mscale)[None]).reshape(span, LANES).astype(jnp.bfloat16)
        scode_ref[there, :] = (square_next * (1.0 / sscale)[None]).reshape(span, LANES).astype(jnp.bfloat16)
        mine = lane == sub + group * SUB
        mline = jnp.where(mine, mscale, mline)
        sline = jnp.where(mine, sscale, sline)
    mscale_ref[...] = jnp.sum(mline, axis=0, keepdims=True).astype(jnp.bfloat16)
    sscale_ref[...] = jnp.sum(sline, axis=0, keepdims=True).astype(jnp.bfloat16)


def adam(old, addends, rows, chunks):
    flat = (rows * chunks, LANES)
    bf16, f32 = jnp.bfloat16, jnp.float32
    vmem = pl.BlockSpec(memory_space=pltpu.VMEM)
    return pl.pallas_call(
        functools.partial(adam_kernel, rows, chunks),
        out_shape=[
            jax.ShapeDtypeStruct(flat, bf16),
            jax.ShapeDtypeStruct(flat, f32),
            jax.ShapeDtypeStruct(flat, bf16),
            jax.ShapeDtypeStruct(flat, bf16),
            jax.ShapeDtypeStruct((1, rows), bf16),
            jax.ShapeDtypeStruct((1, rows), bf16),
        ],
        in_specs=[pl.BlockSpec(memory_space=pl.ANY)] * 6,
        out_specs=[vmem] * 6,
        scratch_shapes=[
            pltpu.VMEM((3, *flat), bf16),
            pltpu.VMEM((ADDENDS, *flat), bf16),
            pltpu.SemaphoreType.DMA((2, 3 + ADDENDS)),
        ],
        compiler_params=pltpu.CompilerParams(vmem_limit_bytes=56 * 1024 * 1024),
        name="adam",
    )(old, *addends)


def place():
    me = lax.axis_index("dp")
    return me // CORES, me % CORES


def shard_at(y, step, core):
    return lax.rem(y + step, RING) * CORES + core


def sends(shift, flip):
    return [
        (y * CORES + c, (y + shift) % RING * CORES + (CORES - 1 - c if flip else c))
        for y in range(RING)
        for c in range(CORES)
    ]


def send(values, shift, flip=False):
    return lax.ppermute(values, "dp", sends(shift, flip))


def cut_kernel(shards, grad_ref, *refs):
    out_refs, (room, in_sems, out_sems) = refs[: len(shards)], refs[len(shards) :]
    y, core = place()
    loads, stores = [], []
    for k, (step, flip) in enumerate(shards):
        shard = shard_at(y, step, CORES - 1 - core if flip else core)
        loads.append(pltpu.make_async_copy(grad_ref.at[shard], room.at[k], in_sems.at[k]))
        stores.append(pltpu.make_async_copy(room.at[k], out_refs[k], out_sems.at[k]))
    for load in loads:
        load.start()
    for load, store in zip(loads, stores):
        load.wait()
        store.start()
    for store in stores:
        store.wait()


def cut(grads, shards):
    _, span, lanes = grads.shape
    count = len(shards)
    hbm = pl.BlockSpec(memory_space=pl.ANY)
    return pl.pallas_call(
        functools.partial(cut_kernel, shards),
        out_shape=[jax.ShapeDtypeStruct((span, lanes), grads.dtype)] * count,
        in_specs=[hbm],
        out_specs=[hbm] * count,
        scratch_shapes=[pltpu.VMEM((count, span, lanes), grads.dtype)] + [pltpu.SemaphoreType.DMA((count,))] * 2,
        compiler_params=pltpu.CompilerParams(vmem_limit_bytes=56 * 1024 * 1024),
        name="cut",
    )(grads)


def add_kernel(windows, sums, *refs):
    count, outs = len(windows), len(sums)
    in_refs, out_refs, rooms, totals = refs[:count], refs[count:][:outs], refs[count + outs :][:count], refs[2 * count + outs : -2]
    in_sems, out_sems = refs[-2:]
    loads = [
        pltpu.make_async_copy(ref.at[pl.ds(*window)], room, in_sems.at[k])
        for k, (ref, window, room) in enumerate(zip(in_refs, windows, rooms))
    ]
    for load in loads:
        load.start()
    stores = []
    for k, terms in enumerate(sums):
        total = None
        for term in terms:
            loads[term].wait()
            values = rooms[term][...].astype(jnp.float32)
            total = values if total is None else total + values
        totals[k][...] = total.astype(totals[k].dtype)
        store = pltpu.make_async_copy(totals[k], out_refs[k], out_sems.at[k])
        store.start()
        stores.append(store)
    for store in stores:
        store.wait()


def add(*sums):
    terms = [term for parts in sums for term in parts]
    lanes, dtype = terms[0][0].shape[1], terms[0][0].dtype
    hbm = pl.BlockSpec(memory_space=pl.ANY)
    order, at = [], 0
    for parts in sums:
        order.append(tuple(range(at, at + len(parts))))
        at += len(parts)
    windows = [(first, rows) for _, first, rows in terms]
    shapes = [(rows, lanes) for _, rows in windows]
    outs = [(parts[0][2], lanes) for parts in sums]
    return pl.pallas_call(
        functools.partial(add_kernel, windows, order),
        out_shape=[jax.ShapeDtypeStruct(shape, dtype) for shape in outs],
        in_specs=[hbm] * len(terms),
        out_specs=[hbm] * len(outs),
        scratch_shapes=[pltpu.VMEM(shape, dtype) for shape in shapes + outs]
        + [pltpu.SemaphoreType.DMA((len(terms),)), pltpu.SemaphoreType.DMA((len(outs),))],
        compiler_params=pltpu.CompilerParams(vmem_limit_bytes=56 * 1024 * 1024),
        name="add",
    )(*[array for array, _, _ in terms])


def reduce_shards(grads, arrived):
    span = grads.shape[1]
    half = span // 2
    steps = (2, 1, 3, 0)
    got = dict(zip(steps, [send(part, 0, True) for part in cut(grads, tuple((step, 1) for step in steps))]))
    own = dict(zip(steps, cut(grads, tuple((step, 0) for step in steps))))

    def both(step, first, rows):
        return [(own[step], first, rows), (got[step], first, rows)]

    opp_lo, opp_hi, up_hi, dn_lo, mine = add(
        both(2, 0, half), both(2, half, half), both(1, half, half), both(3, 0, half), both(0, 0, span)
    )
    opp_up, opp_dn = send(opp_lo, 1), send(opp_hi, 3)
    up_hi_got, dn_lo_got = send(up_hi, 1), send(dn_lo, 3)
    opp_up, opp_dn, arrived = lax.optimization_barrier((opp_up, opp_dn, arrived))
    up_lo, dn_hi = add(both(1, 0, half) + [(opp_up, 0, half)], both(3, half, half) + [(opp_dn, 0, half)])
    return (mine, send(up_lo, 1), up_hi_got, dn_lo_got, send(dn_hi, 3)), arrived


def join_kernel(span, starts, *refs):
    parts, (out_ref, *rooms, in_sems, sems) = refs[: len(starts)], refs[-3 - len(starts) :]
    y, core = place()
    loads = [pltpu.make_async_copy(part, room, in_sems.at[k]) for k, (part, room) in enumerate(zip(parts, rooms))]
    for load in loads:
        load.start()
    copies = []
    for k, (step, flip, offset) in enumerate(starts):
        side = CORES - 1 - core if flip else core
        base = pl.multiple_of(shard_at(y, step, side) * span + offset, span // 2)
        copies.append(pltpu.make_async_copy(rooms[k], out_ref.at[pl.ds(base, parts[k].shape[0])], sems.at[k]))
    for load, copy in zip(loads, copies):
        load.wait()
        copy.start()
    for copy in copies:
        copy.wait()


def join(span, starts, parts, whole=None):
    lanes = parts[0].shape[1]
    hbm = pl.BlockSpec(memory_space=pl.ANY)
    given = list(parts) + ([] if whole is None else [whole])
    return pl.pallas_call(
        functools.partial(join_kernel, span, starts),
        out_shape=jax.ShapeDtypeStruct((RING * CORES * span, lanes), parts[0].dtype),
        in_specs=[hbm] * len(given),
        out_specs=hbm,
        scratch_shapes=[pltpu.VMEM(part.shape, part.dtype) for part in parts]
        + [pltpu.SemaphoreType.DMA((len(parts),))] * 2,
        compiler_params=pltpu.CompilerParams(vmem_limit_bytes=16 * 1024 * 1024),
        input_output_aliases={} if whole is None else {len(parts): 0},
        name="join",
    )(*given)


def gather_shards(mine):
    span = mine.shape[0]
    half = span // 2
    up, dn, sib = send(mine, 1), send(mine, 3), send(mine, 0, True)
    opp_lo, opp_hi = send(up[:half], 1), send(dn[half:], 3)
    up_sib, dn_sib = send(up, 0, True), send(dn, 0, True)
    starts = [(0, 0, 0), (0, 1, 0), (3, 0, 0), (1, 0, 0), (3, 1, 0), (1, 1, 0)]
    most = join(span, starts, [mine, sib, up, dn, up_sib, dn_sib])
    most, opp_lo, opp_hi = lax.optimization_barrier((most, opp_lo, opp_hi))
    starts = [(2, 0, 0), (2, 0, half), (2, 1, 0), (2, 1, half)]
    return join(span, starts, [opp_lo, opp_hi, send(opp_lo, 0, True), send(opp_hi, 0, True)], most)


def arrivals(old_map, block_rows, peer_cap):
    self_index = lax.axis_index(ALL)
    wanted = lax.dynamic_slice_in_dim(old_map, self_index * block_rows, block_rows)
    source = wanted // block_rows
    return source * peer_cap + pair_rank(source, jnp.arange(block_rows, dtype=jnp.int32))


def local(grad_parts, old_master, old_mean, old_mean_scale, old_square, old_square_scale, old_map):
    count_all = lax.axis_size(ALL)
    block_rows, block_len = old_master.shape
    peer_cap = 2
    slot_total = count_all * peer_cap
    chunks = block_len // LANES
    grads = to_tiles(grad_parts[0]).reshape(RING * CORES, block_rows * chunks, LANES)
    packed = pack(old_map, old_mean_scale, old_square_scale, old_master, old_mean, old_square, slot_total)
    packed, late_grads, late_map = lax.optimization_barrier((packed, grads, old_map))
    arrived = lax.all_to_all(
        packed.reshape(count_all, peer_cap * 3 * chunks, LANES), ALL, split_axis=0, concat_axis=0, tiled=True
    ).reshape(slot_total, 3 * chunks, LANES)
    addends, arrived = reduce_shards(late_grads, arrived)
    old = unpack(arrivals(late_map, block_rows, peer_cap), arrived, block_rows, chunks)
    mine, *blocks, mean_scales, square_scales = adam(old, addends, block_rows, chunks)
    master, mean_codes, square_codes = (from_tiles(x, block_rows, block_len) for x in blocks)
    weights = from_tiles(gather_shards(mine), RING * CORES * block_rows, block_len)
    return (weights, master, mean_codes, mean_scales.reshape(-1), square_codes, square_scales.reshape(-1))


def solution(mesh):
    in_specs = (
        P("dp", "fsdp", None),
        P(ALL, None),
        P(ALL, None),
        P(ALL),
        P(ALL, None),
        P(ALL),
        P(),
    )
    out_specs = (
        P("fsdp", None),
        P(ALL, None),
        P(ALL, None),
        P(ALL),
        P(ALL, None),
        P(ALL),
    )
    return jax.shard_map(local, mesh=mesh, in_specs=in_specs, out_specs=out_specs, check_vma=False)
```

time: 133 us -> 106 us (0.80)
  waiting for transfers between devices: 92.8 us -> 40 us
  starting transfers between devices: 11.6 us -> 36.6 us
  Pallas kernels: 6.03 us -> 23.1 us
  between operations: 14.2 us -> 0.82 us
  local copies, waits for them, and re-layouts: 6.65 us -> 3.82 us
    all_to_all x1, waiting for transfers between devices: 41.3 us -> 0.01 us  [local(): lax.all_to_all(packed.reshape(count_all, peer_cap * 3 * chunks, LANES), A...]
    ppermute x0 -> x19, waiting for transfers between devices: none -> 40 us  [send(): return lax.ppermute(values, 'dp', sends(shift, flip))]
    all_gather x1 -> x0, waiting for transfers between devices: 34.6 us -> none  [local(): weights = lax.all_gather(mine, 'dp', axis=0, tiled=True)]
    ppermute x0 -> x19, starting transfers between devices: none -> 25.1 us  [send(): return lax.ppermute(values, 'dp', sends(shift, flip))]
    reduce_scatter x1 -> x0, waiting for transfers between devices: 16.2 us -> none  [local(): lax.psum_scatter(grad_parts[0], 'dp', scatter_dimension=0, tiled=True)]
    pallas_call x0 -> x7, Pallas kernels: none -> 14.3 us  [the longest x2 5.03 us: add(): pl.pallas_call(functools.partial(add_kernel, windows, order), out_shape=[...]
    unnamed x17 -> x18, local copies, waits for them, and re-layouts: 6.65 us -> 3.78 us
    pallas_call x1, Pallas kernels: 2.84 us -> 4.65 us  [pack(): pl.pallas_call(functools.partial(pack_kernel, rows, chunks), out_shape=ja...]
  transfers between devices with their start and end apart: 3 -> 20, of which waited for: 3 -> 9; matrix products, arithmetic and copies ran while one was open for 1% -> 2% of each run, Pallas kernels for 2% -> 12%
where the time goes in v3:
time: 106 us
  waiting for transfers between devices  40 us (38%)
  starting transfers between devices  36.6 us (35%)
  Pallas kernels  23.1 us (22%)
  local copies, waits for them, and re-layouts  3.82 us (4%)
  other arithmetic  1.71 us (2%)
    ppermute x19, waiting for transfers between devices, send(): return lax.ppermute(values, 'dp', sends(shift, flip))  40 us
    ppermute x19, starting transfers between devices, send(): return lax.ppermute(values, 'dp', sends(shift, flip))  25.1 us
    all_to_all x1, starting transfers between devices, local(): lax.all_to_all(packed.reshape(count_all, peer_cap * 3 * chunks, LANES), A...  11.5 us
    pallas_call x2, Pallas kernels, add(): pl.pallas_call(functools.partial(add_kernel, windows, order), out_shape=[...  5.03 us
    pallas_call x2, Pallas kernels, cut(): pl.pallas_call(functools.partial(cut_kernel, shards), out_shape=[jax.Shap...  4.89 us
    pallas_call x1, Pallas kernels, pack(): pl.pallas_call(functools.partial(pack_kernel, rows, chunks), out_shape=ja...  4.65 us
    pallas_call x1, Pallas kernels, adam(): pl.pallas_call(functools.partial(adam_kernel, rows, chunks), out_shape=[j...  4.1 us
    unnamed x18, local copies, waits for them, and re-layouts  3.78 us
  transfers between devices with their start and end apart: 20, of which 9 were waited for; matrix products, arithmetic and copies ran while one was open for 2% of the time, Pallas kernels for 12%

profile of v3, /device:TPU:1, one launch (start us, length us, event | category | flops | bytes accessed | tf_op | source)
XLA Modules:
  0.0 106.0 jit_solution(12875751331843326081)
XLA Ops:
  0.6 4.7 %pack.1 = bf16[256,48,128]{2,1,0:T(8,128)(2,1)} custom-call(s32[128,128]{1,0:T(8,128)} %bitcast.55, bf16[1,128]{1,0:T(2,128)(2,1)} %bitcast.56, bf16[1,128]{1,0:T(2,128)(2,1)} %bitcast.57, f32[2048,128]{1,0:T(8,128)} %bitcast.52, bf16[2048,128]{1,0:T(8,128)(2,1)} %bitcast.53, bf16[2048,128]{1,0:T(8,128)(2,1)} %bitcast.54), custom_call_target="tpu_custom_call" | custom-call | tf_op jit(solution)/shard_map/pack/pallas_call | solution.py:89
  5.3 11.5 %all-to-all-start = ((bf16[128,96,128]{2,1,0:T(8,128)(2,1)}), bf16[128,96,128]{2,1,0:T(8,128)(2,1)S(1)}, u32[]{:S(2)}, u32[]{:S(2)}) async-start(bf16[128,96,128]{2,1,0:T(8,128)(2,1)} %bitcast.51), calls=%async_computation | async-start | bytes 6291456 | tf_op jit(solution)/shard_map/all_to_all | solution.py:410
  16.8 2.5 %cut.3 = (bf16[2048,128]{1,0:T(8,128)(2,1)}, bf16[2048,128]{1,0:T(8,128)(2,1)}, bf16[2048,128]{1,0:T(8,128)(2,1)}, bf16[2048,128]{1,0:T(8,128)(2,1)}) custom-call(bf16[8,2048,128]{2,1,0:T(8,128)(2,1)} %bitcast.49), custom_call_target="tpu_custom_call" | custom-call | tf_op jit(solution)/shard_map/cut/pallas_call | solution.py:267
  19.3 1.1 %collective-permute-start = (bf16[2048,128]{1,0:T(8,128)(2,1)}, bf16[2048,128]{1,0:T(8,128)(2,1)S(1)}, u32[]{:S(2)}, u32[]{:S(2)}) collective-permute-start(bf16[2048,128]{1,0:T(8,128)(2,1)} %get-tuple-element.39), channel_id=1, source_target_pairs={{0,1},{1,0},{2,3},{3,2},{4,5},{5,4},{6,7},{7,6},{8,9},{9,8},{10,11... | collective-permute-start | bytes 1572872 | tf_op jit(solution)/shard_map/ppermute | solution.py:243
  21.0 2.4 %cut.2 = (bf16[2048,128]{1,0:T(8,128)(2,1)}, bf16[2048,128]{1,0:T(8,128)(2,1)}, bf16[2048,128]{1,0:T(8,128)(2,1)}, bf16[2048,128]{1,0:T(8,128)(2,1)}) custom-call(bf16[8,2048,128]{2,1,0:T(8,128)(2,1)} %bitcast.50), custom_call_target="tpu_custom_call" | custom-call | tf_op jit(solution)/shard_map/cut/pallas_call | solution.py:267
  23.7 0.7 collective-permute-done.3.refs_9_
  25.2 2.9 %add.16 = (bf16[1024,128]{1,0:T(8,128)(2,1)}, bf16[1024,128]{1,0:T(8,128)(2,1)}, bf16[1024,128]{1,0:T(8,128)(2,1)}, bf16[1024,128]{1,0:T(8,128)(2,1)}, bf16[2048,128]{1,0:T(8,128)(2,1)}) custom-call(bf16[2048,128]{1,0:T(8,128)(2,1)} %get-tuple-element.38.refs_0_.refs_2_, bf16[2048,128]{1,0:T(8,128)(2,1)} %copy-done.4, ...), custom_call_target="tpu_custom_call" | custom-call | tf_op jit(solution)/shard_map/add/pallas_call | solution.py:314
  28.1 0.8 collective-permute-start.4
  28.8 2.0 %collective-permute-start.5 = (bf16[1024,128]{1,0:T(8,128)(2,1)}, bf16[1024,128]{1,0:T(8,128)(2,1)}, u32[]{:S(2)}, u32[]{:S(2)}) collective-permute-start(bf16[1024,128]{1,0:T(8,128)(2,1)} %get-tuple-element.47), channel_id=1, source_target_pairs={{0,6},{1,7},{2,0},{3,1},{4,2},{5,3},{6,4},{7,5},{8,14},{9,15},{10,... | collective-permute-start | bytes 786440 | tf_op jit(solution)/shard_map/ppermute | solution.py:243
  30.8 0.8 and_select_fusion
  31.6 2.7 %collective-permute-start.8 = (bf16[1024,128]{1,0:T(8,128)(2,1)}, bf16[1024,128]{1,0:T(8,128)(2,1)}, u32[]{:S(2)}, u32[]{:S(2)}) collective-permute-start(bf16[1024,128]{1,0:T(8,128)(2,1)} %get-tuple-element.55), channel_id=1, source_target_pairs={{0,6},{1,7},{2,0},{3,1},{4,2},{5,3},{6,4},{7,5},{8,14},{9,15},{10,... | collective-permute-start | bytes 786440 | tf_op jit(solution)/shard_map/ppermute | solution.py:243
  34.3 25.8 %collective-permute-done.4.refs_2_ = bf16[1024,128]{1,0:T(8,128)(2,1)} collective-permute-done((bf16[1024,128]{1,0:T(8,128)(2,1)}, bf16[1024,128]{1,0:T(8,128)(2,1)}, u32[]{:S(2)}, u32[]{:S(2)}) %collective-permute-start.4) | collective-permute-done | bytes 262176 | tf_op jit(solution)/shard_map/ppermute | solution.py:243
  60.0 2.2 %add.17 = (bf16[1024,128]{1,0:T(8,128)(2,1)}, bf16[1024,128]{1,0:T(8,128)(2,1)}) custom-call(bf16[2048,128]{1,0:T(8,128)(2,1)} %get-tuple-element.40.refs_4_.refs_0_, bf16[2048,128]{1,0:T(8,128)(2,1)} %copy-done.2, bf16[1024,128]{1,0:T(8,128)(2,1)} %collective-permute-done.4.refs_2_, bf16[2048,128]{1,0:T(8,128)(2,1)} %get-tuple-element.42.refs_6_.refs_3_, ...), custom_call_target="tpu_custom_call" | custom-call | tf_op jit(solution)/shard_map/add/pallas_call | solution.py:314
  62.3 2.7 %collective-permute-start.9 = (bf16[1024,128]{1,0:T(8,128)(2,1)}, bf16[1024,128]{1,0:T(8,128)(2,1)S(1)}, u32[]{:S(2)}, u32[]{:S(2)}) collective-permute-start(bf16[1024,128]{1,0:T(8,128)(2,1)} %get-tuple-element.56), channel_id=1, source_target_pairs={{0,6},{1,7},{2,0},{3,1},{4,2},{5,3},{6,4},{7,5},{8,14},{9,15},{10,... | collective-permute-start | bytes 786440 | tf_op jit(solution)/shard_map/ppermute | solution.py:243
  65.1 0.8 multiply_add_fusion.slot_ref
  65.9 1.3 %unpack.1.old_ref = bf16[3,2048,128]{2,1,0:T(8,128)(2,1)S(1)} custom-call(s32[128]{0:T(128)S(1)} %multiply_add_fusion.slot_ref, bf16[256,48,128]{2,1,0:T(8,128)(2,1)S(1)} %bitcast.47), custom_call_target="tpu_custom_call" | custom-call | tf_op jit(solution)/shard_map/unpack/pallas_call | solution.py:139
  67.3 1.1 %copy-done = bf16[3,2048,128]{2,1,0:T(8,128)(2,1)} copy-done((bf16[3,2048,128]{2,1,0:T(8,128)(2,1)}, bf16[3,2048,128]{2,1,0:T(8,128)(2,1)S(1)}, u32[]{:S(2)}) %copy-start) | copy-done | bytes 1572888
  68.4 1.7 %collective-permute-done.6.refs_0_ = bf16[1024,128]{1,0:T(8,128)(2,1)S(1)} collective-permute-done((bf16[1024,128]{1,0:T(8,128)(2,1)}, bf16[1024,128]{1,0:T(8,128)(2,1)S(1)}, u32[]{:S(2)}, u32[]{:S(2)}) %collective-permute-start.6) | collective-permute-done | bytes 262176 | tf_op jit(solution)/shard_map/ppermute | solution.py:243
  70.2 0.7 copy-done.7
  71.0 4.1 %adam.1 = (bf16[2048,128]{1,0:T(8,128)(2,1)}, f32[2048,128]{1,0:T(8,128)}, bf16[2048,128]{1,0:T(8,128)(2,1)}, bf16[2048,128]{1,0:T(8,128)(2,1)}, bf16[1,128]{1,0:T(2,128)(2,1)}, /*index=5*/bf16[1,128]{1,0:T(2,128)(2,1)}) custom-call(bf16[3,2048,128]{2,1,0:T(8,128)(2,1)} %copy-done, bf16[2048,128]{1,0:T(8,128)(2,1)} %get-tuple-element.50.mine_ref, ...), custom_call_target="tpu_custom_call" | custom-call | tf_op jit(solution)/shard_map/adam/pallas_call | solution.py:203
  75.1 2.4 %collective-permute-start.12 = (bf16[2048,128]{1,0:T(8,128)(2,1)}, bf16[2048,128]{1,0:T(8,128)(2,1)S(1)}, u32[]{:S(2)}, u32[]{:S(2)}) collective-permute-start(bf16[2048,128]{1,0:T(8,128)(2,1)} %get-tuple-element.57.refs_0_), channel_id=1, source_target_pairs={{0,6},{1,7},{2,0},{3,1},{4,2},{5,3},{6,4},{7,5},{8,14},{9,15},{10,... | collective-permute-start | bytes 1572872 | tf_op jit(solution)/shard_map/ppermute | solution.py:243
  77.4 2.8 %collective-permute-start.10 = (bf16[2048,128]{1,0:T(8,128)(2,1)}, bf16[2048,128]{1,0:T(8,128)(2,1)S(1)}, u32[]{:S(2)}, u32[]{:S(2)}) collective-permute-start(bf16[2048,128]{1,0:T(8,128)(2,1)} %get-tuple-element.57.refs_0_), channel_id=1, source_target_pairs={{0,1},{1,0},{2,3},{3,2},{4,5},{5,4},{6,7},{7,6},{8,9},{9,8},{10,11... | collective-permute-start | bytes 1572872 | tf_op jit(solution)/shard_map/ppermute | solution.py:243
  80.3 6.2 %collective-permute-done.12.refs_3_ = bf16[2048,128]{1,0:T(8,128)(2,1)S(1)} collective-permute-done((bf16[2048,128]{1,0:T(8,128)(2,1)}, bf16[2048,128]{1,0:T(8,128)(2,1)S(1)}, u32[]{:S(2)}, u32[]{:S(2)}) %collective-permute-start.12) | collective-permute-done | bytes 524320 | tf_op jit(solution)/shard_map/ppermute | solution.py:243
  86.5 3.4 %collective-permute-start.14 = (bf16[2048,128]{1,0:T(8,128)(2,1)S(1)}, bf16[2048,128]{1,0:T(8,128)(2,1)S(1)}, u32[]{:S(2)}, u32[]{:S(2)}) collective-permute-start(bf16[2048,128]{1,0:T(8,128)(2,1)S(1)} %collective-permute-done.12.refs_3_), channel_id=1, source_target_pairs={{0,1},{1,0},{2,3},{3,2},{4,5},{5,4},{6,7},{7,6},{8,9},{9,8},{10,11... | collective-permute-start | bytes 1572872 | tf_op jit(solution)/shard_map/ppermute | solution.py:243
  89.9 3.3 %collective-permute-start.13 = (bf16[2048,128]{1,0:T(8,128)(2,1)S(1)}, bf16[2048,128]{1,0:T(8,128)(2,1)S(1)}, u32[]{:S(2)}, u32[]{:S(2)}) collective-permute-start(bf16[2048,128]{1,0:T(8,128)(2,1)S(1)} %collective-permute-done.11.refs_2_), channel_id=1, source_target_pairs={{0,1},{1,0},{2,3},{3,2},{4,5},{5,4},{6,7},{7,6},{8,9},{9,8},{10,11... | collective-permute-start | bytes 1572872 | tf_op jit(solution)/shard_map/ppermute | solution.py:243
  93.3 1.5 %collective-permute-start.15 = (bf16[1024,128]{1,0:T(8,128)(2,1)S(1)}, bf16[1024,128]{1,0:T(8,128)(2,1)S(1)}, u32[]{:S(2)}, u32[]{:S(2)}) collective-permute-start(bf16[1024,128]{1,0:T(8,128)(2,1)S(1)} %slice.8), channel_id=1, source_target_pairs={{0,2},{1,3},{2,4},{3,5},{4,6},{5,7},{6,0},{7,1},{8,10},{9,11},{10,... | collective-permute-start | bytes 786440 | tf_op jit(solution)/shard_map/ppermute | solution.py:243
  94.9 1.0 copy-done.1
  95.9 2.0 %join.2.refs_4_ = bf16[16384,128]{1,0:T(8,128)(2,1)} custom-call(bf16[2048,128]{1,0:T(8,128)(2,1)S(1)} %copy-done.1, bf16[2048,128]{1,0:T(8,128)(2,1)S(1)} %collective-permute-done.10.refs_1_, bf16[2048,128]{1,0:T(8,128)(2,1)S(1)} %collective-permute-done.11.refs_2_, bf16[2048,128]{1,0:T(8,128)(2,1)S(1)} %collective-permute-done.12.refs_3_, ...), custom_call_target="tpu_custom_call" | custom-call | tf_op jit(solution)/shard_map/join/pallas_call | solution.py:368
  97.9 3.3 %collective-permute-done.16.refs_1_ = bf16[1024,128]{1,0:T(8,128)(2,1)S(1)} collective-permute-done((bf16[1024,128]{1,0:T(8,128)(2,1)S(1)}, bf16[1024,128]{1,0:T(8,128)(2,1)S(1)}, u32[]{:S(2)}, u32[]{:S(2)}) %collective-permute-start.16) | collective-permute-done | bytes 262176 | tf_op jit(solution)/shard_map/ppermute | solution.py:243
  101.7 1.7 %collective-permute-start.17 = (bf16[1024,128]{1,0:T(8,128)(2,1)S(1)}, bf16[1024,128]{1,0:T(8,128)(2,1)S(1)}, u32[]{:S(2)}, u32[]{:S(2)}) collective-permute-start(bf16[1024,128]{1,0:T(8,128)(2,1)S(1)} %collective-permute-done.15.refs_0_), channel_id=1, source_target_pairs={{0,1},{1,0},{2,3},{3,2},{4,5},{5,4},{6,7},{7,6},{8,9},{9,8},{10,11... | collective-permute-start | bytes 786440 | tf_op jit(solution)/shard_map/ppermute | solution.py:243
  103.3 1.2 %collective-permute-done.17.refs_2_ = bf16[1024,128]{1,0:T(8,128)(2,1)S(1)} collective-permute-done((bf16[1024,128]{1,0:T(8,128)(2,1)S(1)}, bf16[1024,128]{1,0:T(8,128)(2,1)S(1)}, u32[]{:S(2)}, u32[]{:S(2)}) %collective-permute-start.17) | collective-permute-done | bytes 262176 | tf_op jit(solution)/shard_map/ppermute | solution.py:243
  104.9 1.1 %join.3 = bf16[16384,128]{1,0:T(8,128)(2,1)} custom-call(bf16[1024,128]{1,0:T(8,128)(2,1)S(1)} %collective-permute-done.15.refs_0_, bf16[1024,128]{1,0:T(8,128)(2,1)S(1)} %collective-permute-done.16.refs_1_, bf16[1024,128]{1,0:T(8,128)(2,1)S(1)} %collective-permute-done.17.refs_2_, ...), custom_call_target="tpu_custom_call", output_to_operand_aliasing={{}: (4, {})} | custom-call | tf_op jit(solution)/shard_map/join/pallas_call | solution.py:368
  (40 shorter events, 2.9 us)
Async XLA Ops:
  5.3 54.7 %all-to-all-start = ((bf16[128,96,128]{2,1,0:T(8,128)(2,1)}), bf16[128,96,128]{2,1,0:T(8,128)(2,1)S(1)}, u32[]{:S(2)}, u32[]{:S(2)}) async-start(bf16[128,96,128]{2,1,0:T(8,128)(2,1)} %bitcast.51), calls=%async_computation | async-start | bytes 6291456 | tf_op jit(solution)/shard_map/all_to_all | solution.py:410
  19.3 4.2 %collective-permute-start = (bf16[2048,128]{1,0:T(8,128)(2,1)}, bf16[2048,128]{1,0:T(8,128)(2,1)S(1)}, u32[]{:S(2)}, u32[]{:S(2)}) collective-permute-start(bf16[2048,128]{1,0:T(8,128)(2,1)} %get-tuple-element.39), channel_id=1, source_target_pairs={{0,1},{1,0},{2,3},{3,2},{4,5},{5,4},{6,7},{7,6},{8,9},{9,8},{10,11... | collective-permute-start | bytes 1572872 | tf_op jit(solution)/shard_map/ppermute | solution.py:243
  20.4 3.1 %collective-permute-start.1 = (bf16[2048,128]{1,0:T(8,128)(2,1)}, bf16[2048,128]{1,0:T(8,128)(2,1)S(1)}, u32[]{:S(2)}, u32[]{:S(2)}) collective-permute-start(bf16[2048,128]{1,0:T(8,128)(2,1)} %get-tuple-element.41), channel_id=1, source_target_pairs={{0,1},{1,0},{2,3},{3,2},{4,5},{5,4},{6,7},{7,6},{8,9},{9,8},{10,11... | collective-permute-start | bytes 1572872 | tf_op jit(solution)/shard_map/ppermute | solution.py:243
  20.5 3.2 %collective-permute-start.2 = (bf16[2048,128]{1,0:T(8,128)(2,1)}, bf16[2048,128]{1,0:T(8,128)(2,1)S(1)}, u32[]{:S(2)}, u32[]{:S(2)}) collective-permute-start(bf16[2048,128]{1,0:T(8,128)(2,1)} %get-tuple-element.43), channel_id=1, source_target_pairs={{0,1},{1,0},{2,3},{3,2},{4,5},{5,4},{6,7},{7,6},{8,9},{9,8},{10,11... | collective-permute-start | bytes 1572872 | tf_op jit(solution)/shard_map/ppermute | solution.py:243
  20.9 3.5 %collective-permute-start.3 = (bf16[2048,128]{1,0:T(8,128)(2,1)}, bf16[2048,128]{1,0:T(8,128)(2,1)S(1)}, u32[]{:S(2)}, u32[]{:S(2)}) collective-permute-start(bf16[2048,128]{1,0:T(8,128)(2,1)} %get-tuple-element.45), channel_id=1, source_target_pairs={{0,1},{1,0},{2,3},{3,2},{4,5},{5,4},{6,7},{7,6},{8,9},{9,8},{10,11... | collective-permute-start | bytes 1572872 | tf_op jit(solution)/shard_map/ppermute | solution.py:243
  23.5 1.0 copy-start.4
  23.5 1.0 copy-start.2
  23.7 1.0 copy-start.3
  24.4 0.8 copy-start.5
  28.1 31.9 %collective-permute-start.4 = (bf16[1024,128]{1,0:T(8,128)(2,1)}, bf16[1024,128]{1,0:T(8,128)(2,1)}, u32[]{:S(2)}, u32[]{:S(2)}) collective-permute-start(bf16[1024,128]{1,0:T(8,128)(2,1)} %get-tuple-element.46), channel_id=1, source_target_pairs={{0,2},{1,3},{2,4},{3,5},{4,6},{5,7},{6,0},{7,1},{8,10},{9,11},{10,... | collective-permute-start | bytes 786440 | tf_op jit(solution)/shard_map/ppermute | solution.py:243
  28.8 31.2 %collective-permute-start.5 = (bf16[1024,128]{1,0:T(8,128)(2,1)}, bf16[1024,128]{1,0:T(8,128)(2,1)}, u32[]{:S(2)}, u32[]{:S(2)}) collective-permute-start(bf16[1024,128]{1,0:T(8,128)(2,1)} %get-tuple-element.47), channel_id=1, source_target_pairs={{0,6},{1,7},{2,0},{3,1},{4,2},{5,3},{6,4},{7,5},{8,14},{9,15},{10,... | collective-permute-start | bytes 786440 | tf_op jit(solution)/shard_map/ppermute | solution.py:243
  31.6 36.8 %collective-permute-start.7 = (bf16[1024,128]{1,0:T(8,128)(2,1)}, bf16[1024,128]{1,0:T(8,128)(2,1)S(1)}, u32[]{:S(2)}, u32[]{:S(2)}) collective-permute-start(bf16[1024,128]{1,0:T(8,128)(2,1)} %get-tuple-element.54), channel_id=1, source_target_pairs={{0,2},{1,3},{2,4},{3,5},{4,6},{5,7},{6,0},{7,1},{8,10},{9,11},{10,... | collective-permute-start | bytes 786440 | tf_op jit(solution)/shard_map/ppermute | solution.py:243
  31.6 36.8 %collective-permute-start.8 = (bf16[1024,128]{1,0:T(8,128)(2,1)}, bf16[1024,128]{1,0:T(8,128)(2,1)}, u32[]{:S(2)}, u32[]{:S(2)}) collective-permute-start(bf16[1024,128]{1,0:T(8,128)(2,1)} %get-tuple-element.55), channel_id=1, source_target_pairs={{0,6},{1,7},{2,0},{3,1},{4,2},{5,3},{6,4},{7,5},{8,14},{9,15},{10,... | collective-permute-start | bytes 786440 | tf_op jit(solution)/shard_map/ppermute | solution.py:243
  62.2 7.9 %collective-permute-start.6 = (bf16[1024,128]{1,0:T(8,128)(2,1)}, bf16[1024,128]{1,0:T(8,128)(2,1)S(1)}, u32[]{:S(2)}, u32[]{:S(2)}) collective-permute-start(bf16[1024,128]{1,0:T(8,128)(2,1)} %get-tuple-element.53), channel_id=1, source_target_pairs={{0,2},{1,3},{2,4},{3,5},{4,6},{5,7},{6,0},{7,1},{8,10},{9,11},{10,... | collective-permute-start | bytes 786440 | tf_op jit(solution)/shard_map/ppermute | solution.py:243
  62.3 7.9 %collective-permute-start.9 = (bf16[1024,128]{1,0:T(8,128)(2,1)}, bf16[1024,128]{1,0:T(8,128)(2,1)S(1)}, u32[]{:S(2)}, u32[]{:S(2)}) collective-permute-start(bf16[1024,128]{1,0:T(8,128)(2,1)} %get-tuple-element.56), channel_id=1, source_target_pairs={{0,6},{1,7},{2,0},{3,1},{4,2},{5,3},{6,4},{7,5},{8,14},{9,15},{10,... | collective-permute-start | bytes 786440 | tf_op jit(solution)/shard_map/ppermute | solution.py:243
  67.2 1.1 %copy-start = (bf16[3,2048,128]{2,1,0:T(8,128)(2,1)}, bf16[3,2048,128]{2,1,0:T(8,128)(2,1)S(1)}, u32[]{:S(2)}) copy-start(bf16[3,2048,128]{2,1,0:T(8,128)(2,1)S(1)} %unpack.1.old_ref) | copy-start | bytes 4718596
  68.4 1.8 %copy-start.6 = (bf16[1024,128]{1,0:T(8,128)(2,1)}, bf16[1024,128]{1,0:T(8,128)(2,1)S(1)}, u32[]{:S(2)}) copy-start(bf16[1024,128]{1,0:T(8,128)(2,1)S(1)} %collective-permute-done.7.refs_1_) | copy-start | bytes 786436
  70.1 0.7 copy-start.7
  70.1 0.8 copy-start.8
  75.1 11.4 %collective-permute-start.12 = (bf16[2048,128]{1,0:T(8,128)(2,1)}, bf16[2048,128]{1,0:T(8,128)(2,1)S(1)}, u32[]{:S(2)}, u32[]{:S(2)}) collective-permute-start(bf16[2048,128]{1,0:T(8,128)(2,1)} %get-tuple-element.57.refs_0_), channel_id=1, source_target_pairs={{0,6},{1,7},{2,0},{3,1},{4,2},{5,3},{6,4},{7,5},{8,14},{9,15},{10,... | collective-permute-start | bytes 1572872 | tf_op jit(solution)/shard_map/ppermute | solution.py:243
  77.4 12.5 %collective-permute-start.11 = (bf16[2048,128]{1,0:T(8,128)(2,1)}, bf16[2048,128]{1,0:T(8,128)(2,1)S(1)}, u32[]{:S(2)}, u32[]{:S(2)}) collective-permute-start(bf16[2048,128]{1,0:T(8,128)(2,1)} %get-tuple-element.57.refs_0_), channel_id=1, source_target_pairs={{0,2},{1,3},{2,4},{3,5},{4,6},{5,7},{6,0},{7,1},{8,10},{9,11},{10,... | collective-permute-start | bytes 1572872 | tf_op jit(solution)/shard_map/ppermute | solution.py:243
  77.4 17.4 %collective-permute-start.10 = (bf16[2048,128]{1,0:T(8,128)(2,1)}, bf16[2048,128]{1,0:T(8,128)(2,1)S(1)}, u32[]{:S(2)}, u32[]{:S(2)}) collective-permute-start(bf16[2048,128]{1,0:T(8,128)(2,1)} %get-tuple-element.57.refs_0_), channel_id=1, source_target_pairs={{0,1},{1,0},{2,3},{3,2},{4,5},{5,4},{6,7},{7,6},{8,9},{9,8},{10,11... | collective-permute-start | bytes 1572872 | tf_op jit(solution)/shard_map/ppermute | solution.py:243
  86.5 8.4 %collective-permute-start.14 = (bf16[2048,128]{1,0:T(8,128)(2,1)S(1)}, bf16[2048,128]{1,0:T(8,128)(2,1)S(1)}, u32[]{:S(2)}, u32[]{:S(2)}) collective-permute-start(bf16[2048,128]{1,0:T(8,128)(2,1)S(1)} %collective-permute-done.12.refs_3_), channel_id=1, source_target_pairs={{0,1},{1,0},{2,3},{3,2},{4,5},{5,4},{6,7},{7,6},{8,9},{9,8},{10,11... | collective-permute-start | bytes 1572872 | tf_op jit(solution)/shard_map/ppermute | solution.py:243
  89.9 5.0 %collective-permute-start.13 = (bf16[2048,128]{1,0:T(8,128)(2,1)S(1)}, bf16[2048,128]{1,0:T(8,128)(2,1)S(1)}, u32[]{:S(2)}, u32[]{:S(2)}) collective-permute-start(bf16[2048,128]{1,0:T(8,128)(2,1)S(1)} %collective-permute-done.11.refs_2_), channel_id=1, source_target_pairs={{0,1},{1,0},{2,3},{3,2},{4,5},{5,4},{6,7},{7,6},{8,9},{9,8},{10,11... | collective-permute-start | bytes 1572872 | tf_op jit(solution)/shard_map/ppermute | solution.py:243
  93.2 8.0 %collective-permute-start.16 = (bf16[1024,128]{1,0:T(8,128)(2,1)S(1)}, bf16[1024,128]{1,0:T(8,128)(2,1)S(1)}, u32[]{:S(2)}, u32[]{:S(2)}) collective-permute-start(bf16[1024,128]{1,0:T(8,128)(2,1)S(1)} %slice.9), channel_id=1, source_target_pairs={{0,6},{1,7},{2,0},{3,1},{4,2},{5,3},{6,4},{7,5},{8,14},{9,15},{10,... | collective-permute-start | bytes 786440 | tf_op jit(solution)/shard_map/ppermute | solution.py:243
  93.3 8.3 %collective-permute-start.15 = (bf16[1024,128]{1,0:T(8,128)(2,1)S(1)}, bf16[1024,128]{1,0:T(8,128)(2,1)S(1)}, u32[]{:S(2)}, u32[]{:S(2)}) collective-permute-start(bf16[1024,128]{1,0:T(8,128)(2,1)S(1)} %slice.8), channel_id=1, source_target_pairs={{0,2},{1,3},{2,4},{3,5},{4,6},{5,7},{6,0},{7,1},{8,10},{9,11},{10,... | collective-permute-start | bytes 786440 | tf_op jit(solution)/shard_map/ppermute | solution.py:243
  94.9 1.0 copy-start.1
  101.7 2.8 %collective-permute-start.17 = (bf16[1024,128]{1,0:T(8,128)(2,1)S(1)}, bf16[1024,128]{1,0:T(8,128)(2,1)S(1)}, u32[]{:S(2)}, u32[]{:S(2)}) collective-permute-start(bf16[1024,128]{1,0:T(8,128)(2,1)S(1)} %collective-permute-done.15.refs_0_), channel_id=1, source_target_pairs={{0,1},{1,0},{2,3},{3,2},{4,5},{5,4},{6,7},{7,6},{8,9},{9,8},{10,11... | collective-permute-start | bytes 786440 | tf_op jit(solution)/shard_map/ppermute | solution.py:243
  103.3 1.5 %collective-permute-start.18 = (bf16[1024,128]{1,0:T(8,128)(2,1)S(1)}, bf16[1024,128]{1,0:T(8,128)(2,1)S(1)}, u32[]{:S(2)}, u32[]{:S(2)}) collective-permute-start(bf16[1024,128]{1,0:T(8,128)(2,1)S(1)} %collective-permute-done.16.refs_1_), channel_id=1, source_target_pairs={{0,1},{1,0},{2,3},{3,2},{4,5},{5,4},{6,7},{7,6},{8,9},{9,8},{10,11... | collective-permute-start | bytes 786440 | tf_op jit(solution)/shard_map/ppermute | solution.py:243

commit v4 on v3

--- a/solution.py
+++ b/solution.py
@@ -147,13 +147,7 @@
     )(slots, arrived)
 
 
-def adam_kernel(rows, chunks, old_ref, mine_ref, *refs):
-    side_refs, refs = refs[:4], refs[4:]
-    weights_ref, master_ref, mcode_ref, scode_ref, mscale_ref, sscale_ref = refs[:6]
-    old, addends, sems = refs[6:]
-    span = chunks * SUB
-    groups = rows // SUB
-    half = groups // 2 * span
+def start_loads(half, old_ref, mine_ref, side_refs, old, addends, sems):
     loads = []
     for h in range(2):
         part = pl.ds(h * half, half)
@@ -163,24 +157,91 @@
         loads.append([pltpu.make_async_copy(ref, room, sems.at[h, k]) for k, (ref, room) in enumerate(pairs)])
     for load in loads[0] + loads[1]:
         load.start()
+    return loads
+
+
+def step_values(old, addends, there):
+    gradient = addends[0, there, :].astype(jnp.float32)
+    for k in range(1, ADDENDS):
+        gradient += addends[k, there, :].astype(jnp.float32)
+    weight_old, mean_old, square_old = (old[k, there, :].astype(jnp.float32) for k in range(3))
+    mean_next = 0.9 * mean_old + 0.1 * gradient
+    square_next = 0.95 * square_old + 0.05 * gradient * gradient
+    master = weight_old - 0.05 * (mean_next / (jnp.sqrt(square_next) + 1e-08) + 0.1 * weight_old)
+    return mean_next, square_next, master
+
+
+def weights_kernel(rows, chunks, old_ref, mine_ref, *refs):
+    side_refs, out_refs = refs[:4], refs[4:6]
+    old, addends, weights, sems, out_sems = refs[6:]
+    span = chunks * SUB
+    groups = rows // SUB
+    half = groups // 2 * span
+    loads = start_loads(half, old_ref, mine_ref, side_refs, old, addends, sems)
+    stores = []
+    for h in range(2):
+        for load in loads[h]:
+            load.wait()
+        for group in range(h * groups // 2, (h + 1) * groups // 2):
+            there = pl.ds(group * span, span)
+            weights[there, :] = step_values(old, addends, there)[2].astype(weights.dtype)
+        stores.append(pltpu.make_async_copy(weights.at[pl.ds(h * half, half)], out_refs[h], out_sems.at[h]))
+        stores[h].start()
+    for store in stores:
+        store.wait()
+
+
+def new_weights(old, addends, rows, chunks):
+    flat = (rows * chunks, LANES)
+    bf16 = jnp.bfloat16
+    hbm = pl.BlockSpec(memory_space=pl.ANY)
+    return pl.pallas_call(
+        functools.partial(weights_kernel, rows, chunks),
+        out_shape=[jax.ShapeDtypeStruct((flat[0] // 2, LANES), bf16)] * 2,
+        in_specs=[hbm] * 6,
+        out_specs=[hbm] * 2,
+        scratch_shapes=[
+            pltpu.VMEM((3, *flat), bf16),
+            pltpu.VMEM((ADDENDS, *flat), bf16),
+            pltpu.VMEM(flat, bf16),
+            pltpu.SemaphoreType.DMA((2, 3 + ADDENDS)),
+            pltpu.SemaphoreType.DMA((2,)),
+        ],
+        compiler_params=pltpu.CompilerParams(vmem_limit_bytes=56 * 1024 * 1024),
+        name="new_weights",
+    )(old, *addends)
+
+
+def adam_kernel(rows, chunks, old_ref, mine_ref, *refs):
+    side_refs, weight_refs, refs = refs[:4], refs[4:6], refs[6:]
+    whole_ref, master_ref, mcode_ref, scode_ref, mscale_ref, sscale_ref = refs[:6]
+    old, addends, weights, sems, in_sems, out_sems = refs[6:]
+    span = chunks * SUB
+    groups = rows // SUB
+    half = groups // 2 * span
+    loads = start_loads(half, old_ref, mine_ref, side_refs, old, addends, sems)
+    own = lax.axis_index("dp") * 2 * half
+    fetches = [pltpu.make_async_copy(weight_refs[h], weights.at[h], in_sems.at[h]) for h in range(2)]
+    stores = [
+        pltpu.make_async_copy(weights.at[h], whole_ref.at[pl.ds(pl.multiple_of(own + h * half, half), half)], out_sems.at[h])
+        for h in range(2)
+    ]
+    for fetch in fetches:
+        fetch.start()
     lane = lax.broadcasted_iota(jnp.int32, (SUB, LANES), 1)
     sub = lax.broadcasted_iota(jnp.int32, (SUB, LANES), 0)
     mline = jnp.zeros((SUB, LANES), jnp.float32)
     sline = jnp.zeros((SUB, LANES), jnp.float32)
     for group in range(groups):
         if group % (groups // 2) == 0:
-            for load in loads[group * 2 // groups]:
+            h = group * 2 // groups
+            for load in loads[h]:
                 load.wait()
+            fetches[h].wait()
+            stores[h].start()
         there = pl.ds(group * span, span)
-        gradient = addends[0, there, :].astype(jnp.float32)
-        for k in range(1, ADDENDS):
-            gradient += addends[k, there, :].astype(jnp.float32)
-        weight_old, mean_old, square_old = (old[k, there, :].astype(jnp.float32) for k in range(3))
-        mean_next = 0.9 * mean_old + 0.1 * gradient
-        square_next = 0.95 * square_old + 0.05 * gradient * gradient
-        master = weight_old - 0.05 * (mean_next / (jnp.sqrt(square_next) + 1e-08) + 0.1 * weight_old)
+        mean_next, square_next, master = step_values(old, addends, there)
         master_ref[there, :] = master
-        weights_ref[there, :] = master.astype(jnp.bfloat16)
         mean_next = mean_next.reshape(chunks, SUB, LANES)
         square_next = square_next.reshape(chunks, SUB, LANES)
         mpeak = jnp.max(jnp.max(jnp.abs(mean_next), axis=0), axis=1, keepdims=True)
@@ -194,32 +255,38 @@
         sline = jnp.where(mine, sscale, sline)
     mscale_ref[...] = jnp.sum(mline, axis=0, keepdims=True).astype(jnp.bfloat16)
     sscale_ref[...] = jnp.sum(sline, axis=0, keepdims=True).astype(jnp.bfloat16)
-
-
-def adam(old, addends, rows, chunks):
+    for store in stores:
+        store.wait()
+
+
+def adam(old, addends, weights, rows, chunks):
     flat = (rows * chunks, LANES)
     bf16, f32 = jnp.bfloat16, jnp.float32
     vmem = pl.BlockSpec(memory_space=pltpu.VMEM)
     return pl.pallas_call(
         functools.partial(adam_kernel, rows, chunks),
         out_shape=[
-            jax.ShapeDtypeStruct(flat, bf16),
+            jax.ShapeDtypeStruct((RING * CORES * flat[0], LANES), bf16),
             jax.ShapeDtypeStruct(flat, f32),
             jax.ShapeDtypeStruct(flat, bf16),
             jax.ShapeDtypeStruct(flat, bf16),
             jax.ShapeDtypeStruct((1, rows), bf16),
             jax.ShapeDtypeStruct((1, rows), bf16),
         ],
-        in_specs=[pl.BlockSpec(memory_space=pl.ANY)] * 6,
-        out_specs=[vmem] * 6,
+        in_specs=[pl.BlockSpec(memory_space=pl.ANY)] * 8,
+        out_specs=[pl.BlockSpec(memory_space=pl.ANY)] + [vmem] * 5,
         scratch_shapes=[
             pltpu.VMEM((3, *flat), bf16),
             pltpu.VMEM((ADDENDS, *flat), bf16),
+            pltpu.VMEM((2, flat[0] // 2, LANES), bf16),
             pltpu.SemaphoreType.DMA((2, 3 + ADDENDS)),
+            pltpu.SemaphoreType.DMA((2,)),
+            pltpu.SemaphoreType.DMA((2,)),
         ],
         compiler_params=pltpu.CompilerParams(vmem_limit_bytes=56 * 1024 * 1024),
+        cost_estimate=pl.CostEstimate(flops=0, transcendentals=0, bytes_accessed=16 * 1024 * 1024),
         name="adam",
-    )(old, *addends)
+    )(old, *addends, *weights)
 
 
 def place():
@@ -239,8 +306,9 @@
     ]
 
 
-def send(values, shift, flip=False):
-    return lax.ppermute(values, "dp", sends(shift, flip))
+def send(values, shift, flip=False, name="r_send"):
+    with jax.named_scope(name):
+        return lax.ppermute(values, "dp", sends(shift, flip))
 
 
 def cut_kernel(shards, grad_ref, *refs):
@@ -374,21 +442,30 @@
         + [pltpu.SemaphoreType.DMA((len(parts),))] * 2,
         compiler_params=pltpu.CompilerParams(vmem_limit_bytes=16 * 1024 * 1024),
         input_output_aliases={} if whole is None else {len(parts): 0},
+        cost_estimate=pl.CostEstimate(flops=0, transcendentals=0, bytes_accessed=0),
         name="join",
     )(*given)
 
 
-def gather_shards(mine):
-    span = mine.shape[0]
-    half = span // 2
-    up, dn, sib = send(mine, 1), send(mine, 3), send(mine, 0, True)
-    opp_lo, opp_hi = send(up[:half], 1), send(dn[half:], 3)
-    up_sib, dn_sib = send(up, 0, True), send(dn, 0, True)
-    starts = [(0, 0, 0), (0, 1, 0), (3, 0, 0), (1, 0, 0), (3, 1, 0), (1, 1, 0)]
-    most = join(span, starts, [mine, sib, up, dn, up_sib, dn_sib])
-    most, opp_lo, opp_hi = lax.optimization_barrier((most, opp_lo, opp_hi))
-    starts = [(2, 0, 0), (2, 0, half), (2, 1, 0), (2, 1, half)]
-    return join(span, starts, [opp_lo, opp_hi, send(opp_lo, 0, True), send(opp_hi, 0, True)], most)
+def gather_shards(lo, hi, run_between):
+    half = lo.shape[0]
+    span = 2 * half
+    up_lo, dn_hi = send(lo, 1, name="g_up_lo"), send(hi, 3, name="g_dn_hi")
+    up_hi, dn_lo = send(hi, 1, name="g_up_hi"), send(lo, 3, name="g_dn_lo")
+    sib_lo, sib_hi = send(lo, 0, True, name="g_sib_lo"), send(hi, 0, True, name="g_sib_hi")
+    whole, *rest = run_between(sib_lo)
+    up_lo, dn_hi, rest[-1] = lax.optimization_barrier((up_lo, dn_hi, rest[-1]))
+    opp_lo, opp_hi = send(up_lo, 1, name="g_opp_lo"), send(dn_hi, 3, name="g_opp_hi")
+    sib_up_lo, sib_dn_hi = send(up_lo, 0, True, name="g_sib_up_lo"), send(dn_hi, 0, True, name="g_sib_dn_hi")
+    starts = [(3, 0, 0), (1, 0, half), (3, 0, half), (1, 0, 0), (0, 1, 0), (0, 1, half)]
+    whole = join(span, starts, [up_lo, dn_hi, up_hi, dn_lo, sib_lo, sib_hi], whole)
+    whole, up_hi, dn_lo, opp_lo, opp_hi = lax.optimization_barrier((whole, up_hi, dn_lo, opp_lo, opp_hi))
+    parts = [opp_lo, opp_hi]
+    for part, name in zip((opp_lo, opp_hi, up_hi, dn_lo), ("opp_lo", "opp_hi", "up_hi", "dn_lo")):
+        parts.append(send(part, 0, True, name="g_sib_" + name))
+    parts += [sib_up_lo, sib_dn_hi]
+    starts = [(2, 0, 0), (2, 0, half), (2, 1, 0), (2, 1, half), (3, 1, half), (1, 1, 0), (3, 1, 0), (1, 1, half)]
+    return join(span, starts, parts, whole), rest
 
 
 def arrivals(old_map, block_rows, peer_cap):
@@ -412,9 +489,16 @@
     ).reshape(slot_total, 3 * chunks, LANES)
     addends, arrived = reduce_shards(late_grads, arrived)
     old = unpack(arrivals(late_map, block_rows, peer_cap), arrived, block_rows, chunks)
-    mine, *blocks, mean_scales, square_scales = adam(old, addends, block_rows, chunks)
+    lo, hi = new_weights(old, addends, block_rows, chunks)
+
+    def run_between(*arrived_first):
+        late_old, late_addends, _ = lax.optimization_barrier((old, addends, arrived_first))
+        return adam(late_old, late_addends, (lo, hi), block_rows, chunks)
+
+    weights, rest = gather_shards(lo, hi, run_between)
+    *blocks, mean_scales, square_scales = rest
     master, mean_codes, square_codes = (from_tiles(x, block_rows, block_len) for x in blocks)
-    weights = from_tiles(gather_shards(mine), RING * CORES * block_rows, block_len)
+    weights = from_tiles(weights, RING * CORES * block_rows, block_len)
     return (weights, master, mean_codes, mean_scales.reshape(-1), square_codes, square_scales.reshape(-1))
 
 

time: 106 us -> 102 us (0.962)
  waiting for transfers between devices: 40 us -> 34.9 us
  Pallas kernels: 23.1 us -> 26.6 us
  starting transfers between devices: 36.6 us -> 34.9 us
  local copies, waits for them, and re-layouts: 3.82 us -> 2.76 us
    ppermute x19 -> x24, waiting for transfers between devices: 40 us -> 34.9 us  [send(): return lax.ppermute(values, 'dp', sends(shift, flip))]
    pallas_call x0 -> x1, Pallas kernels: none -> 3.2 us  [new_weights(): pl.pallas_call(functools.partial(weights_kernel, rows, chunks), out_shape...]
    ppermute x19 -> x24, starting transfers between devices: 25.1 us -> 23.4 us  [send(): return lax.ppermute(values, 'dp', sends(shift, flip))]
    unnamed x18 -> x16, local copies, waits for them, and re-layouts: 3.78 us -> 2.76 us
  transfers between devices with their start and end apart: 20 -> 25, of which waited for: 9 -> 10; matrix products, arithmetic and copies ran while one was open for 2% -> 2% of each run, Pallas kernels for 12% -> 17%
where the time goes in v4:
time: 102 us
  starting transfers between devices  34.9 us (34%)
  waiting for transfers between devices  34.9 us (34%)
  Pallas kernels  26.6 us (26%)
  local copies, waits for them, and re-layouts  2.76 us (3%)
  other arithmetic  1.71 us (2%)
    ppermute x24, waiting for transfers between devices, send(): return lax.ppermute(values, 'dp', sends(shift, flip))  34.9 us
    ppermute x24, starting transfers between devices, send(): return lax.ppermute(values, 'dp', sends(shift, flip))  23.4 us
    all_to_all x1, starting transfers between devices, local(): lax.all_to_all(packed.reshape(count_all, peer_cap * 3 * chunks, LANES), A...  11.5 us
    pallas_call x2, Pallas kernels, add(): pl.pallas_call(functools.partial(add_kernel, windows, order), out_shape=[...  5 us
    pallas_call x2, Pallas kernels, cut(): pl.pallas_call(functools.partial(cut_kernel, shards), out_shape=[jax.Shap...  4.87 us
    pallas_call x1, Pallas kernels, pack(): pl.pallas_call(functools.partial(pack_kernel, rows, chunks), out_shape=ja...  4.65 us
    pallas_call x1, Pallas kernels, adam(): pl.pallas_call(functools.partial(adam_kernel, rows, chunks), out_shape=[j...  4.59 us
    pallas_call x1, Pallas kernels, new_weights(): pl.pallas_call(functools.partial(weights_kernel, rows, chunks), out_shape...  3.2 us
  transfers between devices with their start and end apart: 25, of which 10 were waited for; matrix products, arithmetic and copies ran while one was open for 2% of the time, Pallas kernels for 17%

profile of v4, /device:TPU:1, one launch (start us, length us, event | category | flops | bytes accessed | tf_op | source)
XLA Modules:
  0.0 101.8 jit_solution(16575465711735207949)
XLA Ops:
  0.6 4.7 %pack.1 = bf16[256,48,128]{2,1,0:T(8,128)(2,1)} custom-call(s32[128,128]{1,0:T(8,128)} %bitcast.55, bf16[1,128]{1,0:T(2,128)(2,1)} %bitcast.56, bf16[1,128]{1,0:T(2,128)(2,1)} %bitcast.57, f32[2048,128]{1,0:T(8,128)} %bitcast.52, bf16[2048,128]{1,0:T(8,128)(2,1)} %bitcast.53, bf16[2048,128]{1,0:T(8,128)(2,1)} %bitcast.54), custom_call_target="tpu_custom_call" | custom-call | tf_op jit(solution)/shard_map/pack/pallas_call | solution.py:89
  5.3 11.5 %all-to-all-start = ((bf16[128,96,128]{2,1,0:T(8,128)(2,1)}), bf16[128,96,128]{2,1,0:T(8,128)(2,1)S(1)}, u32[]{:S(2)}, u32[]{:S(2)}) async-start(bf16[128,96,128]{2,1,0:T(8,128)(2,1)} %bitcast.51), calls=%async_computation | async-start | bytes 6291456 | tf_op jit(solution)/shard_map/all_to_all | solution.py:487
  16.8 2.5 %cut.3 = (bf16[2048,128]{1,0:T(8,128)(2,1)}, bf16[2048,128]{1,0:T(8,128)(2,1)}, bf16[2048,128]{1,0:T(8,128)(2,1)}, bf16[2048,128]{1,0:T(8,128)(2,1)}) custom-call(bf16[8,2048,128]{2,1,0:T(8,128)(2,1)} %bitcast.48), custom_call_target="tpu_custom_call" | custom-call | tf_op jit(solution)/shard_map/cut/pallas_call | solution.py:335
  19.3 1.1 %collective-permute-start = (bf16[2048,128]{1,0:T(8,128)(2,1)}, bf16[2048,128]{1,0:T(8,128)(2,1)S(1)}, u32[]{:S(2)}, u32[]{:S(2)}) collective-permute-start(bf16[2048,128]{1,0:T(8,128)(2,1)} %get-tuple-element.52), channel_id=1, source_target_pairs={{0,1},{1,0},{2,3},{3,2},{4,5},{5,4},{6,7},{7,6},{8,9},{9,8},{10,11... | collective-permute-start | bytes 1572872 | tf_op jit(solution)/shard_map/r_send/ppermute | solution.py:311
  21.0 2.4 %cut.2 = (bf16[2048,128]{1,0:T(8,128)(2,1)}, bf16[2048,128]{1,0:T(8,128)(2,1)}, bf16[2048,128]{1,0:T(8,128)(2,1)}, bf16[2048,128]{1,0:T(8,128)(2,1)}) custom-call(bf16[8,2048,128]{2,1,0:T(8,128)(2,1)} %bitcast.49), custom_call_target="tpu_custom_call" | custom-call | tf_op jit(solution)/shard_map/cut/pallas_call | solution.py:335
  23.7 0.7 collective-permute-done.3.refs_9_
  25.2 2.8 %add.16 = (bf16[1024,128]{1,0:T(8,128)(2,1)}, bf16[1024,128]{1,0:T(8,128)(2,1)}, bf16[1024,128]{1,0:T(8,128)(2,1)}, bf16[1024,128]{1,0:T(8,128)(2,1)}, bf16[2048,128]{1,0:T(8,128)(2,1)}) custom-call(bf16[2048,128]{1,0:T(8,128)(2,1)} %get-tuple-element.51.refs_0_.refs_2_, bf16[2048,128]{1,0:T(8,128)(2,1)} %copy-done.3, ...), custom_call_target="tpu_custom_call" | custom-call | tf_op jit(solution)/shard_map/add/pallas_call | solution.py:382
  28.1 0.8 collective-permute-start.4
  28.8 2.0 %collective-permute-start.5 = (bf16[1024,128]{1,0:T(8,128)(2,1)}, bf16[1024,128]{1,0:T(8,128)(2,1)}, u32[]{:S(2)}, u32[]{:S(2)}) collective-permute-start(bf16[1024,128]{1,0:T(8,128)(2,1)} %get-tuple-element.60), channel_id=1, source_target_pairs={{0,6},{1,7},{2,0},{3,1},{4,2},{5,3},{6,4},{7,5},{8,14},{9,15},{10,... | collective-permute-start | bytes 786440 | tf_op jit(solution)/shard_map/r_send/ppermute | solution.py:311
  30.8 0.8 and_select_fusion
  31.6 2.7 %collective-permute-start.8 = (bf16[1024,128]{1,0:T(8,128)(2,1)}, bf16[1024,128]{1,0:T(8,128)(2,1)}, u32[]{:S(2)}, u32[]{:S(2)}) collective-permute-start(bf16[1024,128]{1,0:T(8,128)(2,1)} %get-tuple-element.68), channel_id=1, source_target_pairs={{0,6},{1,7},{2,0},{3,1},{4,2},{5,3},{6,4},{7,5},{8,14},{9,15},{10,... | collective-permute-start | bytes 786440 | tf_op jit(solution)/shard_map/r_send/ppermute | solution.py:311
  34.2 25.8 %collective-permute-done.4.refs_2_ = bf16[1024,128]{1,0:T(8,128)(2,1)} collective-permute-done((bf16[1024,128]{1,0:T(8,128)(2,1)}, bf16[1024,128]{1,0:T(8,128)(2,1)}, u32[]{:S(2)}, u32[]{:S(2)}) %collective-permute-start.4) | collective-permute-done | bytes 262176 | tf_op jit(solution)/shard_map/r_send/ppermute | solution.py:311
  60.0 2.2 %add.17 = (bf16[1024,128]{1,0:T(8,128)(2,1)}, bf16[1024,128]{1,0:T(8,128)(2,1)}) custom-call(bf16[2048,128]{1,0:T(8,128)(2,1)} %get-tuple-element.53.refs_4_.refs_0_, bf16[2048,128]{1,0:T(8,128)(2,1)} %copy-done.1, bf16[1024,128]{1,0:T(8,128)(2,1)} %collective-permute-done.4.refs_2_, bf16[2048,128]{1,0:T(8,128)(2,1)} %get-tuple-element.55.refs_6_.refs_3_, ...), custom_call_target="tpu_custom_call" | custom-call | tf_op jit(solution)/shard_map/add/pallas_call | solution.py:382
  62.3 2.7 %collective-permute-start.9 = (bf16[1024,128]{1,0:T(8,128)(2,1)}, bf16[1024,128]{1,0:T(8,128)(2,1)S(1)}, u32[]{:S(2)}, u32[]{:S(2)}) collective-permute-start(bf16[1024,128]{1,0:T(8,128)(2,1)} %get-tuple-element.69), channel_id=1, source_target_pairs={{0,6},{1,7},{2,0},{3,1},{4,2},{5,3},{6,4},{7,5},{8,14},{9,15},{10,... | collective-permute-start | bytes 786440 | tf_op jit(solution)/shard_map/r_send/ppermute | solution.py:311
  65.1 0.8 multiply_add_fusion.slot_ref
  65.9 1.3 %unpack.1.old_ref = bf16[3,2048,128]{2,1,0:T(8,128)(2,1)S(1)} custom-call(s32[128]{0:T(128)S(1)} %multiply_add_fusion.slot_ref, bf16[256,48,128]{2,1,0:T(8,128)(2,1)S(1)} %bitcast.47), custom_call_target="tpu_custom_call" | custom-call | tf_op jit(solution)/shard_map/unpack/pallas_call | solution.py:139
  67.2 1.2 %copy-done = bf16[3,2048,128]{2,1,0:T(8,128)(2,1)} copy-done((bf16[3,2048,128]{2,1,0:T(8,128)(2,1)}, bf16[3,2048,128]{2,1,0:T(8,128)(2,1)S(1)}, u32[]{:S(2)}) %copy-start) | copy-done | bytes 1572888
  68.4 1.7 %collective-permute-done.6.refs_0_ = bf16[1024,128]{1,0:T(8,128)(2,1)S(1)} collective-permute-done((bf16[1024,128]{1,0:T(8,128)(2,1)}, bf16[1024,128]{1,0:T(8,128)(2,1)S(1)}, u32[]{:S(2)}, u32[]{:S(2)}) %collective-permute-start.6) | collective-permute-done | bytes 262176 | tf_op jit(solution)/shard_map/r_send/ppermute | solution.py:311
  70.1 0.7 copy-done.5
  70.9 3.2 %new_weights.1 = (bf16[1024,128]{1,0:T(8,128)(2,1)}, bf16[1024,128]{1,0:T(8,128)(2,1)}) custom-call(bf16[3,2048,128]{2,1,0:T(8,128)(2,1)} %copy-done, bf16[2048,128]{1,0:T(8,128)(2,1)} %get-tuple-element.73.mine_ref, bf16[1024,128]{1,0:T(8,128)(2,1)} %copy-done.5, bf16[1024,128]{1,0:T(8,128)(2,1)} %copy-done.4, ...), custom_call_target="tpu_custom_call" | custom-call | tf_op jit(solution)/shard_map/new_weights/pallas_call | solution.py:198
  74.1 2.4 %collective-permute-start.12 = (bf16[1024,128]{1,0:T(8,128)(2,1)}, bf16[1024,128]{1,0:T(8,128)(2,1)S(1)}, u32[]{:S(2)}, u32[]{:S(2)}) collective-permute-start(bf16[1024,128]{1,0:T(8,128)(2,1)} %get-tuple-element.70.refs_4_), channel_id=1, source_target_pairs={{0,1},{1,0},{2,3},{3,2},{4,5},{5,4},{6,7},{7,6},{8,9},{9,8},{10,11... | collective-permute-start | bytes 786440 | tf_op jit(solution)/shard_map/g_sib_lo/ppermute | solution.py:311
  76.5 2.7 %collective-permute-start.11 = (bf16[1024,128]{1,0:T(8,128)(2,1)}, bf16[1024,128]{1,0:T(8,128)(2,1)S(1)}, u32[]{:S(2)}, u32[]{:S(2)}) collective-permute-start(bf16[1024,128]{1,0:T(8,128)(2,1)} %get-tuple-element.71.refs_5_), channel_id=1, source_target_pairs={{0,6},{1,7},{2,0},{3,1},{4,2},{5,3},{6,4},{7,5},{8,14},{9,15},{10,... | collective-permute-start | bytes 786440 | tf_op jit(solution)/shard_map/g_dn_hi/ppermute | solution.py:311
  79.2 1.4 %collective-permute-start.14 = (bf16[1024,128]{1,0:T(8,128)(2,1)}, bf16[1024,128]{1,0:T(8,128)(2,1)S(1)}, u32[]{:S(2)}, u32[]{:S(2)}) collective-permute-start(bf16[1024,128]{1,0:T(8,128)(2,1)} %get-tuple-element.70.refs_4_), channel_id=1, source_target_pairs={{0,6},{1,7},{2,0},{3,1},{4,2},{5,3},{6,4},{7,5},{8,14},{9,15},{10,... | collective-permute-start | bytes 786440 | tf_op jit(solution)/shard_map/g_dn_lo/ppermute | solution.py:311
  80.5 0.9 collective-permute-start.15
  81.6 4.6 %adam.1 = (bf16[16384,128]{1,0:T(8,128)(2,1)}, f32[2048,128]{1,0:T(8,128)}, bf16[2048,128]{1,0:T(8,128)(2,1)}, bf16[2048,128]{1,0:T(8,128)(2,1)}, bf16[1,128]{1,0:T(2,128)(2,1)}, /*index=5*/bf16[1,128]{1,0:T(2,128)(2,1)}) custom-call(bf16[3,2048,128]{2,1,0:T(8,128)(2,1)} %copy-done, bf16[2048,128]{1,0:T(8,128)(2,1)} %get-tuple-element.73.mine_ref, ...), custom_call_target="tpu_custom_call" | custom-call | bytes 16777216 | tf_op jit(solution)/shard_map/adam/pallas_call | solution.py:266
  86.5 2.4 %collective-permute-start.17 = (bf16[1024,128]{1,0:T(8,128)(2,1)S(1)}, bf16[1024,128]{1,0:T(8,128)(2,1)S(1)}, u32[]{:S(2)}, u32[]{:S(2)}) collective-permute-start(bf16[1024,128]{1,0:T(8,128)(2,1)S(1)} %collective-permute-done.11.refs_1_), channel_id=1, source_target_pairs={{0,6},{1,7},{2,0},{3,1},{4,2},{5,3},{6,4},{7,5},{8,14},{9,15},{10,... | collective-permute-start | bytes 786440 | tf_op jit(solution)/shard_map/g_opp_hi/ppermute | solution.py:311
  88.9 1.5 %collective-permute-done.14.refs_3_ = bf16[1024,128]{1,0:T(8,128)(2,1)S(1)} collective-permute-done((bf16[1024,128]{1,0:T(8,128)(2,1)}, bf16[1024,128]{1,0:T(8,128)(2,1)S(1)}, u32[]{:S(2)}, u32[]{:S(2)}) %collective-permute-start.14) | collective-permute-done | bytes 262176 | tf_op jit(solution)/shard_map/g_dn_lo/ppermute | solution.py:311
  90.5 2.0 %collective-permute-start.22 = (bf16[1024,128]{1,0:T(8,128)(2,1)S(1)}, bf16[1024,128]{1,0:T(8,128)(2,1)S(1)}, u32[]{:S(2)}, u32[]{:S(2)}) collective-permute-start(bf16[1024,128]{1,0:T(8,128)(2,1)S(1)} %collective-permute-done.10.refs_0_), channel_id=1, source_target_pairs={{0,1},{1,0},{2,3},{3,2},{4,5},{5,4},{6,7},{7,6},{8,9},{9,8},{10,11... | collective-permute-start | bytes 786440 | tf_op jit(solution)/shard_map/g_sib_up_lo/ppermute | solution.py:311
  92.4 1.4 %join.2.refs_8_ = bf16[16384,128]{1,0:T(8,128)(2,1)} custom-call(bf16[1024,128]{1,0:T(8,128)(2,1)S(1)} %collective-permute-done.10.refs_0_, bf16[1024,128]{1,0:T(8,128)(2,1)S(1)} %collective-permute-done.11.refs_1_, bf16[1024,128]{1,0:T(8,128)(2,1)S(1)} %collective-permute-done.13.refs_2_, ...), custom_call_target="tpu_custom_call", output_to_operand_aliasing={{}: (6, {})} | custom-call | tf_op jit(solution)/shard_map/join/pallas_call | solution.py:436
  93.8 3.2 %collective-permute-done.16.refs_0_ = bf16[1024,128]{1,0:T(8,128)(2,1)S(1)} collective-permute-done((bf16[1024,128]{1,0:T(8,128)(2,1)S(1)}, bf16[1024,128]{1,0:T(8,128)(2,1)S(1)}, u32[]{:S(2)}, u32[]{:S(2)}) %collective-permute-start.16) | collective-permute-done | bytes 262176 | tf_op jit(solution)/shard_map/g_opp_lo/ppermute | solution.py:311
  97.0 0.9 collective-permute-start.20
  100.2 1.6 %join.3 = bf16[16384,128]{1,0:T(8,128)(2,1)} custom-call(bf16[1024,128]{1,0:T(8,128)(2,1)S(1)} %collective-permute-done.16.refs_0_, bf16[1024,128]{1,0:T(8,128)(2,1)S(1)} %collective-permute-done.17.refs_1_, bf16[1024,128]{1,0:T(8,128)(2,1)S(1)} %collective-permute-done.18.refs_2_, ...), custom_call_target="tpu_custom_call", output_to_operand_aliasing={{}: (8, {})} | custom-call | tf_op jit(solution)/shard_map/join/pallas_call | solution.py:436
  (47 shorter events, 4.7 us)
Async XLA Ops:
  5.3 54.7 %all-to-all-start = ((bf16[128,96,128]{2,1,0:T(8,128)(2,1)}), bf16[128,96,128]{2,1,0:T(8,128)(2,1)S(1)}, u32[]{:S(2)}, u32[]{:S(2)}) async-start(bf16[128,96,128]{2,1,0:T(8,128)(2,1)} %bitcast.51), calls=%async_computation | async-start | bytes 6291456 | tf_op jit(solution)/shard_map/all_to_all | solution.py:487
  19.3 4.2 %collective-permute-start = (bf16[2048,128]{1,0:T(8,128)(2,1)}, bf16[2048,128]{1,0:T(8,128)(2,1)S(1)}, u32[]{:S(2)}, u32[]{:S(2)}) collective-permute-start(bf16[2048,128]{1,0:T(8,128)(2,1)} %get-tuple-element.52), channel_id=1, source_target_pairs={{0,1},{1,0},{2,3},{3,2},{4,5},{5,4},{6,7},{7,6},{8,9},{9,8},{10,11... | collective-permute-start | bytes 1572872 | tf_op jit(solution)/shard_map/r_send/ppermute | solution.py:311
  20.4 3.0 %collective-permute-start.1 = (bf16[2048,128]{1,0:T(8,128)(2,1)}, bf16[2048,128]{1,0:T(8,128)(2,1)S(1)}, u32[]{:S(2)}, u32[]{:S(2)}) collective-permute-start(bf16[2048,128]{1,0:T(8,128)(2,1)} %get-tuple-element.54), channel_id=1, source_target_pairs={{0,1},{1,0},{2,3},{3,2},{4,5},{5,4},{6,7},{7,6},{8,9},{9,8},{10,11... | collective-permute-start | bytes 1572872 | tf_op jit(solution)/shard_map/r_send/ppermute | solution.py:311
  20.5 3.2 %collective-permute-start.2 = (bf16[2048,128]{1,0:T(8,128)(2,1)}, bf16[2048,128]{1,0:T(8,128)(2,1)S(1)}, u32[]{:S(2)}, u32[]{:S(2)}) collective-permute-start(bf16[2048,128]{1,0:T(8,128)(2,1)} %get-tuple-element.56), channel_id=1, source_target_pairs={{0,1},{1,0},{2,3},{3,2},{4,5},{5,4},{6,7},{7,6},{8,9},{9,8},{10,11... | collective-permute-start | bytes 1572872 | tf_op jit(solution)/shard_map/r_send/ppermute | solution.py:311
  20.9 3.5 %collective-permute-start.3 = (bf16[2048,128]{1,0:T(8,128)(2,1)}, bf16[2048,128]{1,0:T(8,128)(2,1)S(1)}, u32[]{:S(2)}, u32[]{:S(2)}) collective-permute-start(bf16[2048,128]{1,0:T(8,128)(2,1)} %get-tuple-element.58), channel_id=1, source_target_pairs={{0,1},{1,0},{2,3},{3,2},{4,5},{5,4},{6,7},{7,6},{8,9},{9,8},{10,11... | collective-permute-start | bytes 1572872 | tf_op jit(solution)/shard_map/r_send/ppermute | solution.py:311
  23.4 1.0 copy-start.3
  23.5 1.0 copy-start.1
  23.7 0.9 copy-start.2
  24.4 0.8 copy-start.7
  28.1 32.0 %collective-permute-start.4 = (bf16[1024,128]{1,0:T(8,128)(2,1)}, bf16[1024,128]{1,0:T(8,128)(2,1)}, u32[]{:S(2)}, u32[]{:S(2)}) collective-permute-start(bf16[1024,128]{1,0:T(8,128)(2,1)} %get-tuple-element.59), channel_id=1, source_target_pairs={{0,2},{1,3},{2,4},{3,5},{4,6},{5,7},{6,0},{7,1},{8,10},{9,11},{10,... | collective-permute-start | bytes 786440 | tf_op jit(solution)/shard_map/r_send/ppermute | solution.py:311
  28.8 31.2 %collective-permute-start.5 = (bf16[1024,128]{1,0:T(8,128)(2,1)}, bf16[1024,128]{1,0:T(8,128)(2,1)}, u32[]{:S(2)}, u32[]{:S(2)}) collective-permute-start(bf16[1024,128]{1,0:T(8,128)(2,1)} %get-tuple-element.60), channel_id=1, source_target_pairs={{0,6},{1,7},{2,0},{3,1},{4,2},{5,3},{6,4},{7,5},{8,14},{9,15},{10,... | collective-permute-start | bytes 786440 | tf_op jit(solution)/shard_map/r_send/ppermute | solution.py:311
  31.6 36.9 %collective-permute-start.7 = (bf16[1024,128]{1,0:T(8,128)(2,1)}, bf16[1024,128]{1,0:T(8,128)(2,1)S(1)}, u32[]{:S(2)}, u32[]{:S(2)}) collective-permute-start(bf16[1024,128]{1,0:T(8,128)(2,1)} %get-tuple-element.67), channel_id=1, source_target_pairs={{0,2},{1,3},{2,4},{3,5},{4,6},{5,7},{6,0},{7,1},{8,10},{9,11},{10,... | collective-permute-start | bytes 786440 | tf_op jit(solution)/shard_map/r_send/ppermute | solution.py:311
  31.6 36.8 %collective-permute-start.8 = (bf16[1024,128]{1,0:T(8,128)(2,1)}, bf16[1024,128]{1,0:T(8,128)(2,1)}, u32[]{:S(2)}, u32[]{:S(2)}) collective-permute-start(bf16[1024,128]{1,0:T(8,128)(2,1)} %get-tuple-element.68), channel_id=1, source_target_pairs={{0,6},{1,7},{2,0},{3,1},{4,2},{5,3},{6,4},{7,5},{8,14},{9,15},{10,... | collective-permute-start | bytes 786440 | tf_op jit(solution)/shard_map/r_send/ppermute | solution.py:311
  62.2 7.9 %collective-permute-start.6 = (bf16[1024,128]{1,0:T(8,128)(2,1)}, bf16[1024,128]{1,0:T(8,128)(2,1)S(1)}, u32[]{:S(2)}, u32[]{:S(2)}) collective-permute-start(bf16[1024,128]{1,0:T(8,128)(2,1)} %get-tuple-element.66), channel_id=1, source_target_pairs={{0,2},{1,3},{2,4},{3,5},{4,6},{5,7},{6,0},{7,1},{8,10},{9,11},{10,... | collective-permute-start | bytes 786440 | tf_op jit(solution)/shard_map/r_send/ppermute | solution.py:311
  62.3 7.9 %collective-permute-start.9 = (bf16[1024,128]{1,0:T(8,128)(2,1)}, bf16[1024,128]{1,0:T(8,128)(2,1)S(1)}, u32[]{:S(2)}, u32[]{:S(2)}) collective-permute-start(bf16[1024,128]{1,0:T(8,128)(2,1)} %get-tuple-element.69), channel_id=1, source_target_pairs={{0,6},{1,7},{2,0},{3,1},{4,2},{5,3},{6,4},{7,5},{8,14},{9,15},{10,... | collective-permute-start | bytes 786440 | tf_op jit(solution)/shard_map/r_send/ppermute | solution.py:311
  67.2 1.2 %copy-start = (bf16[3,2048,128]{2,1,0:T(8,128)(2,1)}, bf16[3,2048,128]{2,1,0:T(8,128)(2,1)S(1)}, u32[]{:S(2)}) copy-start(bf16[3,2048,128]{2,1,0:T(8,128)(2,1)S(1)} %unpack.1.old_ref) | copy-start | bytes 4718596
  68.4 1.7 %copy-start.4 = (bf16[1024,128]{1,0:T(8,128)(2,1)}, bf16[1024,128]{1,0:T(8,128)(2,1)S(1)}, u32[]{:S(2)}) copy-start(bf16[1024,128]{1,0:T(8,128)(2,1)S(1)} %collective-permute-done.7.refs_1_) | copy-start | bytes 786436
  70.1 0.8 copy-start.6
  74.1 7.3 %collective-permute-start.12 = (bf16[1024,128]{1,0:T(8,128)(2,1)}, bf16[1024,128]{1,0:T(8,128)(2,1)S(1)}, u32[]{:S(2)}, u32[]{:S(2)}) collective-permute-start(bf16[1024,128]{1,0:T(8,128)(2,1)} %get-tuple-element.70.refs_4_), channel_id=1, source_target_pairs={{0,1},{1,0},{2,3},{3,2},{4,5},{5,4},{6,7},{7,6},{8,9},{9,8},{10,11... | collective-permute-start | bytes 786440 | tf_op jit(solution)/shard_map/g_sib_lo/ppermute | solution.py:311
  76.5 9.7 %collective-permute-start.10 = (bf16[1024,128]{1,0:T(8,128)(2,1)}, bf16[1024,128]{1,0:T(8,128)(2,1)S(1)}, u32[]{:S(2)}, u32[]{:S(2)}) collective-permute-start(bf16[1024,128]{1,0:T(8,128)(2,1)} %get-tuple-element.70.refs_4_), channel_id=1, source_target_pairs={{0,2},{1,3},{2,4},{3,5},{4,6},{5,7},{6,0},{7,1},{8,10},{9,11},{10,... | collective-permute-start | bytes 786440 | tf_op jit(solution)/shard_map/g_up_lo/ppermute | solution.py:311
  76.5 9.7 %collective-permute-start.11 = (bf16[1024,128]{1,0:T(8,128)(2,1)}, bf16[1024,128]{1,0:T(8,128)(2,1)S(1)}, u32[]{:S(2)}, u32[]{:S(2)}) collective-permute-start(bf16[1024,128]{1,0:T(8,128)(2,1)} %get-tuple-element.71.refs_5_), channel_id=1, source_target_pairs={{0,6},{1,7},{2,0},{3,1},{4,2},{5,3},{6,4},{7,5},{8,14},{9,15},{10,... | collective-permute-start | bytes 786440 | tf_op jit(solution)/shard_map/g_dn_hi/ppermute | solution.py:311
  79.2 11.3 %collective-permute-start.14 = (bf16[1024,128]{1,0:T(8,128)(2,1)}, bf16[1024,128]{1,0:T(8,128)(2,1)S(1)}, u32[]{:S(2)}, u32[]{:S(2)}) collective-permute-start(bf16[1024,128]{1,0:T(8,128)(2,1)} %get-tuple-element.70.refs_4_), channel_id=1, source_target_pairs={{0,6},{1,7},{2,0},{3,1},{4,2},{5,3},{6,4},{7,5},{8,14},{9,15},{10,... | collective-permute-start | bytes 786440 | tf_op jit(solution)/shard_map/g_dn_lo/ppermute | solution.py:311
  80.5 11.9 %collective-permute-start.15 = (bf16[1024,128]{1,0:T(8,128)(2,1)}, bf16[1024,128]{1,0:T(8,128)(2,1)S(1)}, u32[]{:S(2)}, u32[]{:S(2)}) collective-permute-start(bf16[1024,128]{1,0:T(8,128)(2,1)} %get-tuple-element.71.refs_5_), channel_id=1, source_target_pairs={{0,1},{1,0},{2,3},{3,2},{4,5},{5,4},{6,7},{7,6},{8,9},{9,8},{10,11... | collective-permute-start | bytes 786440 | tf_op jit(solution)/shard_map/g_sib_hi/ppermute | solution.py:311
  81.5 11.0 %collective-permute-start.13 = (bf16[1024,128]{1,0:T(8,128)(2,1)}, bf16[1024,128]{1,0:T(8,128)(2,1)S(1)}, u32[]{:S(2)}, u32[]{:S(2)}) collective-permute-start(bf16[1024,128]{1,0:T(8,128)(2,1)} %get-tuple-element.71.refs_5_), channel_id=1, source_target_pairs={{0,2},{1,3},{2,4},{3,5},{4,6},{5,7},{6,0},{7,1},{8,10},{9,11},{10,... | collective-permute-start | bytes 786440 | tf_op jit(solution)/shard_map/g_up_hi/ppermute | solution.py:311
  86.2 10.8 %collective-permute-start.16 = (bf16[1024,128]{1,0:T(8,128)(2,1)S(1)}, bf16[1024,128]{1,0:T(8,128)(2,1)S(1)}, u32[]{:S(2)}, u32[]{:S(2)}) collective-permute-start(bf16[1024,128]{1,0:T(8,128)(2,1)S(1)} %collective-permute-done.10.refs_0_), channel_id=1, source_target_pairs={{0,2},{1,3},{2,4},{3,5},{4,6},{5,7},{6,0},{7,1},{8,10},{9,11},{10,... | collective-permute-start | bytes 786440 | tf_op jit(solution)/shard_map/g_opp_lo/ppermute | solution.py:311
  86.5 10.5 %collective-permute-start.17 = (bf16[1024,128]{1,0:T(8,128)(2,1)S(1)}, bf16[1024,128]{1,0:T(8,128)(2,1)S(1)}, u32[]{:S(2)}, u32[]{:S(2)}) collective-permute-start(bf16[1024,128]{1,0:T(8,128)(2,1)S(1)} %collective-permute-done.11.refs_1_), channel_id=1, source_target_pairs={{0,6},{1,7},{2,0},{3,1},{4,2},{5,3},{6,4},{7,5},{8,14},{9,15},{10,... | collective-permute-start | bytes 786440 | tf_op jit(solution)/shard_map/g_opp_hi/ppermute | solution.py:311
  90.5 7.9 %collective-permute-start.22 = (bf16[1024,128]{1,0:T(8,128)(2,1)S(1)}, bf16[1024,128]{1,0:T(8,128)(2,1)S(1)}, u32[]{:S(2)}, u32[]{:S(2)}) collective-permute-start(bf16[1024,128]{1,0:T(8,128)(2,1)S(1)} %collective-permute-done.10.refs_0_), channel_id=1, source_target_pairs={{0,1},{1,0},{2,3},{3,2},{4,5},{5,4},{6,7},{7,6},{8,9},{9,8},{10,11... | collective-permute-start | bytes 786440 | tf_op jit(solution)/shard_map/g_sib_up_lo/ppermute | solution.py:311
  92.4 6.0 %collective-permute-start.23 = (bf16[1024,128]{1,0:T(8,128)(2,1)S(1)}, bf16[1024,128]{1,0:T(8,128)(2,1)S(1)}, u32[]{:S(2)}, u32[]{:S(2)}) collective-permute-start(bf16[1024,128]{1,0:T(8,128)(2,1)S(1)} %collective-permute-done.11.refs_1_), channel_id=1, source_target_pairs={{0,1},{1,0},{2,3},{3,2},{4,5},{5,4},{6,7},{7,6},{8,9},{9,8},{10,11... | collective-permute-start | bytes 786440 | tf_op jit(solution)/shard_map/g_sib_dn_hi/ppermute | solution.py:311
  97.0 2.0 %collective-permute-start.20 = (bf16[1024,128]{1,0:T(8,128)(2,1)S(1)}, bf16[1024,128]{1,0:T(8,128)(2,1)S(1)}, u32[]{:S(2)}, u32[]{:S(2)}) collective-permute-start(bf16[1024,128]{1,0:T(8,128)(2,1)S(1)} %collective-permute-done.13.refs_2_), channel_id=1, source_target_pairs={{0,1},{1,0},{2,3},{3,2},{4,5},{5,4},{6,7},{7,6},{8,9},{9,8},{10,11... | collective-permute-start | bytes 786440 | tf_op jit(solution)/shard_map/g_sib_up_hi/ppermute | solution.py:311
  97.9 1.5 %collective-permute-start.21 = (bf16[1024,128]{1,0:T(8,128)(2,1)S(1)}, bf16[1024,128]{1,0:T(8,128)(2,1)S(1)}, u32[]{:S(2)}, u32[]{:S(2)}) collective-permute-start(bf16[1024,128]{1,0:T(8,128)(2,1)S(1)} %collective-permute-done.14.refs_3_), channel_id=1, source_target_pairs={{0,1},{1,0},{2,3},{3,2},{4,5},{5,4},{6,7},{7,6},{8,9},{9,8},{10,11... | collective-permute-start | bytes 786440 | tf_op jit(solution)/shard_map/g_sib_dn_lo/ppermute | solution.py:311
  97.9 1.9 %collective-permute-start.18 = (bf16[1024,128]{1,0:T(8,128)(2,1)S(1)}, bf16[1024,128]{1,0:T(8,128)(2,1)S(1)}, u32[]{:S(2)}, u32[]{:S(2)}) collective-permute-start(bf16[1024,128]{1,0:T(8,128)(2,1)S(1)} %collective-permute-done.16.refs_0_), channel_id=1, source_target_pairs={{0,1},{1,0},{2,3},{3,2},{4,5},{5,4},{6,7},{7,6},{8,9},{9,8},{10,11... | collective-permute-start | bytes 786440 | tf_op jit(solution)/shard_map/g_sib_opp_lo/ppermute | solution.py:311
  98.4 1.8 %collective-permute-start.19 = (bf16[1024,128]{1,0:T(8,128)(2,1)S(1)}, bf16[1024,128]{1,0:T(8,128)(2,1)S(1)}, u32[]{:S(2)}, u32[]{:S(2)}) collective-permute-start(bf16[1024,128]{1,0:T(8,128)(2,1)S(1)} %collective-permute-done.17.refs_1_), channel_id=1, source_target_pairs={{0,1},{1,0},{2,3},{3,2},{4,5},{5,4},{6,7},{7,6},{8,9},{9,8},{10,11... | collective-permute-start | bytes 786440 | tf_op jit(solution)/shard_map/g_sib_opp_hi/ppermute | solution.py:311
  (1 other events, 0.7 us)

commit v5 on v4

--- a/solution.py
+++ b/solution.py
@@ -13,6 +13,7 @@
 RING = 4
 CORES = 2
 ADDENDS = 3
+STRIP = 32
 
 
 def to_tiles(values):
@@ -50,7 +51,11 @@
 def pack_kernel(rows, chunks, map_ref, mscale_ref, sscale_ref, master_ref, mean_ref, square_ref, out_ref, *scratch):
     held_map, master, mean, square, wide_mean, wide_square, slots, mscale, sscale, slot_of, mscale_of, sscale_of = scratch[:12]
     load_sems, table_sems = scratch[12:]
-    pairs = [(map_ref, held_map), (mean_ref, mean), (square_ref, square), (master_ref, master)]
+    part = rows * chunks // 2
+    pairs = [(map_ref, held_map)]
+    for h in range(2):
+        here = pl.ds(h * part, part)
+        pairs += [(ref.at[here], room.at[here]) for ref, room in ((mean_ref, mean), (square_ref, square), (master_ref, master))]
     loads = [pltpu.make_async_copy(ref, room, load_sems.at[k]) for k, (ref, room) in enumerate(pairs)]
     for load in loads:
         load.start()
@@ -62,14 +67,18 @@
     tables = [pltpu.make_async_copy(table, room, table_sems.at[k]) for k, (table, room) in enumerate(tables)]
     for table in tables:
         table.start()
-    loads[1].wait()
-    wide_mean[...] = mean[...].astype(jnp.float32)
-    loads[2].wait()
-    wide_square[...] = square[...].astype(jnp.float32)
-    for table in tables:
-        table.wait()
-    loads[3].wait()
     for row in range(rows):
+        if row % (rows // 2) == 0:
+            first = 1 + 3 * (row * 2 // rows)
+            here = pl.ds(row * chunks, part)
+            loads[first].wait()
+            wide_mean[here, :] = mean[here, :].astype(jnp.float32)
+            loads[first + 1].wait()
+            wide_square[here, :] = square[here, :].astype(jnp.float32)
+            loads[first + 2].wait()
+        if row == 0:
+            for table in tables:
+                table.wait()
         base = (row // SUB) * chunks * SUB + row % SUB
         spots = pl.ds(base, chunks, stride=SUB)
         slot = slot_of[0, row]
@@ -104,7 +113,7 @@
             pltpu.SMEM((1, rows), i32),
             pltpu.SMEM((1, rows), f32),
             pltpu.SMEM((1, rows), f32),
-            pltpu.SemaphoreType.DMA((4,)),
+            pltpu.SemaphoreType.DMA((7,)),
             pltpu.SemaphoreType.DMA((3,)),
         ],
         compiler_params=pltpu.CompilerParams(vmem_limit_bytes=56 * 1024 * 1024),
@@ -160,54 +169,36 @@
     return loads
 
 
-def step_values(old, addends, there):
-    gradient = addends[0, there, :].astype(jnp.float32)
-    for k in range(1, ADDENDS):
-        gradient += addends[k, there, :].astype(jnp.float32)
-    weight_old, mean_old, square_old = (old[k, there, :].astype(jnp.float32) for k in range(3))
+def step_values(old, gradient):
+    weight_old, mean_old, square_old = (x.astype(jnp.float32) for x in old)
     mean_next = 0.9 * mean_old + 0.1 * gradient
     square_next = 0.95 * square_old + 0.05 * gradient * gradient
-    master = weight_old - 0.05 * (mean_next / (jnp.sqrt(square_next) + 1e-08) + 0.1 * weight_old)
+    root = square_next * lax.rsqrt(square_next)
+    master = weight_old - 0.05 * (mean_next / (root + 1e-08) + 0.1 * weight_old)
     return mean_next, square_next, master
 
 
-def weights_kernel(rows, chunks, old_ref, mine_ref, *refs):
-    side_refs, out_refs = refs[:4], refs[4:6]
-    old, addends, weights, sems, out_sems = refs[6:]
-    span = chunks * SUB
-    groups = rows // SUB
-    half = groups // 2 * span
-    loads = start_loads(half, old_ref, mine_ref, side_refs, old, addends, sems)
-    stores = []
+def weights_kernel(old_ref, mine_ref, *refs):
+    side_refs, out_refs = refs[:4], refs[4:]
+    half = out_refs[0].shape[0]
     for h in range(2):
-        for load in loads[h]:
-            load.wait()
-        for group in range(h * groups // 2, (h + 1) * groups // 2):
-            there = pl.ds(group * span, span)
-            weights[there, :] = step_values(old, addends, there)[2].astype(weights.dtype)
-        stores.append(pltpu.make_async_copy(weights.at[pl.ds(h * half, half)], out_refs[h], out_sems.at[h]))
-        stores[h].start()
-    for store in stores:
-        store.wait()
+        for start in range(0, half, STRIP):
+            there, inside = pl.ds(h * half + start, STRIP), pl.ds(start, STRIP)
+            gradient = mine_ref[there, :].astype(jnp.float32)
+            for side in range(2):
+                gradient += side_refs[2 * side + h][inside, :].astype(jnp.float32)
+            master = step_values([old_ref[k, there, :] for k in range(3)], gradient)[2]
+            out_refs[h][inside, :] = master.astype(out_refs[h].dtype)
 
 
 def new_weights(old, addends, rows, chunks):
-    flat = (rows * chunks, LANES)
-    bf16 = jnp.bfloat16
-    hbm = pl.BlockSpec(memory_space=pl.ANY)
-    return pl.pallas_call(
-        functools.partial(weights_kernel, rows, chunks),
-        out_shape=[jax.ShapeDtypeStruct((flat[0] // 2, LANES), bf16)] * 2,
-        in_specs=[hbm] * 6,
-        out_specs=[hbm] * 2,
-        scratch_shapes=[
-            pltpu.VMEM((3, *flat), bf16),
-            pltpu.VMEM((ADDENDS, *flat), bf16),
-            pltpu.VMEM(flat, bf16),
-            pltpu.SemaphoreType.DMA((2, 3 + ADDENDS)),
-            pltpu.SemaphoreType.DMA((2,)),
-        ],
-        compiler_params=pltpu.CompilerParams(vmem_limit_bytes=56 * 1024 * 1024),
+    vmem = pl.BlockSpec(memory_space=pltpu.VMEM)
+    return pl.pallas_call(
+        weights_kernel,
+        out_shape=[jax.ShapeDtypeStruct((rows * chunks // 2, LANES), jnp.bfloat16)] * 2,
+        in_specs=[vmem] * 6,
+        out_specs=[vmem] * 2,
+        compiler_params=pltpu.CompilerParams(vmem_limit_bytes=12 * 1024 * 1024),
         name="new_weights",
     )(old, *addends)
 
@@ -240,7 +231,10 @@
             fetches[h].wait()
             stores[h].start()
         there = pl.ds(group * span, span)
-        mean_next, square_next, master = step_values(old, addends, there)
+        gradient = addends[0, there, :].astype(jnp.float32)
+        for k in range(1, ADDENDS):
+            gradient += addends[k, there, :].astype(jnp.float32)
+        mean_next, square_next, master = step_values([old[k, there, :] for k in range(3)], gradient)
         master_ref[there, :] = master
         mean_next = mean_next.reshape(chunks, SUB, LANES)
         square_next = square_next.reshape(chunks, SUB, LANES)
@@ -412,39 +406,30 @@
 
 
 def join_kernel(span, starts, *refs):
-    parts, (out_ref, *rooms, in_sems, sems) = refs[: len(starts)], refs[-3 - len(starts) :]
+    parts, (out_ref, sems) = refs[: len(starts)], refs[-2:]
     y, core = place()
-    loads = [pltpu.make_async_copy(part, room, in_sems.at[k]) for k, (part, room) in enumerate(zip(parts, rooms))]
-    for load in loads:
-        load.start()
     copies = []
     for k, (step, flip, offset) in enumerate(starts):
         side = CORES - 1 - core if flip else core
         base = pl.multiple_of(shard_at(y, step, side) * span + offset, span // 2)
-        copies.append(pltpu.make_async_copy(rooms[k], out_ref.at[pl.ds(base, parts[k].shape[0])], sems.at[k]))
-    for load, copy in zip(loads, copies):
-        load.wait()
+        copies.append(pltpu.make_async_copy(parts[k], out_ref.at[pl.ds(base, parts[k].shape[0])], sems.at[k]))
+    for copy in copies:
         copy.start()
     for copy in copies:
         copy.wait()
 
 
-def join(span, starts, parts, whole=None):
-    lanes = parts[0].shape[1]
-    hbm = pl.BlockSpec(memory_space=pl.ANY)
-    given = list(parts) + ([] if whole is None else [whole])
+def join(span, starts, parts, whole):
     return pl.pallas_call(
         functools.partial(join_kernel, span, starts),
-        out_shape=jax.ShapeDtypeStruct((RING * CORES * span, lanes), parts[0].dtype),
-        in_specs=[hbm] * len(given),
-        out_specs=hbm,
-        scratch_shapes=[pltpu.VMEM(part.shape, part.dtype) for part in parts]
-        + [pltpu.SemaphoreType.DMA((len(parts),))] * 2,
-        compiler_params=pltpu.CompilerParams(vmem_limit_bytes=16 * 1024 * 1024),
-        input_output_aliases={} if whole is None else {len(parts): 0},
-        cost_estimate=pl.CostEstimate(flops=0, transcendentals=0, bytes_accessed=0),
+        out_shape=jax.ShapeDtypeStruct(whole.shape, whole.dtype),
+        in_specs=[pl.BlockSpec(memory_space=pltpu.VMEM)] * len(parts) + [pl.BlockSpec(memory_space=pl.ANY)],
+        out_specs=pl.BlockSpec(memory_space=pl.ANY),
+        scratch_shapes=[pltpu.SemaphoreType.DMA((len(parts),))],
+        compiler_params=pltpu.CompilerParams(vmem_limit_bytes=8 * 1024 * 1024),
+        input_output_aliases={len(parts): 0},
         name="join",
-    )(*given)
+    )(*parts, whole)
 
 
 def gather_shards(lo, hi, run_between):

time: 102 us -> 100 us (0.980)
  local copies, waits for them, and re-layouts: 2.76 us -> 0.83 us
  Pallas kernels: 26.6 us -> 25.2 us
  waiting for transfers between devices: 34.9 us -> 36 us
    unnamed x16 -> x22, local copies, waits for them, and re-layouts: 2.76 us -> 0.83 us
    pallas_call x1, Pallas kernels: 3.2 us -> 1.98 us  [new_weights(): pl.pallas_call(weights_kernel, out_shape=[jax.ShapeDtypeStruct((rows * ch...]
    ppermute x24, waiting for transfers between devices: 34.9 us -> 36 us  [send(): return lax.ppermute(values, 'dp', sends(shift, flip))]
where the time goes in v5:
time: 100 us; the launch traced here: 99.5 us
  waiting for transfers between devices  36 us (36%)
  starting transfers between devices  34.9 us (35%)
  Pallas kernels  25.2 us (25%)
  other arithmetic  1.71 us (2%)
    ppermute x24, waiting for transfers between devices, send(): return lax.ppermute(values, 'dp', sends(shift, flip))  36 us
    ppermute x24, starting transfers between devices, send(): return lax.ppermute(values, 'dp', sends(shift, flip))  23.4 us
    all_to_all x1, starting transfers between devices, local(): lax.all_to_all(packed.reshape(count_all, peer_cap * 3 * chunks, LANES), A...  11.5 us
    pallas_call x2, Pallas kernels, add(): pl.pallas_call(functools.partial(add_kernel, windows, order), out_shape=[...  5.08 us
    pallas_call x2, Pallas kernels, cut(): pl.pallas_call(functools.partial(cut_kernel, shards), out_shape=[jax.Shap...  4.91 us
    pallas_call x1, Pallas kernels, pack(): pl.pallas_call(functools.partial(pack_kernel, rows, chunks), out_shape=ja...  4.76 us
    pallas_call x1, Pallas kernels, adam(): pl.pallas_call(functools.partial(adam_kernel, rows, chunks), out_shape=[j...  4.51 us
    pallas_call x2, Pallas kernels, join(): pl.pallas_call(functools.partial(join_kernel, span, starts), out_shape=ja...  2.58 us
  transfers between devices with their start and end apart: 25, of which 10 were waited for; matrix products, arithmetic and copies ran while one was open for 2% of the time, Pallas kernels for 17%

profile of v5, /device:TPU:1, one launch (start us, length us, event | category | flops | bytes accessed | tf_op | source)
XLA Modules:
  0.0 99.5 jit_solution(7140962144581607645)
XLA Ops:
  0.6 4.8 %pack.1 = bf16[256,48,128]{2,1,0:T(8,128)(2,1)} custom-call(s32[128,128]{1,0:T(8,128)} %bitcast.55, bf16[1,128]{1,0:T(2,128)(2,1)} %bitcast.56, bf16[1,128]{1,0:T(2,128)(2,1)} %bitcast.57, f32[2048,128]{1,0:T(8,128)} %bitcast.52, bf16[2048,128]{1,0:T(8,128)(2,1)} %bitcast.53, bf16[2048,128]{1,0:T(8,128)(2,1)} %bitcast.54), custom_call_target="tpu_custom_call" | custom-call | tf_op jit(solution)/shard_map/pack/pallas_call | solution.py:98
  5.4 11.5 %all-to-all-start = ((bf16[128,96,128]{2,1,0:T(8,128)(2,1)}), bf16[128,96,128]{2,1,0:T(8,128)(2,1)S(1)}, u32[]{:S(2)}, u32[]{:S(2)}) async-start(bf16[128,96,128]{2,1,0:T(8,128)(2,1)} %bitcast.51), calls=%async_computation | async-start | bytes 6291456 | tf_op jit(solution)/shard_map/all_to_all | solution.py:472
  16.9 2.5 %cut.3 = (bf16[2048,128]{1,0:T(8,128)(2,1)}, bf16[2048,128]{1,0:T(8,128)(2,1)}, bf16[2048,128]{1,0:T(8,128)(2,1)}, bf16[2048,128]{1,0:T(8,128)(2,1)}) custom-call(bf16[8,2048,128]{2,1,0:T(8,128)(2,1)} %bitcast.48), custom_call_target="tpu_custom_call" | custom-call | tf_op jit(solution)/shard_map/cut/pallas_call | solution.py:329
  19.4 1.1 %collective-permute-start = (bf16[2048,128]{1,0:T(8,128)(2,1)}, bf16[2048,128]{1,0:T(8,128)(2,1)S(1)}, u32[]{:S(2)}, u32[]{:S(2)}) collective-permute-start(bf16[2048,128]{1,0:T(8,128)(2,1)} %get-tuple-element.52), channel_id=1, source_target_pairs={{0,1},{1,0},{2,3},{3,2},{4,5},{5,4},{6,7},{7,6},{8,9},{9,8},{10,11... | collective-permute-start | bytes 1572872 | tf_op jit(solution)/shard_map/r_send/ppermute | solution.py:305
  21.2 2.4 %cut.2 = (bf16[2048,128]{1,0:T(8,128)(2,1)}, bf16[2048,128]{1,0:T(8,128)(2,1)}, bf16[2048,128]{1,0:T(8,128)(2,1)}, bf16[2048,128]{1,0:T(8,128)(2,1)}) custom-call(bf16[8,2048,128]{2,1,0:T(8,128)(2,1)} %bitcast.49), custom_call_target="tpu_custom_call" | custom-call | tf_op jit(solution)/shard_map/cut/pallas_call | solution.py:329
  23.8 0.7 collective-permute-done.3.refs_9_
  24.7 0.6 copy-done.10
  25.3 2.9 %add.16 = (bf16[1024,128]{1,0:T(8,128)(2,1)}, bf16[1024,128]{1,0:T(8,128)(2,1)}, bf16[1024,128]{1,0:T(8,128)(2,1)}, bf16[1024,128]{1,0:T(8,128)(2,1)}, bf16[2048,128]{1,0:T(8,128)(2,1)}) custom-call(bf16[2048,128]{1,0:T(8,128)(2,1)} %get-tuple-element.51.refs_0_.refs_2_, bf16[2048,128]{1,0:T(8,128)(2,1)} %copy-done.9, ...), custom_call_target="tpu_custom_call" | custom-call | tf_op jit(solution)/shard_map/add/pallas_call | solution.py:376
  28.2 0.8 collective-permute-start.4
  29.0 2.0 %collective-permute-start.5 = (bf16[1024,128]{1,0:T(8,128)(2,1)}, bf16[1024,128]{1,0:T(8,128)(2,1)}, u32[]{:S(2)}, u32[]{:S(2)}) collective-permute-start(bf16[1024,128]{1,0:T(8,128)(2,1)} %get-tuple-element.60), channel_id=1, source_target_pairs={{0,6},{1,7},{2,0},{3,1},{4,2},{5,3},{6,4},{7,5},{8,14},{9,15},{10,... | collective-permute-start | bytes 786440 | tf_op jit(solution)/shard_map/r_send/ppermute | solution.py:305
  31.0 0.8 and_select_fusion
  31.7 2.7 %collective-permute-start.8 = (bf16[1024,128]{1,0:T(8,128)(2,1)}, bf16[1024,128]{1,0:T(8,128)(2,1)}, u32[]{:S(2)}, u32[]{:S(2)}) collective-permute-start(bf16[1024,128]{1,0:T(8,128)(2,1)} %get-tuple-element.68), channel_id=1, source_target_pairs={{0,6},{1,7},{2,0},{3,1},{4,2},{5,3},{6,4},{7,5},{8,14},{9,15},{10,... | collective-permute-start | bytes 786440 | tf_op jit(solution)/shard_map/r_send/ppermute | solution.py:305
  34.4 25.7 %collective-permute-done.4.refs_2_ = bf16[1024,128]{1,0:T(8,128)(2,1)} collective-permute-done((bf16[1024,128]{1,0:T(8,128)(2,1)}, bf16[1024,128]{1,0:T(8,128)(2,1)}, u32[]{:S(2)}, u32[]{:S(2)}) %collective-permute-start.4) | collective-permute-done | bytes 262176 | tf_op jit(solution)/shard_map/r_send/ppermute | solution.py:305
  60.1 2.2 %add.17 = (bf16[1024,128]{1,0:T(8,128)(2,1)}, bf16[1024,128]{1,0:T(8,128)(2,1)}) custom-call(bf16[2048,128]{1,0:T(8,128)(2,1)} %get-tuple-element.53.refs_4_.refs_0_, bf16[2048,128]{1,0:T(8,128)(2,1)} %copy-done.7, bf16[1024,128]{1,0:T(8,128)(2,1)} %collective-permute-done.4.refs_2_, bf16[2048,128]{1,0:T(8,128)(2,1)} %get-tuple-element.55.refs_6_.refs_3_, ...), custom_call_target="tpu_custom_call" | custom-call | tf_op jit(solution)/shard_map/add/pallas_call | solution.py:376
  62.4 2.7 %collective-permute-start.9 = (bf16[1024,128]{1,0:T(8,128)(2,1)}, bf16[1024,128]{1,0:T(8,128)(2,1)S(1)}, u32[]{:S(2)}, u32[]{:S(2)}) collective-permute-start(bf16[1024,128]{1,0:T(8,128)(2,1)} %get-tuple-element.69), channel_id=1, source_target_pairs={{0,6},{1,7},{2,0},{3,1},{4,2},{5,3},{6,4},{7,5},{8,14},{9,15},{10,... | collective-permute-start | bytes 786440 | tf_op jit(solution)/shard_map/r_send/ppermute | solution.py:305
  65.3 0.8 multiply_add_fusion.slot_ref
  66.1 1.3 %unpack.1.old_ref = bf16[3,2048,128]{2,1,0:T(8,128)(2,1)S(1)} custom-call(s32[128]{0:T(128)S(1)} %multiply_add_fusion.slot_ref, bf16[256,48,128]{2,1,0:T(8,128)(2,1)S(1)} %bitcast.47), custom_call_target="tpu_custom_call" | custom-call | tf_op jit(solution)/shard_map/unpack/pallas_call | solution.py:148
  67.4 2.9 %collective-permute-done.6.refs_0_ = bf16[1024,128]{1,0:T(8,128)(2,1)S(1)} collective-permute-done((bf16[1024,128]{1,0:T(8,128)(2,1)}, bf16[1024,128]{1,0:T(8,128)(2,1)S(1)}, u32[]{:S(2)}, u32[]{:S(2)}) %collective-permute-start.6) | collective-permute-done | bytes 262176 | tf_op jit(solution)/shard_map/r_send/ppermute | solution.py:305
  70.3 2.0 %new_weights.1 = (bf16[1024,128]{1,0:T(8,128)(2,1)S(1)}, bf16[1024,128]{1,0:T(8,128)(2,1)S(1)}) custom-call(bf16[3,2048,128]{2,1,0:T(8,128)(2,1)S(1)} %unpack.1.old_ref, bf16[2048,128]{1,0:T(8,128)(2,1)S(1)} %copy-done.1, bf16[1024,128]{1,0:T(8,128)(2,1)S(1)} %collective-permute-done.6.refs_0_, bf16[1024,128]{1,0:T(8,128)(2,1)S(1)} %collective-permute-done.7.refs_1_, ...), custom_call_target="tpu_custom_call" | custom-call | tf_op jit(solution)/shard_map/new_weights/pallas_call | solution.py:196
  72.3 2.4 %collective-permute-start.12 = (bf16[1024,128]{1,0:T(8,128)(2,1)S(1)}, bf16[1024,128]{1,0:T(8,128)(2,1)S(1)}, u32[]{:S(2)}, u32[]{:S(2)}) collective-permute-start(bf16[1024,128]{1,0:T(8,128)(2,1)S(1)} %get-tuple-element.70.refs_4_), channel_id=1, source_target_pairs={{0,1},{1,0},{2,3},{3,2},{4,5},{5,4},{6,7},{7,6},{8,9},{9,8},{10,11... | collective-permute-start | bytes 786440 | tf_op jit(solution)/shard_map/g_sib_lo/ppermute | solution.py:305
  74.7 2.7 %collective-permute-start.11 = (bf16[1024,128]{1,0:T(8,128)(2,1)S(1)}, bf16[1024,128]{1,0:T(8,128)(2,1)S(1)}, u32[]{:S(2)}, u32[]{:S(2)}) collective-permute-start(bf16[1024,128]{1,0:T(8,128)(2,1)S(1)} %get-tuple-element.71.refs_5_), channel_id=1, source_target_pairs={{0,6},{1,7},{2,0},{3,1},{4,2},{5,3},{6,4},{7,5},{8,14},{9,15},{10,... | collective-permute-start | bytes 786440 | tf_op jit(solution)/shard_map/g_dn_hi/ppermute | solution.py:305
  77.4 1.4 %collective-permute-start.14 = (bf16[1024,128]{1,0:T(8,128)(2,1)S(1)}, bf16[1024,128]{1,0:T(8,128)(2,1)S(1)}, u32[]{:S(2)}, u32[]{:S(2)}) collective-permute-start(bf16[1024,128]{1,0:T(8,128)(2,1)S(1)} %get-tuple-element.70.refs_4_), channel_id=1, source_target_pairs={{0,6},{1,7},{2,0},{3,1},{4,2},{5,3},{6,4},{7,5},{8,14},{9,15},{10,... | collective-permute-start | bytes 786440 | tf_op jit(solution)/shard_map/g_dn_lo/ppermute | solution.py:305
  78.7 0.9 collective-permute-start.15
  79.8 4.5 %adam.1 = (bf16[16384,128]{1,0:T(8,128)(2,1)}, f32[2048,128]{1,0:T(8,128)}, bf16[2048,128]{1,0:T(8,128)(2,1)}, bf16[2048,128]{1,0:T(8,128)(2,1)}, bf16[1,128]{1,0:T(2,128)(2,1)}, /*index=5*/bf16[1,128]{1,0:T(2,128)(2,1)}) custom-call(bf16[3,2048,128]{2,1,0:T(8,128)(2,1)} %copy-done, bf16[2048,128]{1,0:T(8,128)(2,1)} %get-tuple-element.73.mine_ref, ...), custom_call_target="tpu_custom_call" | custom-call | bytes 16777216 | tf_op jit(solution)/shard_map/adam/pallas_call | solution.py:260
  84.5 2.5 %collective-permute-start.17 = (bf16[1024,128]{1,0:T(8,128)(2,1)S(1)}, bf16[1024,128]{1,0:T(8,128)(2,1)S(1)}, u32[]{:S(2)}, u32[]{:S(2)}) collective-permute-start(bf16[1024,128]{1,0:T(8,128)(2,1)S(1)} %collective-permute-done.11.refs_1_), channel_id=1, source_target_pairs={{0,6},{1,7},{2,0},{3,1},{4,2},{5,3},{6,4},{7,5},{8,14},{9,15},{10,... | collective-permute-start | bytes 786440 | tf_op jit(solution)/shard_map/g_opp_hi/ppermute | solution.py:305
  87.1 1.3 %collective-permute-done.14.refs_3_ = bf16[1024,128]{1,0:T(8,128)(2,1)S(1)} collective-permute-done((bf16[1024,128]{1,0:T(8,128)(2,1)S(1)}, bf16[1024,128]{1,0:T(8,128)(2,1)S(1)}, u32[]{:S(2)}, u32[]{:S(2)}) %collective-permute-start.14) | collective-permute-done | bytes 262176 | tf_op jit(solution)/shard_map/g_dn_lo/ppermute | solution.py:305
  88.3 2.0 %collective-permute-start.22 = (bf16[1024,128]{1,0:T(8,128)(2,1)S(1)}, bf16[1024,128]{1,0:T(8,128)(2,1)S(1)}, u32[]{:S(2)}, u32[]{:S(2)}) collective-permute-start(bf16[1024,128]{1,0:T(8,128)(2,1)S(1)} %collective-permute-done.10.refs_0_), channel_id=1, source_target_pairs={{0,1},{1,0},{2,3},{3,2},{4,5},{5,4},{6,7},{7,6},{8,9},{9,8},{10,11... | collective-permute-start | bytes 786440 | tf_op jit(solution)/shard_map/g_sib_up_lo/ppermute | solution.py:305
  90.3 1.2 %join.2.refs_8_ = bf16[16384,128]{1,0:T(8,128)(2,1)} custom-call(bf16[1024,128]{1,0:T(8,128)(2,1)S(1)} %collective-permute-done.10.refs_0_, bf16[1024,128]{1,0:T(8,128)(2,1)S(1)} %collective-permute-done.11.refs_1_, bf16[1024,128]{1,0:T(8,128)(2,1)S(1)} %collective-permute-done.13.refs_2_, ...), custom_call_target="tpu_custom_call", output_to_operand_aliasing={{}: (6, {})} | custom-call | tf_op jit(solution)/shard_map/join/pallas_call | solution.py:423
  91.5 3.5 %collective-permute-done.16.refs_0_ = bf16[1024,128]{1,0:T(8,128)(2,1)S(1)} collective-permute-done((bf16[1024,128]{1,0:T(8,128)(2,1)S(1)}, bf16[1024,128]{1,0:T(8,128)(2,1)S(1)}, u32[]{:S(2)}, u32[]{:S(2)}) %collective-permute-start.16) | collective-permute-done | bytes 262176 | tf_op jit(solution)/shard_map/g_opp_lo/ppermute | solution.py:305
  95.0 0.9 collective-permute-start.20
  96.4 0.6 collective-permute-done.20.refs_4_
  98.1 1.4 %join.3 = bf16[16384,128]{1,0:T(8,128)(2,1)} custom-call(bf16[1024,128]{1,0:T(8,128)(2,1)S(1)} %collective-permute-done.16.refs_0_, bf16[1024,128]{1,0:T(8,128)(2,1)S(1)} %collective-permute-done.17.refs_1_, bf16[1024,128]{1,0:T(8,128)(2,1)S(1)} %collective-permute-done.18.refs_2_, ...), custom_call_target="tpu_custom_call", output_to_operand_aliasing={{}: (8, {})} | custom-call | tf_op jit(solution)/shard_map/join/pallas_call | solution.py:423
  (53 shorter events, 3.2 us)
Async XLA Ops:
  5.4 54.7 %all-to-all-start = ((bf16[128,96,128]{2,1,0:T(8,128)(2,1)}), bf16[128,96,128]{2,1,0:T(8,128)(2,1)S(1)}, u32[]{:S(2)}, u32[]{:S(2)}) async-start(bf16[128,96,128]{2,1,0:T(8,128)(2,1)} %bitcast.51), calls=%async_computation | async-start | bytes 6291456 | tf_op jit(solution)/shard_map/all_to_all | solution.py:472
  19.4 4.2 %collective-permute-start = (bf16[2048,128]{1,0:T(8,128)(2,1)}, bf16[2048,128]{1,0:T(8,128)(2,1)S(1)}, u32[]{:S(2)}, u32[]{:S(2)}) collective-permute-start(bf16[2048,128]{1,0:T(8,128)(2,1)} %get-tuple-element.52), channel_id=1, source_target_pairs={{0,1},{1,0},{2,3},{3,2},{4,5},{5,4},{6,7},{7,6},{8,9},{9,8},{10,11... | collective-permute-start | bytes 1572872 | tf_op jit(solution)/shard_map/r_send/ppermute | solution.py:305
  20.6 3.1 %collective-permute-start.1 = (bf16[2048,128]{1,0:T(8,128)(2,1)}, bf16[2048,128]{1,0:T(8,128)(2,1)S(1)}, u32[]{:S(2)}, u32[]{:S(2)}) collective-permute-start(bf16[2048,128]{1,0:T(8,128)(2,1)} %get-tuple-element.54), channel_id=1, source_target_pairs={{0,1},{1,0},{2,3},{3,2},{4,5},{5,4},{6,7},{7,6},{8,9},{9,8},{10,11... | collective-permute-start | bytes 1572872 | tf_op jit(solution)/shard_map/r_send/ppermute | solution.py:305
  20.6 3.2 %collective-permute-start.2 = (bf16[2048,128]{1,0:T(8,128)(2,1)}, bf16[2048,128]{1,0:T(8,128)(2,1)S(1)}, u32[]{:S(2)}, u32[]{:S(2)}) collective-permute-start(bf16[2048,128]{1,0:T(8,128)(2,1)} %get-tuple-element.56), channel_id=1, source_target_pairs={{0,1},{1,0},{2,3},{3,2},{4,5},{5,4},{6,7},{7,6},{8,9},{9,8},{10,11... | collective-permute-start | bytes 1572872 | tf_op jit(solution)/shard_map/r_send/ppermute | solution.py:305
  21.1 3.5 %collective-permute-start.3 = (bf16[2048,128]{1,0:T(8,128)(2,1)}, bf16[2048,128]{1,0:T(8,128)(2,1)S(1)}, u32[]{:S(2)}, u32[]{:S(2)}) collective-permute-start(bf16[2048,128]{1,0:T(8,128)(2,1)} %get-tuple-element.58), channel_id=1, source_target_pairs={{0,1},{1,0},{2,3},{3,2},{4,5},{5,4},{6,7},{7,6},{8,9},{9,8},{10,11... | collective-permute-start | bytes 1572872 | tf_op jit(solution)/shard_map/r_send/ppermute | solution.py:305
  28.2 31.9 %collective-permute-start.4 = (bf16[1024,128]{1,0:T(8,128)(2,1)}, bf16[1024,128]{1,0:T(8,128)(2,1)}, u32[]{:S(2)}, u32[]{:S(2)}) collective-permute-start(bf16[1024,128]{1,0:T(8,128)(2,1)} %get-tuple-element.59), channel_id=1, source_target_pairs={{0,2},{1,3},{2,4},{3,5},{4,6},{5,7},{6,0},{7,1},{8,10},{9,11},{10,... | collective-permute-start | bytes 786440 | tf_op jit(solution)/shard_map/r_send/ppermute | solution.py:305
  29.0 31.1 %collective-permute-start.5 = (bf16[1024,128]{1,0:T(8,128)(2,1)}, bf16[1024,128]{1,0:T(8,128)(2,1)}, u32[]{:S(2)}, u32[]{:S(2)}) collective-permute-start(bf16[1024,128]{1,0:T(8,128)(2,1)} %get-tuple-element.60), channel_id=1, source_target_pairs={{0,6},{1,7},{2,0},{3,1},{4,2},{5,3},{6,4},{7,5},{8,14},{9,15},{10,... | collective-permute-start | bytes 786440 | tf_op jit(solution)/shard_map/r_send/ppermute | solution.py:305
  31.7 35.7 %collective-permute-start.7 = (bf16[1024,128]{1,0:T(8,128)(2,1)}, bf16[1024,128]{1,0:T(8,128)(2,1)S(1)}, u32[]{:S(2)}, u32[]{:S(2)}) collective-permute-start(bf16[1024,128]{1,0:T(8,128)(2,1)} %get-tuple-element.67), channel_id=1, source_target_pairs={{0,2},{1,3},{2,4},{3,5},{4,6},{5,7},{6,0},{7,1},{8,10},{9,11},{10,... | collective-permute-start | bytes 786440 | tf_op jit(solution)/shard_map/r_send/ppermute | solution.py:305
  31.7 35.7 %collective-permute-start.8 = (bf16[1024,128]{1,0:T(8,128)(2,1)}, bf16[1024,128]{1,0:T(8,128)(2,1)}, u32[]{:S(2)}, u32[]{:S(2)}) collective-permute-start(bf16[1024,128]{1,0:T(8,128)(2,1)} %get-tuple-element.68), channel_id=1, source_target_pairs={{0,6},{1,7},{2,0},{3,1},{4,2},{5,3},{6,4},{7,5},{8,14},{9,15},{10,... | collective-permute-start | bytes 786440 | tf_op jit(solution)/shard_map/r_send/ppermute | solution.py:305
  60.1 10.2 %copy-start.1 = (bf16[2048,128]{1,0:T(8,128)(2,1)S(1)}, bf16[2048,128]{1,0:T(8,128)(2,1)}, u32[]{:S(2)}) copy-start(bf16[2048,128]{1,0:T(8,128)(2,1)} %get-tuple-element.73.mine_ref) | copy-start | bytes 1572868
  62.4 7.9 %collective-permute-start.6 = (bf16[1024,128]{1,0:T(8,128)(2,1)}, bf16[1024,128]{1,0:T(8,128)(2,1)S(1)}, u32[]{:S(2)}, u32[]{:S(2)}) collective-permute-start(bf16[1024,128]{1,0:T(8,128)(2,1)} %get-tuple-element.66), channel_id=1, source_target_pairs={{0,2},{1,3},{2,4},{3,5},{4,6},{5,7},{6,0},{7,1},{8,10},{9,11},{10,... | collective-permute-start | bytes 786440 | tf_op jit(solution)/shard_map/r_send/ppermute | solution.py:305
  62.4 7.9 %collective-permute-start.9 = (bf16[1024,128]{1,0:T(8,128)(2,1)}, bf16[1024,128]{1,0:T(8,128)(2,1)S(1)}, u32[]{:S(2)}, u32[]{:S(2)}) collective-permute-start(bf16[1024,128]{1,0:T(8,128)(2,1)} %get-tuple-element.69), channel_id=1, source_target_pairs={{0,6},{1,7},{2,0},{3,1},{4,2},{5,3},{6,4},{7,5},{8,14},{9,15},{10,... | collective-permute-start | bytes 786440 | tf_op jit(solution)/shard_map/r_send/ppermute | solution.py:305
  67.4 12.3 %copy-start = (bf16[3,2048,128]{2,1,0:T(8,128)(2,1)}, bf16[3,2048,128]{2,1,0:T(8,128)(2,1)S(1)}, u32[]{:S(2)}) copy-start(bf16[3,2048,128]{2,1,0:T(8,128)(2,1)S(1)} %unpack.1.old_ref) | copy-start | bytes 4718596
  67.4 12.3 %copy-start.2 = (bf16[1024,128]{1,0:T(8,128)(2,1)}, bf16[1024,128]{1,0:T(8,128)(2,1)S(1)}, u32[]{:S(2)}) copy-start(bf16[1024,128]{1,0:T(8,128)(2,1)S(1)} %collective-permute-done.7.refs_1_) | copy-start | bytes 786436
  70.3 9.4 %copy-start.3 = (bf16[1024,128]{1,0:T(8,128)(2,1)}, bf16[1024,128]{1,0:T(8,128)(2,1)S(1)}, u32[]{:S(2)}) copy-start(bf16[1024,128]{1,0:T(8,128)(2,1)S(1)} %collective-permute-done.6.refs_0_) | copy-start | bytes 786436
  70.3 9.4 %copy-start.4 = (bf16[1024,128]{1,0:T(8,128)(2,1)}, bf16[1024,128]{1,0:T(8,128)(2,1)S(1)}, u32[]{:S(2)}) copy-start(bf16[1024,128]{1,0:T(8,128)(2,1)S(1)} %collective-permute-done.9.refs_3_) | copy-start | bytes 786436
  72.3 7.5 %copy-start.5 = (bf16[1024,128]{1,0:T(8,128)(2,1)}, bf16[1024,128]{1,0:T(8,128)(2,1)S(1)}, u32[]{:S(2)}) copy-start(bf16[1024,128]{1,0:T(8,128)(2,1)S(1)} %get-tuple-element.71.refs_5_) | copy-start | bytes 786436
  72.3 7.5 %copy-start.6 = (bf16[1024,128]{1,0:T(8,128)(2,1)}, bf16[1024,128]{1,0:T(8,128)(2,1)S(1)}, u32[]{:S(2)}) copy-start(bf16[1024,128]{1,0:T(8,128)(2,1)S(1)} %get-tuple-element.70.refs_4_) | copy-start | bytes 786436
  72.3 7.3 %collective-permute-start.12 = (bf16[1024,128]{1,0:T(8,128)(2,1)S(1)}, bf16[1024,128]{1,0:T(8,128)(2,1)S(1)}, u32[]{:S(2)}, u32[]{:S(2)}) collective-permute-start(bf16[1024,128]{1,0:T(8,128)(2,1)S(1)} %get-tuple-element.70.refs_4_), channel_id=1, source_target_pairs={{0,1},{1,0},{2,3},{3,2},{4,5},{5,4},{6,7},{7,6},{8,9},{9,8},{10,11... | collective-permute-start | bytes 786440 | tf_op jit(solution)/shard_map/g_sib_lo/ppermute | solution.py:305
  74.7 9.6 %collective-permute-start.10 = (bf16[1024,128]{1,0:T(8,128)(2,1)S(1)}, bf16[1024,128]{1,0:T(8,128)(2,1)S(1)}, u32[]{:S(2)}, u32[]{:S(2)}) collective-permute-start(bf16[1024,128]{1,0:T(8,128)(2,1)S(1)} %get-tuple-element.70.refs_4_), channel_id=1, source_target_pairs={{0,2},{1,3},{2,4},{3,5},{4,6},{5,7},{6,0},{7,1},{8,10},{9,11},{10,... | collective-permute-start | bytes 786440 | tf_op jit(solution)/shard_map/g_up_lo/ppermute | solution.py:305
  74.7 9.6 %collective-permute-start.11 = (bf16[1024,128]{1,0:T(8,128)(2,1)S(1)}, bf16[1024,128]{1,0:T(8,128)(2,1)S(1)}, u32[]{:S(2)}, u32[]{:S(2)}) collective-permute-start(bf16[1024,128]{1,0:T(8,128)(2,1)S(1)} %get-tuple-element.71.refs_5_), channel_id=1, source_target_pairs={{0,6},{1,7},{2,0},{3,1},{4,2},{5,3},{6,4},{7,5},{8,14},{9,15},{10,... | collective-permute-start | bytes 786440 | tf_op jit(solution)/shard_map/g_dn_hi/ppermute | solution.py:305
  77.4 11.0 %collective-permute-start.14 = (bf16[1024,128]{1,0:T(8,128)(2,1)S(1)}, bf16[1024,128]{1,0:T(8,128)(2,1)S(1)}, u32[]{:S(2)}, u32[]{:S(2)}) collective-permute-start(bf16[1024,128]{1,0:T(8,128)(2,1)S(1)} %get-tuple-element.70.refs_4_), channel_id=1, source_target_pairs={{0,6},{1,7},{2,0},{3,1},{4,2},{5,3},{6,4},{7,5},{8,14},{9,15},{10,... | collective-permute-start | bytes 786440 | tf_op jit(solution)/shard_map/g_dn_lo/ppermute | solution.py:305
  78.7 11.6 %collective-permute-start.15 = (bf16[1024,128]{1,0:T(8,128)(2,1)S(1)}, bf16[1024,128]{1,0:T(8,128)(2,1)S(1)}, u32[]{:S(2)}, u32[]{:S(2)}) collective-permute-start(bf16[1024,128]{1,0:T(8,128)(2,1)S(1)} %get-tuple-element.71.refs_5_), channel_id=1, source_target_pairs={{0,1},{1,0},{2,3},{3,2},{4,5},{5,4},{6,7},{7,6},{8,9},{9,8},{10,11... | collective-permute-start | bytes 786440 | tf_op jit(solution)/shard_map/g_sib_hi/ppermute | solution.py:305
  79.6 10.7 %collective-permute-start.13 = (bf16[1024,128]{1,0:T(8,128)(2,1)S(1)}, bf16[1024,128]{1,0:T(8,128)(2,1)S(1)}, u32[]{:S(2)}, u32[]{:S(2)}) collective-permute-start(bf16[1024,128]{1,0:T(8,128)(2,1)S(1)} %get-tuple-element.71.refs_5_), channel_id=1, source_target_pairs={{0,2},{1,3},{2,4},{3,5},{4,6},{5,7},{6,0},{7,1},{8,10},{9,11},{10,... | collective-permute-start | bytes 786440 | tf_op jit(solution)/shard_map/g_up_hi/ppermute | solution.py:305
  84.3 10.7 %collective-permute-start.16 = (bf16[1024,128]{1,0:T(8,128)(2,1)S(1)}, bf16[1024,128]{1,0:T(8,128)(2,1)S(1)}, u32[]{:S(2)}, u32[]{:S(2)}) collective-permute-start(bf16[1024,128]{1,0:T(8,128)(2,1)S(1)} %collective-permute-done.10.refs_0_), channel_id=1, source_target_pairs={{0,2},{1,3},{2,4},{3,5},{4,6},{5,7},{6,0},{7,1},{8,10},{9,11},{10,... | collective-permute-start | bytes 786440 | tf_op jit(solution)/shard_map/g_opp_lo/ppermute | solution.py:305
  84.5 10.5 %collective-permute-start.17 = (bf16[1024,128]{1,0:T(8,128)(2,1)S(1)}, bf16[1024,128]{1,0:T(8,128)(2,1)S(1)}, u32[]{:S(2)}, u32[]{:S(2)}) collective-permute-start(bf16[1024,128]{1,0:T(8,128)(2,1)S(1)} %collective-permute-done.11.refs_1_), channel_id=1, source_target_pairs={{0,6},{1,7},{2,0},{3,1},{4,2},{5,3},{6,4},{7,5},{8,14},{9,15},{10,... | collective-permute-start | bytes 786440 | tf_op jit(solution)/shard_map/g_opp_hi/ppermute | solution.py:305
  88.3 8.0 %collective-permute-start.22 = (bf16[1024,128]{1,0:T(8,128)(2,1)S(1)}, bf16[1024,128]{1,0:T(8,128)(2,1)S(1)}, u32[]{:S(2)}, u32[]{:S(2)}) collective-permute-start(bf16[1024,128]{1,0:T(8,128)(2,1)S(1)} %collective-permute-done.10.refs_0_), channel_id=1, source_target_pairs={{0,1},{1,0},{2,3},{3,2},{4,5},{5,4},{6,7},{7,6},{8,9},{9,8},{10,11... | collective-permute-start | bytes 786440 | tf_op jit(solution)/shard_map/g_sib_up_lo/ppermute | solution.py:305
  90.3 6.1 %collective-permute-start.23 = (bf16[1024,128]{1,0:T(8,128)(2,1)S(1)}, bf16[1024,128]{1,0:T(8,128)(2,1)S(1)}, u32[]{:S(2)}, u32[]{:S(2)}) collective-permute-start(bf16[1024,128]{1,0:T(8,128)(2,1)S(1)} %collective-permute-done.11.refs_1_), channel_id=1, source_target_pairs={{0,1},{1,0},{2,3},{3,2},{4,5},{5,4},{6,7},{7,6},{8,9},{9,8},{10,11... | collective-permute-start | bytes 786440 | tf_op jit(solution)/shard_map/g_sib_dn_hi/ppermute | solution.py:305
  95.0 2.0 %collective-permute-start.20 = (bf16[1024,128]{1,0:T(8,128)(2,1)S(1)}, bf16[1024,128]{1,0:T(8,128)(2,1)S(1)}, u32[]{:S(2)}, u32[]{:S(2)}) collective-permute-start(bf16[1024,128]{1,0:T(8,128)(2,1)S(1)} %collective-permute-done.13.refs_2_), channel_id=1, source_target_pairs={{0,1},{1,0},{2,3},{3,2},{4,5},{5,4},{6,7},{7,6},{8,9},{9,8},{10,11... | collective-permute-start | bytes 786440 | tf_op jit(solution)/shard_map/g_sib_up_hi/ppermute | solution.py:305
  95.9 1.5 %collective-permute-start.21 = (bf16[1024,128]{1,0:T(8,128)(2,1)S(1)}, bf16[1024,128]{1,0:T(8,128)(2,1)S(1)}, u32[]{:S(2)}, u32[]{:S(2)}) collective-permute-start(bf16[1024,128]{1,0:T(8,128)(2,1)S(1)} %collective-permute-done.14.refs_3_), channel_id=1, source_target_pairs={{0,1},{1,0},{2,3},{3,2},{4,5},{5,4},{6,7},{7,6},{8,9},{9,8},{10,11... | collective-permute-start | bytes 786440 | tf_op jit(solution)/shard_map/g_sib_dn_lo/ppermute | solution.py:305
  95.9 1.9 %collective-permute-start.18 = (bf16[1024,128]{1,0:T(8,128)(2,1)S(1)}, bf16[1024,128]{1,0:T(8,128)(2,1)S(1)}, u32[]{:S(2)}, u32[]{:S(2)}) collective-permute-start(bf16[1024,128]{1,0:T(8,128)(2,1)S(1)} %collective-permute-done.16.refs_0_), channel_id=1, source_target_pairs={{0,1},{1,0},{2,3},{3,2},{4,5},{5,4},{6,7},{7,6},{8,9},{9,8},{10,11... | collective-permute-start | bytes 786440 | tf_op jit(solution)/shard_map/g_sib_opp_lo/ppermute | solution.py:305
  96.4 1.8 %collective-permute-start.19 = (bf16[1024,128]{1,0:T(8,128)(2,1)S(1)}, bf16[1024,128]{1,0:T(8,128)(2,1)S(1)}, u32[]{:S(2)}, u32[]{:S(2)}) collective-permute-start(bf16[1024,128]{1,0:T(8,128)(2,1)S(1)} %collective-permute-done.17.refs_1_), channel_id=1, source_target_pairs={{0,1},{1,0},{2,3},{3,2},{4,5},{5,4},{6,7},{7,6},{8,9},{9,8},{10,11... | collective-permute-start | bytes 786440 | tf_op jit(solution)/shard_map/g_sib_opp_hi/ppermute | solution.py:305
  (4 other events, 3.6 us)

commit v6 on v5

--- a/solution.py
+++ b/solution.py
@@ -395,13 +395,19 @@
     def both(step, first, rows):
         return [(own[step], first, rows), (got[step], first, rows)]
 
-    opp_lo, opp_hi, up_hi, dn_lo, mine = add(
-        both(2, 0, half), both(2, half, half), both(1, half, half), both(3, 0, half), both(0, 0, span)
+    opp_lo, opp_hi, up_hi, dn_lo, up_lo, dn_hi, mine = add(
+        both(2, 0, half),
+        both(2, half, half),
+        both(1, half, half),
+        both(3, 0, half),
+        both(1, 0, half),
+        both(3, half, half),
+        both(0, 0, span),
     )
     opp_up, opp_dn = send(opp_lo, 1), send(opp_hi, 3)
     up_hi_got, dn_lo_got = send(up_hi, 1), send(dn_lo, 3)
     opp_up, opp_dn, arrived = lax.optimization_barrier((opp_up, opp_dn, arrived))
-    up_lo, dn_hi = add(both(1, 0, half) + [(opp_up, 0, half)], both(3, half, half) + [(opp_dn, 0, half)])
+    up_lo, dn_hi = add([(up_lo, 0, half), (opp_up, 0, half)], [(dn_hi, 0, half), (opp_dn, 0, half)])
     return (mine, send(up_lo, 1), up_hi_got, dn_lo_got, send(dn_hi, 3)), arrived
 
 
@@ -450,7 +456,10 @@
         parts.append(send(part, 0, True, name="g_sib_" + name))
     parts += [sib_up_lo, sib_dn_hi]
     starts = [(2, 0, 0), (2, 0, half), (2, 1, 0), (2, 1, half), (3, 1, half), (1, 1, 0), (3, 1, 0), (1, 1, half)]
-    return join(span, starts, parts, whole), rest
+    late = [k for k in range(len(parts)) if k in (2, 3)]
+    soon = [k for k in range(len(parts)) if k not in late]
+    whole = join(span, [starts[k] for k in soon], [parts[k] for k in soon], whole)
+    return join(span, [starts[k] for k in late], [parts[k] for k in late], whole), rest
 
 
 def arrivals(old_map, block_rows, peer_cap):

time: 100 us -> 99.7 us (level)
  waiting for transfers between devices: 36 us -> 34.7 us
  Pallas kernels: 25.2 us -> 26.2 us
    ppermute x24, waiting for transfers between devices: 36 us -> 34.7 us  [send(): return lax.ppermute(values, 'dp', sends(shift, flip))]
    pallas_call x2 -> x3, Pallas kernels: 2.58 us -> 3.22 us  [join(): pl.pallas_call(functools.partial(join_kernel, span, starts), out_shape=ja...]
  transfers between devices with their start and end apart: 25 -> 25, of which waited for: 10 -> 8; matrix products, arithmetic and copies ran while one was open for 2% -> 2% of each run, Pallas kernels for 17% -> 19%
where the time goes in v6:
time: 99.7 us; the launch traced here: 99.3 us
  starting transfers between devices  34.9 us (35%)
  waiting for transfers between devices  34.7 us (35%)
  Pallas kernels  26.2 us (26%)
  other arithmetic  1.71 us (2%)
    ppermute x24, waiting for transfers between devices, send(): return lax.ppermute(values, 'dp', sends(shift, flip))  34.7 us
    ppermute x24, starting transfers between devices, send(): return lax.ppermute(values, 'dp', sends(shift, flip))  23.4 us
    all_to_all x1, starting transfers between devices, local(): lax.all_to_all(packed.reshape(count_all, peer_cap * 3 * chunks, LANES), A...  11.5 us
    pallas_call x2, Pallas kernels, add(): pl.pallas_call(functools.partial(add_kernel, windows, order), out_shape=[...  5.55 us
    pallas_call x2, Pallas kernels, cut(): pl.pallas_call(functools.partial(cut_kernel, shards), out_shape=[jax.Shap...  4.88 us
    pallas_call x1, Pallas kernels, pack(): pl.pallas_call(functools.partial(pack_kernel, rows, chunks), out_shape=ja...  4.76 us
    pallas_call x1, Pallas kernels, adam(): pl.pallas_call(functools.partial(adam_kernel, rows, chunks), out_shape=[j...  4.51 us
    pallas_call x3, Pallas kernels, join(): pl.pallas_call(functools.partial(join_kernel, span, starts), out_shape=ja...  3.22 us
  transfers between devices with their start and end apart: 25, of which 8 were waited for; matrix products, arithmetic and copies ran while one was open for 2% of the time, Pallas kernels for 19%

profile of v6, /device:TPU:1, one launch (start us, length us, event | category | flops | bytes accessed | tf_op | source)
XLA Modules:
  0.0 99.3 jit_solution(1042962745004817152)
XLA Ops:
  0.6 4.8 %pack.1 = bf16[256,48,128]{2,1,0:T(8,128)(2,1)} custom-call(s32[128,128]{1,0:T(8,128)} %bitcast.55, bf16[1,128]{1,0:T(2,128)(2,1)} %bitcast.56, bf16[1,128]{1,0:T(2,128)(2,1)} %bitcast.57, f32[2048,128]{1,0:T(8,128)} %bitcast.52, bf16[2048,128]{1,0:T(8,128)(2,1)} %bitcast.53, bf16[2048,128]{1,0:T(8,128)(2,1)} %bitcast.54), custom_call_target="tpu_custom_call" | custom-call | tf_op jit(solution)/shard_map/pack/pallas_call | solution.py:98
  5.4 11.5 %all-to-all-start = ((bf16[128,96,128]{2,1,0:T(8,128)(2,1)}), bf16[128,96,128]{2,1,0:T(8,128)(2,1)S(1)}, u32[]{:S(2)}, u32[]{:S(2)}) async-start(bf16[128,96,128]{2,1,0:T(8,128)(2,1)} %bitcast.51), calls=%async_computation | async-start | bytes 6291456 | tf_op jit(solution)/shard_map/all_to_all | solution.py:481
  16.9 2.5 %cut.3 = (bf16[2048,128]{1,0:T(8,128)(2,1)}, bf16[2048,128]{1,0:T(8,128)(2,1)}, bf16[2048,128]{1,0:T(8,128)(2,1)}, bf16[2048,128]{1,0:T(8,128)(2,1)}) custom-call(bf16[8,2048,128]{2,1,0:T(8,128)(2,1)} %bitcast.49), custom_call_target="tpu_custom_call" | custom-call | tf_op jit(solution)/shard_map/cut/pallas_call | solution.py:329
  19.4 1.1 %collective-permute-start = (bf16[2048,128]{1,0:T(8,128)(2,1)}, bf16[2048,128]{1,0:T(8,128)(2,1)S(1)}, u32[]{:S(2)}, u32[]{:S(2)}) collective-permute-start(bf16[2048,128]{1,0:T(8,128)(2,1)} %get-tuple-element.54), channel_id=1, source_target_pairs={{0,1},{1,0},{2,3},{3,2},{4,5},{5,4},{6,7},{7,6},{8,9},{9,8},{10,11... | collective-permute-start | bytes 1572872 | tf_op jit(solution)/shard_map/r_send/ppermute | solution.py:305
  21.1 2.4 %cut.2 = (bf16[2048,128]{1,0:T(8,128)(2,1)}, bf16[2048,128]{1,0:T(8,128)(2,1)}, bf16[2048,128]{1,0:T(8,128)(2,1)}, bf16[2048,128]{1,0:T(8,128)(2,1)}) custom-call(bf16[8,2048,128]{2,1,0:T(8,128)(2,1)} %bitcast.50), custom_call_target="tpu_custom_call" | custom-call | tf_op jit(solution)/shard_map/cut/pallas_call | solution.py:329
  23.8 0.7 collective-permute-done.3.refs_13_
  25.3 3.5 %add.16 = (bf16[1024,128]{1,0:T(8,128)(2,1)}, bf16[1024,128]{1,0:T(8,128)(2,1)}, bf16[1024,128]{1,0:T(8,128)(2,1)}, bf16[1024,128]{1,0:T(8,128)(2,1)}, bf16[1024...) custom-call(bf16[2048,128]{1,0:T(8,128)(2,1)} %get-tuple-element.53.refs_0_.refs_2_, ...), custom_call_target="tpu_custom_call" | custom-call | tf_op jit(solution)/shard_map/add/pallas_call | solution.py:376
  28.8 0.8 collective-permute-start.4
  29.6 2.0 %collective-permute-start.5 = (bf16[1024,128]{1,0:T(8,128)(2,1)}, bf16[1024,128]{1,0:T(8,128)(2,1)}, u32[]{:S(2)}, u32[]{:S(2)}) collective-permute-start(bf16[1024,128]{1,0:T(8,128)(2,1)} %get-tuple-element.62), channel_id=1, source_target_pairs={{0,6},{1,7},{2,0},{3,1},{4,2},{5,3},{6,4},{7,5},{8,14},{9,15},{10,... | collective-permute-start | bytes 786440 | tf_op jit(solution)/shard_map/r_send/ppermute | solution.py:305
  31.6 0.8 and_select_fusion
  32.4 2.7 %collective-permute-start.8 = (bf16[1024,128]{1,0:T(8,128)(2,1)}, bf16[1024,128]{1,0:T(8,128)(2,1)}, u32[]{:S(2)}, u32[]{:S(2)}) collective-permute-start(bf16[1024,128]{1,0:T(8,128)(2,1)} %get-tuple-element.72), channel_id=1, source_target_pairs={{0,6},{1,7},{2,0},{3,1},{4,2},{5,3},{6,4},{7,5},{8,14},{9,15},{10,... | collective-permute-start | bytes 786440 | tf_op jit(solution)/shard_map/r_send/ppermute | solution.py:305
  35.0 25.1 %collective-permute-done.4.refs_1_ = bf16[1024,128]{1,0:T(8,128)(2,1)} collective-permute-done((bf16[1024,128]{1,0:T(8,128)(2,1)}, bf16[1024,128]{1,0:T(8,128)(2,1)}, u32[]{:S(2)}, u32[]{:S(2)}) %collective-permute-start.4) | collective-permute-done | bytes 262176 | tf_op jit(solution)/shard_map/r_send/ppermute | solution.py:305
  60.1 2.0 %add.17 = (bf16[1024,128]{1,0:T(8,128)(2,1)}, bf16[1024,128]{1,0:T(8,128)(2,1)}) custom-call(bf16[1024,128]{1,0:T(8,128)(2,1)} %get-tuple-element.66.refs_0_, bf16[1024,128]{1,0:T(8,128)(2,1)} %collective-permute-done.4.refs_1_, bf16[1024,128]{1,0:T(8,128)(2,1)} %get-tuple-element.68.refs_2_, bf16[1024,128]{1,0:T(8,128)(2,1)} %collective-permute-done.5.refs_3_), custom_call_target="tpu_custom_call" | custom-call | tf_op jit(solution)/shard_map/add/pallas_call | solution.py:376
  62.3 2.7 %collective-permute-start.9 = (bf16[1024,128]{1,0:T(8,128)(2,1)}, bf16[1024,128]{1,0:T(8,128)(2,1)S(1)}, u32[]{:S(2)}, u32[]{:S(2)}) collective-permute-start(bf16[1024,128]{1,0:T(8,128)(2,1)} %get-tuple-element.73), channel_id=1, source_target_pairs={{0,6},{1,7},{2,0},{3,1},{4,2},{5,3},{6,4},{7,5},{8,14},{9,15},{10,... | collective-permute-start | bytes 786440 | tf_op jit(solution)/shard_map/r_send/ppermute | solution.py:305
  65.1 0.8 multiply_add_fusion.slot_ref
  65.9 1.3 %unpack.1.old_ref = bf16[3,2048,128]{2,1,0:T(8,128)(2,1)S(1)} custom-call(s32[128]{0:T(128)S(1)} %multiply_add_fusion.slot_ref, bf16[256,48,128]{2,1,0:T(8,128)(2,1)S(1)} %bitcast.47), custom_call_target="tpu_custom_call" | custom-call | tf_op jit(solution)/shard_map/unpack/pallas_call | solution.py:148
  67.3 2.9 %collective-permute-done.6.refs_0_ = bf16[1024,128]{1,0:T(8,128)(2,1)S(1)} collective-permute-done((bf16[1024,128]{1,0:T(8,128)(2,1)}, bf16[1024,128]{1,0:T(8,128)(2,1)S(1)}, u32[]{:S(2)}, u32[]{:S(2)}) %collective-permute-start.6) | collective-permute-done | bytes 262176 | tf_op jit(solution)/shard_map/r_send/ppermute | solution.py:305
  70.1 2.0 %new_weights.1 = (bf16[1024,128]{1,0:T(8,128)(2,1)S(1)}, bf16[1024,128]{1,0:T(8,128)(2,1)S(1)}) custom-call(bf16[3,2048,128]{2,1,0:T(8,128)(2,1)S(1)} %unpack.1.old_ref, bf16[2048,128]{1,0:T(8,128)(2,1)S(1)} %copy-done.1, bf16[1024,128]{1,0:T(8,128)(2,1)S(1)} %collective-permute-done.6.refs_0_, bf16[1024,128]{1,0:T(8,128)(2,1)S(1)} %collective-permute-done.7.refs_1_, ...), custom_call_target="tpu_custom_call" | custom-call | tf_op jit(solution)/shard_map/new_weights/pallas_call | solution.py:196
  72.1 2.4 %collective-permute-start.12 = (bf16[1024,128]{1,0:T(8,128)(2,1)S(1)}, bf16[1024,128]{1,0:T(8,128)(2,1)S(1)}, u32[]{:S(2)}, u32[]{:S(2)}) collective-permute-start(bf16[1024,128]{1,0:T(8,128)(2,1)S(1)} %get-tuple-element.74.refs_4_), channel_id=1, source_target_pairs={{0,1},{1,0},{2,3},{3,2},{4,5},{5,4},{6,7},{7,6},{8,9},{9,8},{10,11... | collective-permute-start | bytes 786440 | tf_op jit(solution)/shard_map/g_sib_lo/ppermute | solution.py:305
  74.5 2.7 %collective-permute-start.11 = (bf16[1024,128]{1,0:T(8,128)(2,1)S(1)}, bf16[1024,128]{1,0:T(8,128)(2,1)S(1)}, u32[]{:S(2)}, u32[]{:S(2)}) collective-permute-start(bf16[1024,128]{1,0:T(8,128)(2,1)S(1)} %get-tuple-element.75.refs_5_), channel_id=1, source_target_pairs={{0,6},{1,7},{2,0},{3,1},{4,2},{5,3},{6,4},{7,5},{8,14},{9,15},{10,... | collective-permute-start | bytes 786440 | tf_op jit(solution)/shard_map/g_dn_hi/ppermute | solution.py:305
  77.2 1.4 %collective-permute-start.14 = (bf16[1024,128]{1,0:T(8,128)(2,1)S(1)}, bf16[1024,128]{1,0:T(8,128)(2,1)S(1)}, u32[]{:S(2)}, u32[]{:S(2)}) collective-permute-start(bf16[1024,128]{1,0:T(8,128)(2,1)S(1)} %get-tuple-element.74.refs_4_), channel_id=1, source_target_pairs={{0,6},{1,7},{2,0},{3,1},{4,2},{5,3},{6,4},{7,5},{8,14},{9,15},{10,... | collective-permute-start | bytes 786440 | tf_op jit(solution)/shard_map/g_dn_lo/ppermute | solution.py:305
  78.5 0.9 collective-permute-start.15
  79.6 4.5 %adam.1 = (bf16[16384,128]{1,0:T(8,128)(2,1)}, f32[2048,128]{1,0:T(8,128)}, bf16[2048,128]{1,0:T(8,128)(2,1)}, bf16[2048,128]{1,0:T(8,128)(2,1)}, bf16[1,128]{1,0:T(2,128)(2,1)}, /*index=5*/bf16[1,128]{1,0:T(2,128)(2,1)}) custom-call(bf16[3,2048,128]{2,1,0:T(8,128)(2,1)} %copy-done, bf16[2048,128]{1,0:T(8,128)(2,1)} %get-tuple-element.77.mine_ref, ...), custom_call_target="tpu_custom_call" | custom-call | bytes 16777216 | tf_op jit(solution)/shard_map/adam/pallas_call | solution.py:260
  84.3 2.5 %collective-permute-start.17 = (bf16[1024,128]{1,0:T(8,128)(2,1)S(1)}, bf16[1024,128]{1,0:T(8,128)(2,1)S(1)}, u32[]{:S(2)}, u32[]{:S(2)}) collective-permute-start(bf16[1024,128]{1,0:T(8,128)(2,1)S(1)} %collective-permute-done.11.refs_1_), channel_id=1, source_target_pairs={{0,6},{1,7},{2,0},{3,1},{4,2},{5,3},{6,4},{7,5},{8,14},{9,15},{10,... | collective-permute-start | bytes 786440 | tf_op jit(solution)/shard_map/g_opp_hi/ppermute | solution.py:305
  86.9 1.3 %collective-permute-done.14.refs_3_ = bf16[1024,128]{1,0:T(8,128)(2,1)S(1)} collective-permute-done((bf16[1024,128]{1,0:T(8,128)(2,1)S(1)}, bf16[1024,128]{1,0:T(8,128)(2,1)S(1)}, u32[]{:S(2)}, u32[]{:S(2)}) %collective-permute-start.14) | collective-permute-done | bytes 262176 | tf_op jit(solution)/shard_map/g_dn_lo/ppermute | solution.py:305
  88.1 2.0 %collective-permute-start.22 = (bf16[1024,128]{1,0:T(8,128)(2,1)S(1)}, bf16[1024,128]{1,0:T(8,128)(2,1)S(1)}, u32[]{:S(2)}, u32[]{:S(2)}) collective-permute-start(bf16[1024,128]{1,0:T(8,128)(2,1)S(1)} %collective-permute-done.10.refs_0_), channel_id=1, source_target_pairs={{0,1},{1,0},{2,3},{3,2},{4,5},{5,4},{6,7},{7,6},{8,9},{9,8},{10,11... | collective-permute-start | bytes 786440 | tf_op jit(solution)/shard_map/g_sib_up_lo/ppermute | solution.py:305
  90.1 1.2 %join.3.refs_6_ = bf16[16384,128]{1,0:T(8,128)(2,1)} custom-call(bf16[1024,128]{1,0:T(8,128)(2,1)S(1)} %collective-permute-done.10.refs_0_, bf16[1024,128]{1,0:T(8,128)(2,1)S(1)} %collective-permute-done.11.refs_1_, bf16[1024,128]{1,0:T(8,128)(2,1)S(1)} %collective-permute-done.13.refs_2_, ...), custom_call_target="tpu_custom_call", output_to_operand_aliasing={{}: (6, {})} | custom-call | tf_op jit(solution)/shard_map/join/pallas_call | solution.py:429
  91.3 3.5 %collective-permute-done.16.refs_0_ = bf16[1024,128]{1,0:T(8,128)(2,1)S(1)} collective-permute-done((bf16[1024,128]{1,0:T(8,128)(2,1)S(1)}, bf16[1024,128]{1,0:T(8,128)(2,1)S(1)}, u32[]{:S(2)}, u32[]{:S(2)}) %collective-permute-start.16) | collective-permute-done | bytes 262176 | tf_op jit(solution)/shard_map/g_opp_lo/ppermute | solution.py:305
  94.8 0.9 collective-permute-start.20
  96.2 0.6 collective-permute-done.20.refs_2_
  97.2 1.2 %join.4.refs_2_ = bf16[16384,128]{1,0:T(8,128)(2,1)} custom-call(bf16[1024,128]{1,0:T(8,128)(2,1)S(1)} %collective-permute-done.16.refs_0_, bf16[1024,128]{1,0:T(8,128)(2,1)S(1)} %collective-permute-done.17.refs_1_, bf16[1024,128]{1,0:T(8,128)(2,1)S(1)} %collective-permute-done.20.refs_2_, ...), custom_call_target="tpu_custom_call", output_to_operand_aliasing={{}: (6, {})} | custom-call | tf_op jit(solution)/shard_map/join/pallas_call | solution.py:429
  98.4 0.8 join.5
  (54 shorter events, 3.1 us)
Async XLA Ops:
  5.4 54.7 %all-to-all-start = ((bf16[128,96,128]{2,1,0:T(8,128)(2,1)}), bf16[128,96,128]{2,1,0:T(8,128)(2,1)S(1)}, u32[]{:S(2)}, u32[]{:S(2)}) async-start(bf16[128,96,128]{2,1,0:T(8,128)(2,1)} %bitcast.51), calls=%async_computation | async-start | bytes 6291456 | tf_op jit(solution)/shard_map/all_to_all | solution.py:481
  19.4 4.2 %collective-permute-start = (bf16[2048,128]{1,0:T(8,128)(2,1)}, bf16[2048,128]{1,0:T(8,128)(2,1)S(1)}, u32[]{:S(2)}, u32[]{:S(2)}) collective-permute-start(bf16[2048,128]{1,0:T(8,128)(2,1)} %get-tuple-element.54), channel_id=1, source_target_pairs={{0,1},{1,0},{2,3},{3,2},{4,5},{5,4},{6,7},{7,6},{8,9},{9,8},{10,11... | collective-permute-start | bytes 1572872 | tf_op jit(solution)/shard_map/r_send/ppermute | solution.py:305
  20.5 3.1 %collective-permute-start.1 = (bf16[2048,128]{1,0:T(8,128)(2,1)}, bf16[2048,128]{1,0:T(8,128)(2,1)S(1)}, u32[]{:S(2)}, u32[]{:S(2)}) collective-permute-start(bf16[2048,128]{1,0:T(8,128)(2,1)} %get-tuple-element.56), channel_id=1, source_target_pairs={{0,1},{1,0},{2,3},{3,2},{4,5},{5,4},{6,7},{7,6},{8,9},{9,8},{10,11... | collective-permute-start | bytes 1572872 | tf_op jit(solution)/shard_map/r_send/ppermute | solution.py:305
  20.6 3.2 %collective-permute-start.2 = (bf16[2048,128]{1,0:T(8,128)(2,1)}, bf16[2048,128]{1,0:T(8,128)(2,1)S(1)}, u32[]{:S(2)}, u32[]{:S(2)}) collective-permute-start(bf16[2048,128]{1,0:T(8,128)(2,1)} %get-tuple-element.58), channel_id=1, source_target_pairs={{0,1},{1,0},{2,3},{3,2},{4,5},{5,4},{6,7},{7,6},{8,9},{9,8},{10,11... | collective-permute-start | bytes 1572872 | tf_op jit(solution)/shard_map/r_send/ppermute | solution.py:305
  21.0 3.5 %collective-permute-start.3 = (bf16[2048,128]{1,0:T(8,128)(2,1)}, bf16[2048,128]{1,0:T(8,128)(2,1)S(1)}, u32[]{:S(2)}, u32[]{:S(2)}) collective-permute-start(bf16[2048,128]{1,0:T(8,128)(2,1)} %get-tuple-element.60), channel_id=1, source_target_pairs={{0,1},{1,0},{2,3},{3,2},{4,5},{5,4},{6,7},{7,6},{8,9},{9,8},{10,11... | collective-permute-start | bytes 1572872 | tf_op jit(solution)/shard_map/r_send/ppermute | solution.py:305
  28.8 31.3 %collective-permute-start.4 = (bf16[1024,128]{1,0:T(8,128)(2,1)}, bf16[1024,128]{1,0:T(8,128)(2,1)}, u32[]{:S(2)}, u32[]{:S(2)}) collective-permute-start(bf16[1024,128]{1,0:T(8,128)(2,1)} %get-tuple-element.61), channel_id=1, source_target_pairs={{0,2},{1,3},{2,4},{3,5},{4,6},{5,7},{6,0},{7,1},{8,10},{9,11},{10,... | collective-permute-start | bytes 786440 | tf_op jit(solution)/shard_map/r_send/ppermute | solution.py:305
  29.6 30.5 %collective-permute-start.5 = (bf16[1024,128]{1,0:T(8,128)(2,1)}, bf16[1024,128]{1,0:T(8,128)(2,1)}, u32[]{:S(2)}, u32[]{:S(2)}) collective-permute-start(bf16[1024,128]{1,0:T(8,128)(2,1)} %get-tuple-element.62), channel_id=1, source_target_pairs={{0,6},{1,7},{2,0},{3,1},{4,2},{5,3},{6,4},{7,5},{8,14},{9,15},{10,... | collective-permute-start | bytes 786440 | tf_op jit(solution)/shard_map/r_send/ppermute | solution.py:305
  32.4 34.9 %collective-permute-start.7 = (bf16[1024,128]{1,0:T(8,128)(2,1)}, bf16[1024,128]{1,0:T(8,128)(2,1)S(1)}, u32[]{:S(2)}, u32[]{:S(2)}) collective-permute-start(bf16[1024,128]{1,0:T(8,128)(2,1)} %get-tuple-element.71), channel_id=1, source_target_pairs={{0,2},{1,3},{2,4},{3,5},{4,6},{5,7},{6,0},{7,1},{8,10},{9,11},{10,... | collective-permute-start | bytes 786440 | tf_op jit(solution)/shard_map/r_send/ppermute | solution.py:305
  32.4 34.9 %collective-permute-start.8 = (bf16[1024,128]{1,0:T(8,128)(2,1)}, bf16[1024,128]{1,0:T(8,128)(2,1)}, u32[]{:S(2)}, u32[]{:S(2)}) collective-permute-start(bf16[1024,128]{1,0:T(8,128)(2,1)} %get-tuple-element.72), channel_id=1, source_target_pairs={{0,6},{1,7},{2,0},{3,1},{4,2},{5,3},{6,4},{7,5},{8,14},{9,15},{10,... | collective-permute-start | bytes 786440 | tf_op jit(solution)/shard_map/r_send/ppermute | solution.py:305
  60.1 10.0 %copy-start.1 = (bf16[2048,128]{1,0:T(8,128)(2,1)S(1)}, bf16[2048,128]{1,0:T(8,128)(2,1)}, u32[]{:S(2)}) copy-start(bf16[2048,128]{1,0:T(8,128)(2,1)} %get-tuple-element.77.mine_ref) | copy-start | bytes 1572868
  62.2 7.9 %collective-permute-start.6 = (bf16[1024,128]{1,0:T(8,128)(2,1)}, bf16[1024,128]{1,0:T(8,128)(2,1)S(1)}, u32[]{:S(2)}, u32[]{:S(2)}) collective-permute-start(bf16[1024,128]{1,0:T(8,128)(2,1)} %get-tuple-element.70), channel_id=1, source_target_pairs={{0,2},{1,3},{2,4},{3,5},{4,6},{5,7},{6,0},{7,1},{8,10},{9,11},{10,... | collective-permute-start | bytes 786440 | tf_op jit(solution)/shard_map/r_send/ppermute | solution.py:305
  62.3 7.9 %collective-permute-start.9 = (bf16[1024,128]{1,0:T(8,128)(2,1)}, bf16[1024,128]{1,0:T(8,128)(2,1)S(1)}, u32[]{:S(2)}, u32[]{:S(2)}) collective-permute-start(bf16[1024,128]{1,0:T(8,128)(2,1)} %get-tuple-element.73), channel_id=1, source_target_pairs={{0,6},{1,7},{2,0},{3,1},{4,2},{5,3},{6,4},{7,5},{8,14},{9,15},{10,... | collective-permute-start | bytes 786440 | tf_op jit(solution)/shard_map/r_send/ppermute | solution.py:305
  67.2 12.3 %copy-start = (bf16[3,2048,128]{2,1,0:T(8,128)(2,1)}, bf16[3,2048,128]{2,1,0:T(8,128)(2,1)S(1)}, u32[]{:S(2)}) copy-start(bf16[3,2048,128]{2,1,0:T(8,128)(2,1)S(1)} %unpack.1.old_ref) | copy-start | bytes 4718596
  67.2 12.3 %copy-start.2 = (bf16[1024,128]{1,0:T(8,128)(2,1)}, bf16[1024,128]{1,0:T(8,128)(2,1)S(1)}, u32[]{:S(2)}) copy-start(bf16[1024,128]{1,0:T(8,128)(2,1)S(1)} %collective-permute-done.7.refs_1_) | copy-start | bytes 786436
  70.1 9.4 %copy-start.3 = (bf16[1024,128]{1,0:T(8,128)(2,1)}, bf16[1024,128]{1,0:T(8,128)(2,1)S(1)}, u32[]{:S(2)}) copy-start(bf16[1024,128]{1,0:T(8,128)(2,1)S(1)} %collective-permute-done.6.refs_0_) | copy-start | bytes 786436
  70.1 9.4 %copy-start.4 = (bf16[1024,128]{1,0:T(8,128)(2,1)}, bf16[1024,128]{1,0:T(8,128)(2,1)S(1)}, u32[]{:S(2)}) copy-start(bf16[1024,128]{1,0:T(8,128)(2,1)S(1)} %collective-permute-done.9.refs_3_) | copy-start | bytes 786436
  72.1 7.5 %copy-start.5 = (bf16[1024,128]{1,0:T(8,128)(2,1)}, bf16[1024,128]{1,0:T(8,128)(2,1)S(1)}, u32[]{:S(2)}) copy-start(bf16[1024,128]{1,0:T(8,128)(2,1)S(1)} %get-tuple-element.75.refs_5_) | copy-start | bytes 786436
  72.1 7.5 %copy-start.6 = (bf16[1024,128]{1,0:T(8,128)(2,1)}, bf16[1024,128]{1,0:T(8,128)(2,1)S(1)}, u32[]{:S(2)}) copy-start(bf16[1024,128]{1,0:T(8,128)(2,1)S(1)} %get-tuple-element.74.refs_4_) | copy-start | bytes 786436
  72.1 7.3 %collective-permute-start.12 = (bf16[1024,128]{1,0:T(8,128)(2,1)S(1)}, bf16[1024,128]{1,0:T(8,128)(2,1)S(1)}, u32[]{:S(2)}, u32[]{:S(2)}) collective-permute-start(bf16[1024,128]{1,0:T(8,128)(2,1)S(1)} %get-tuple-element.74.refs_4_), channel_id=1, source_target_pairs={{0,1},{1,0},{2,3},{3,2},{4,5},{5,4},{6,7},{7,6},{8,9},{9,8},{10,11... | collective-permute-start | bytes 786440 | tf_op jit(solution)/shard_map/g_sib_lo/ppermute | solution.py:305
  74.5 9.6 %collective-permute-start.10 = (bf16[1024,128]{1,0:T(8,128)(2,1)S(1)}, bf16[1024,128]{1,0:T(8,128)(2,1)S(1)}, u32[]{:S(2)}, u32[]{:S(2)}) collective-permute-start(bf16[1024,128]{1,0:T(8,128)(2,1)S(1)} %get-tuple-element.74.refs_4_), channel_id=1, source_target_pairs={{0,2},{1,3},{2,4},{3,5},{4,6},{5,7},{6,0},{7,1},{8,10},{9,11},{10,... | collective-permute-start | bytes 786440 | tf_op jit(solution)/shard_map/g_up_lo/ppermute | solution.py:305
  74.5 9.6 %collective-permute-start.11 = (bf16[1024,128]{1,0:T(8,128)(2,1)S(1)}, bf16[1024,128]{1,0:T(8,128)(2,1)S(1)}, u32[]{:S(2)}, u32[]{:S(2)}) collective-permute-start(bf16[1024,128]{1,0:T(8,128)(2,1)S(1)} %get-tuple-element.75.refs_5_), channel_id=1, source_target_pairs={{0,6},{1,7},{2,0},{3,1},{4,2},{5,3},{6,4},{7,5},{8,14},{9,15},{10,... | collective-permute-start | bytes 786440 | tf_op jit(solution)/shard_map/g_dn_hi/ppermute | solution.py:305
  77.2 11.0 %collective-permute-start.14 = (bf16[1024,128]{1,0:T(8,128)(2,1)S(1)}, bf16[1024,128]{1,0:T(8,128)(2,1)S(1)}, u32[]{:S(2)}, u32[]{:S(2)}) collective-permute-start(bf16[1024,128]{1,0:T(8,128)(2,1)S(1)} %get-tuple-element.74.refs_4_), channel_id=1, source_target_pairs={{0,6},{1,7},{2,0},{3,1},{4,2},{5,3},{6,4},{7,5},{8,14},{9,15},{10,... | collective-permute-start | bytes 786440 | tf_op jit(solution)/shard_map/g_dn_lo/ppermute | solution.py:305
  78.5 11.6 %collective-permute-start.15 = (bf16[1024,128]{1,0:T(8,128)(2,1)S(1)}, bf16[1024,128]{1,0:T(8,128)(2,1)S(1)}, u32[]{:S(2)}, u32[]{:S(2)}) collective-permute-start(bf16[1024,128]{1,0:T(8,128)(2,1)S(1)} %get-tuple-element.75.refs_5_), channel_id=1, source_target_pairs={{0,1},{1,0},{2,3},{3,2},{4,5},{5,4},{6,7},{7,6},{8,9},{9,8},{10,11... | collective-permute-start | bytes 786440 | tf_op jit(solution)/shard_map/g_sib_hi/ppermute | solution.py:305
  79.5 10.7 %collective-permute-start.13 = (bf16[1024,128]{1,0:T(8,128)(2,1)S(1)}, bf16[1024,128]{1,0:T(8,128)(2,1)S(1)}, u32[]{:S(2)}, u32[]{:S(2)}) collective-permute-start(bf16[1024,128]{1,0:T(8,128)(2,1)S(1)} %get-tuple-element.75.refs_5_), channel_id=1, source_target_pairs={{0,2},{1,3},{2,4},{3,5},{4,6},{5,7},{6,0},{7,1},{8,10},{9,11},{10,... | collective-permute-start | bytes 786440 | tf_op jit(solution)/shard_map/g_up_hi/ppermute | solution.py:305
  84.1 10.7 %collective-permute-start.16 = (bf16[1024,128]{1,0:T(8,128)(2,1)S(1)}, bf16[1024,128]{1,0:T(8,128)(2,1)S(1)}, u32[]{:S(2)}, u32[]{:S(2)}) collective-permute-start(bf16[1024,128]{1,0:T(8,128)(2,1)S(1)} %collective-permute-done.10.refs_0_), channel_id=1, source_target_pairs={{0,2},{1,3},{2,4},{3,5},{4,6},{5,7},{6,0},{7,1},{8,10},{9,11},{10,... | collective-permute-start | bytes 786440 | tf_op jit(solution)/shard_map/g_opp_lo/ppermute | solution.py:305
  84.3 10.5 %collective-permute-start.17 = (bf16[1024,128]{1,0:T(8,128)(2,1)S(1)}, bf16[1024,128]{1,0:T(8,128)(2,1)S(1)}, u32[]{:S(2)}, u32[]{:S(2)}) collective-permute-start(bf16[1024,128]{1,0:T(8,128)(2,1)S(1)} %collective-permute-done.11.refs_1_), channel_id=1, source_target_pairs={{0,6},{1,7},{2,0},{3,1},{4,2},{5,3},{6,4},{7,5},{8,14},{9,15},{10,... | collective-permute-start | bytes 786440 | tf_op jit(solution)/shard_map/g_opp_hi/ppermute | solution.py:305
  88.1 8.0 %collective-permute-start.22 = (bf16[1024,128]{1,0:T(8,128)(2,1)S(1)}, bf16[1024,128]{1,0:T(8,128)(2,1)S(1)}, u32[]{:S(2)}, u32[]{:S(2)}) collective-permute-start(bf16[1024,128]{1,0:T(8,128)(2,1)S(1)} %collective-permute-done.10.refs_0_), channel_id=1, source_target_pairs={{0,1},{1,0},{2,3},{3,2},{4,5},{5,4},{6,7},{7,6},{8,9},{9,8},{10,11... | collective-permute-start | bytes 786440 | tf_op jit(solution)/shard_map/g_sib_up_lo/ppermute | solution.py:305
  90.1 6.1 %collective-permute-start.23 = (bf16[1024,128]{1,0:T(8,128)(2,1)S(1)}, bf16[1024,128]{1,0:T(8,128)(2,1)S(1)}, u32[]{:S(2)}, u32[]{:S(2)}) collective-permute-start(bf16[1024,128]{1,0:T(8,128)(2,1)S(1)} %collective-permute-done.11.refs_1_), channel_id=1, source_target_pairs={{0,1},{1,0},{2,3},{3,2},{4,5},{5,4},{6,7},{7,6},{8,9},{9,8},{10,11... | collective-permute-start | bytes 786440 | tf_op jit(solution)/shard_map/g_sib_dn_hi/ppermute | solution.py:305
  94.8 2.0 %collective-permute-start.20 = (bf16[1024,128]{1,0:T(8,128)(2,1)S(1)}, bf16[1024,128]{1,0:T(8,128)(2,1)S(1)}, u32[]{:S(2)}, u32[]{:S(2)}) collective-permute-start(bf16[1024,128]{1,0:T(8,128)(2,1)S(1)} %collective-permute-done.13.refs_2_), channel_id=1, source_target_pairs={{0,1},{1,0},{2,3},{3,2},{4,5},{5,4},{6,7},{7,6},{8,9},{9,8},{10,11... | collective-permute-start | bytes 786440 | tf_op jit(solution)/shard_map/g_sib_up_hi/ppermute | solution.py:305
  95.7 1.5 %collective-permute-start.21 = (bf16[1024,128]{1,0:T(8,128)(2,1)S(1)}, bf16[1024,128]{1,0:T(8,128)(2,1)S(1)}, u32[]{:S(2)}, u32[]{:S(2)}) collective-permute-start(bf16[1024,128]{1,0:T(8,128)(2,1)S(1)} %collective-permute-done.14.refs_3_), channel_id=1, source_target_pairs={{0,1},{1,0},{2,3},{3,2},{4,5},{5,4},{6,7},{7,6},{8,9},{9,8},{10,11... | collective-permute-start | bytes 786440 | tf_op jit(solution)/shard_map/g_sib_dn_lo/ppermute | solution.py:305
  95.7 2.7 %collective-permute-start.18 = (bf16[1024,128]{1,0:T(8,128)(2,1)S(1)}, bf16[1024,128]{1,0:T(8,128)(2,1)S(1)}, u32[]{:S(2)}, u32[]{:S(2)}) collective-permute-start(bf16[1024,128]{1,0:T(8,128)(2,1)S(1)} %collective-permute-done.16.refs_0_), channel_id=1, source_target_pairs={{0,1},{1,0},{2,3},{3,2},{4,5},{5,4},{6,7},{7,6},{8,9},{9,8},{10,11... | collective-permute-start | bytes 786440 | tf_op jit(solution)/shard_map/g_sib_opp_lo/ppermute | solution.py:305
  96.2 2.2 %collective-permute-start.19 = (bf16[1024,128]{1,0:T(8,128)(2,1)S(1)}, bf16[1024,128]{1,0:T(8,128)(2,1)S(1)}, u32[]{:S(2)}, u32[]{:S(2)}) collective-permute-start(bf16[1024,128]{1,0:T(8,128)(2,1)S(1)} %collective-permute-done.17.refs_1_), channel_id=1, source_target_pairs={{0,1},{1,0},{2,3},{3,2},{4,5},{5,4},{6,7},{7,6},{8,9},{9,8},{10,11... | collective-permute-start | bytes 786440 | tf_op jit(solution)/shard_map/g_sib_opp_hi/ppermute | solution.py:305
  (4 other events, 3.7 us)
